TPU v7x, 32 devices: a whole 2x2x4 slice. The times are simulated.
32 devices in a mesh: groups: 2 (over y), space: 8 (over z, x), vec: 2 (over core).
Axes of the slice: x: 2, y: 2, z: 4, core: 2. Of those that a mesh axis runs over, the one named last changes fastest.
Arguments:
- perturbation: float32 [8, 5, 64, 8, 128], P(('groups', 'vec'), None, 'space'), parts along dimension 0, may hold values from -6 to 6
- forcing: float32 [8, 5, 64, 8, 128], P(('groups', 'vec'), None, 'space'), parts along dimension 0, may hold values from -6 to 6
- frequency: float32 [8], P(('groups', 'vec')), parts along dimension 0, may hold values from 0.5 to 6
- base_flow: float32 [6, 5, 64, 8, 128], P('vec', None, 'space'), may hold values from -1 to 1.4, as said below
- phase_slot: int32 [6], replicated, may hold values from 0 to 5, each once
Outputs:
- response: float32 [8, 5, 64, 8, 128], P(('groups', 'vec'), None, 'space'), parts along dimension 0
There are 2 independent parts, one for each index of `groups`. A program takes and returns all parts, laid end to end along the dimension named above; an argument that names none is the same for every part. Nothing has to cross between parts.
Inputs may be any that keep to these rules, and one draw needn't show every extreme that they name: `phase_slot`: each stored slot serves exactly one time step. `base_flow`: field 0 (density) lies in 0.7 to 1.3, field 4 (pressure) in 0.6 to 1.4, fields 1 to 3 are velocities.
All inputs are finite; a program needn't handle non-finite values.
Results may differ from a plain program's by a relative error of at most 0.00002.
Values sent between devices are 32-bit elements; how exact they have to be, the bound alone decides.
No kernel may reach another device: no remote copies, remote signals or barrier semaphores. Data moves between devices by JAX's collectives and lax.ppermute only.
A program may use at most 128 MiB of HBM per device.

v0:
```python
import functools

import jax
import jax.numpy as jnp
from jax import lax
from jax.experimental import pallas as pl
from jax.experimental.pallas import tpu as pltpu
from jax.sharding import PartitionSpec as P

HEAT_RATIO = 1.4
VISCOSITY = 0.1
TIME_STEP = 0.4
FIELDS = 5
TERMS = 26
STAGES = 4
UNROLL = 2


VMEM = pl.BlockSpec(memory_space=pltpu.VMEM)
SMEM = pl.BlockSpec(memory_space=pltpu.SMEM)


def copy_planes(pairs):
    for dst, value in pairs:
        dst[...] = value


def pack_kernel(width, who, pert, force, base, swap_out, own_out, other_out):
    mine = who[0]
    other = 1 - mine
    tile = pert.shape[2]
    start = mine * (tile - width)
    edge = pl.ds(start, width)
    f = FIELDS
    swap_out[0:f] = pert[other]
    swap_out[f : 2 * f] = force[other]
    own_out[0:f] = pert[mine, :, edge]
    own_out[f : 2 * f] = force[mine, :, edge]
    other_out[0:f] = pert[other, :, edge]
    other_out[f : 2 * f] = force[other, :, edge]
    for slot in range(base.shape[0]):
        lo = (2 + slot) * f
        swap_out[lo : lo + f] = base[slot]
        own_out[lo : lo + f] = base[slot, :, edge]
        other_out[lo : lo + f] = base[slot, :, edge]


def assemble_kernel(width, who, pert, force, base, swap_in, own_in, other_in, state_out, force_out, base_out):
    mine = who[0]
    tile = pert.shape[2]
    f = FIELDS
    here = pl.ds(width + mine * tile, tile)
    there = pl.ds(width + (1 - mine) * tile, tile)
    far = width + 2 * tile
    own_at = pl.ds((1 - mine) * far, width)
    other_at = pl.ds(mine * far, width)
    state_out[:, here] = pert[mine]
    state_out[:, there] = swap_in[0:f]
    state_out[:, own_at] = own_in[0:f]
    state_out[:, other_at] = other_in[0:f]
    force_out[:, here] = force[mine]
    force_out[:, there] = swap_in[f : 2 * f]
    force_out[:, own_at] = own_in[f : 2 * f]
    force_out[:, other_at] = other_in[f : 2 * f]
    for slot in range(base.shape[0]):
        lo = slot * f
        base_out[lo : lo + f, here] = base[slot]
        base_out[lo : lo + f, there] = swap_in[2 * f + lo : 3 * f + lo]
        base_out[lo : lo + f, own_at] = own_in[2 * f + lo : 3 * f + lo]
        base_out[lo : lo + f, other_at] = other_in[2 * f + lo : 3 * f + lo]


def neighbours(ref, field, at, count):
    block = ref[field, pl.ds(at - 1, count + 2)]
    centre = block[1 : count + 1]
    return (
        centre,
        (block[2:], block[:count]),
        (pltpu.roll(centre, centre.shape[1] - 1, 1), pltpu.roll(centre, 1, 1)),
        (pltpu.roll(centre, centre.shape[2] - 1, 2), pltpu.roll(centre, 1, 2)),
    )


def base_terms(base, terms, at, count):
    centre, diff = [], []
    for field in range(FIELDS):
        mid, along_x, along_y, along_z = neighbours(base, field, at, count)
        centre.append(mid)
        diff.append([up - down for up, down in (along_x, along_y, along_z)])
    density, pressure = centre[0], centre[4]
    inverse = 1.0 / density
    square = 0.5 * inverse * inverse
    divergence = diff[1][0] + diff[2][1] + diff[3][2]
    out = [-0.5 * centre[1 + j] for j in range(3)]
    out += [-0.5 * diff[0][j] for j in range(3)]
    out += [-0.5 * density, -0.5 * divergence]
    for j in range(3):
        for k in range(3):
            slope = -0.5 * diff[1 + k][j]
            out.append(slope - 6.0 * VISCOSITY if j == k else slope)
    out += [-0.5 * inverse]
    out += [diff[4][k] * square for k in range(3)]
    out += [-0.5 * diff[4][j] for j in range(3)]
    out += [-0.5 * HEAT_RATIO * pressure, -0.5 * HEAT_RATIO * divergence]
    for index, value in enumerate(out):
        terms[index, pl.ds(at, count)] = value


def rates(state, terms, force, wave, at, count):
    here = pl.ds(at, count)
    centre, diff, around = [], [], []
    for field in range(FIELDS):
        mid, along_x, along_y, along_z = neighbours(state, field, at, count)
        centre.append(mid)
        diff.append([up - down for up, down in (along_x, along_y, along_z)])
        if 1 <= field <= 3:
            around.append((along_x[0] + along_x[1]) + (along_y[0] + along_y[1]) + (along_z[0] + along_z[1]))
    term = lambda index: terms[index, here]
    speed = [term(j) for j in range(3)]
    spread = diff[1][0] + diff[2][1] + diff[3][2]

    def carried(field, first, stride):
        total = force[field, here] * wave
        for j in range(3):
            total = total + (speed[j] * diff[field][j] + centre[1 + j] * term(first + stride * j))
        return total

    out = [carried(0, 3, 1) + (term(6) * spread + centre[0] * term(7))]
    inverse = term(17)
    for k in range(3):
        pull = inverse * diff[4][k] + centre[0] * term(18 + k)
        out.append(carried(1 + k, 8 + k, 3) + (pull + VISCOSITY * around[k]))
    out.append(carried(4, 21, 1) + (term(24) * spread + centre[4] * term(25)))
    return out


def over_planes(first, last, body):
    count = last - first
    whole = count // UNROLL

    def step(index, carry):
        body(first + index * UNROLL, UNROLL)
        return carry

    lax.fori_loop(0, whole, step, 0)
    if count % UNROLL:
        body(first + whole * UNROLL, count % UNROLL)


def one_step(inset, state, force, terms, waves, second, third, fourth):
    planes = state.shape[1]

    def stage(number, source, size, wave, target):
        def body(at, count):
            here = pl.ds(at, count)
            for field, rate in enumerate(rates(source, terms, force, wave, at, count)):
                target[field, here] = state[field, here] + size * rate

        over_planes(inset + number, planes - inset - number, body)

    stage(1, state, 0.5 * TIME_STEP, waves[0][None], second)
    stage(2, second, 0.5 * TIME_STEP, waves[1][None], third)
    stage(3, third, TIME_STEP, waves[1][None], fourth)

    def body(at, count):
        here = pl.ds(at, count)
        for field, rate in enumerate(rates(fourth, terms, force, waves[2][None], at, count)):
            mixed = second[field, here] + fourth[field, here] + 2.0 * third[field, here] - state[field, here]
            state[field, here] = mixed * (1.0 / 3.0) + (TIME_STEP / 6.0) * rate

    over_planes(inset + STAGES, planes - inset - STAGES, body)


def fetch_base(slot, who, base_here, base_there, base):
    local = base_here.shape[0] // FIELDS
    lo = lax.rem(slot, local) * FIELDS
    held = lax.div(slot, local) == who[1]

    @pl.when(held)
    def _():
        base[...] = base_here[pl.ds(lo, FIELDS)]

    @pl.when(jnp.logical_not(held))
    def _():
        base[...] = base_there[pl.ds(lo, FIELDS)]


def advance_kernel(first_step, width, ends, who, phase_slot, waves, force, base_here, base_there, *refs):
    first, last = ends
    if first:
        (state_in,), refs = refs[:1], refs[1:]
    else:
        (slab_in, left_in, right_in), refs = refs[:3], refs[3:]
    outs, (state, base, terms, second, third, fourth) = refs[:-6], refs[-6:]
    planes = state.shape[1]
    if first:
        state[...] = state_in[...]
    else:
        state[:, 0:width] = left_in[...]
        state[:, width : planes - width] = slab_in[...]
        state[:, planes - width :] = right_in[...]
    for index in range(width // STAGES):
        inset = STAGES * index
        fetch_base(phase_slot[first_step + index], who, base_here, base_there, base)
        over_planes(inset + 1, planes - inset - 1, functools.partial(base_terms, base, terms))
        wave = [waves[3 * index + which] for which in range(3)]
        one_step(inset, state, force, terms, wave, second, third, fourth)
    if last:
        keep, give = outs
        tile = keep.shape[1]
        mine = who[0]
        keep[...] = state[:, pl.ds(width + mine * tile, tile)]
        give[...] = state[:, pl.ds(width + (1 - mine) * tile, tile)]
    else:
        slab, left, right = outs
        slab[...] = state[:, width : planes - width]
        left[...] = state[:, width : 2 * width]
        right[...] = state[:, planes - 2 * width : planes - width]


def advance(first_step, width, ends, who, phase_slot, waves, force, base_here, base_there, carried):
    planes = force.shape[1]
    rows, lanes = force.shape[2:]
    block = lambda *lead: jax.ShapeDtypeStruct((*lead, rows, lanes), jnp.float32)
    slab = planes - 2 * width
    if ends[1]:
        outs = [block(FIELDS, slab // 2)] * 2
    else:
        outs = [block(FIELDS, slab), block(FIELDS, width), block(FIELDS, width)]
    scratch = lambda lead: pltpu.VMEM((lead, planes, rows, lanes), jnp.float32)
    return pl.pallas_call(
        functools.partial(advance_kernel, first_step, width, ends),
        out_shape=outs,
        in_specs=[SMEM, SMEM] + [VMEM] * (4 + len(carried)),
        out_specs=[VMEM] * len(outs),
        scratch_shapes=[scratch(FIELDS), scratch(FIELDS), scratch(TERMS)] + [scratch(FIELDS)] * 3,
        compiler_params=pltpu.CompilerParams(vmem_limit_bytes=32 << 20),
        name="advance",
    )(who, phase_slot, waves, force, base_here, base_there, *carried)


def per_device(width, perturbation, forcing, frequency, base_flow, phase_slot):
    _, _, tile, rows, lanes = perturbation.shape
    slots = base_flow.shape[0]
    count = lax.axis_size("space")
    steps = phase_slot.shape[0]
    place = lax.axis_index("space")
    mine = lax.rem(place, 2)
    who = jnp.stack([mine, lax.axis_index("vec")]).astype(jnp.int32)
    block = lambda *lead: jax.ShapeDtypeStruct((*lead, rows, lanes), jnp.float32)

    swap = [(i, i ^ 1) for i in range(count)]
    own = [(i, (i + 2 * (1 if i % 2 else -1)) % count) for i in range(count)]
    other = [(i, (i + (1 if i % 2 else -1)) % count) for i in range(count)]
    ahead = [(i, (i + 2) % count) for i in range(count)]
    behind = [(i, (i - 2) % count) for i in range(count)]
    core = [(0, 1), (1, 0)]

    lead = FIELDS * (2 + slots)
    swap_out, own_out, other_out = pl.pallas_call(
        functools.partial(pack_kernel, width),
        out_shape=[block(lead, tile), block(lead, width), block(lead, width)],
        in_specs=[SMEM] + [VMEM] * 3,
        out_specs=[VMEM] * 3,
        name="pack",
    )(who, perturbation, forcing, base_flow)
    swap_in = lax.ppermute(swap_out, "space", swap)
    own_in = lax.ppermute(own_out, "space", own)
    other_in = lax.ppermute(other_out, "space", other)

    planes = 2 * (tile + width)
    state, force, base_here = pl.pallas_call(
        functools.partial(assemble_kernel, width),
        out_shape=[block(FIELDS, planes), block(FIELDS, planes), block(FIELDS * slots, planes)],
        in_specs=[SMEM] + [VMEM] * 6,
        out_specs=[VMEM] * 3,
        name="assemble",
    )(who, perturbation, forcing, base_flow, swap_in, own_in, other_in)
    base_there = lax.ppermute(base_here, "vec", core)

    moments = jnp.array(
        [step * TIME_STEP + part for step in range(steps) for part in (0.0, 0.5 * TIME_STEP, TIME_STEP)],
        jnp.float32,
    )
    tuned = lax.dynamic_index_in_dim(frequency, mine, 0, keepdims=False)
    waves = jnp.broadcast_to(jnp.cos(tuned * moments)[:, None, None], (3 * steps, rows, lanes))

    per_round = width // STAGES
    carried = (state,)
    for first_step in range(0, steps, per_round):
        ends = (first_step == 0, first_step + per_round == steps)
        part = waves[3 * first_step : 3 * (first_step + per_round)]
        outs = advance(first_step, width, ends, who, phase_slot, part, force, base_here, base_there, carried)
        if not ends[1]:
            slab, left, right = outs
            carried = (slab, lax.ppermute(right, "space", ahead), lax.ppermute(left, "space", behind))
    keep, give = outs
    given = lax.ppermute(give, "space", swap)
    low, high = jnp.where(mine == 0, keep, given), jnp.where(mine == 0, given, keep)
    return jnp.stack([low, high])


def solution(mesh):
    return jax.shard_map(
        functools.partial(per_device, STAGES),
        mesh=mesh,
        in_specs=(
            P(("groups", "vec"), None, "space", None, None),
            P(("groups", "vec"), None, "space", None, None),
            P(("groups", "vec")),
            P("vec", None, "space", None, None),
            P(),
        ),
        out_specs=P(("groups", "vec"), None, "space", None, None),
        check_vma=False,
    )
```

profile of v0, /device:TPU:0, one launch (start us, length us, event | category | flops | bytes accessed | tf_op | source)
XLA Modules:
  0.0 117.7 jit_solution(1085260848377356724)
XLA Ops:
  0.6 2.5 %pack.1 = (f32[25,8,8,128]{3,2,1,0:T(8,128)}, f32[25,4,8,128]{3,2,1,0:T(8,128)}, f32[25,4,8,128]{3,2,1,0:T(8,128)}) custom-call(s32[2]{0:T(128)} %pad_add_fusion.who, f32[2,5,8,8,128]{4,3,2,1,0:T(8,128)} %pert.3, f32[2,5,8,8,128]{4,3,2,1,0:T(8,128)} %force.3, f32[3,5,8,8,128]{4,3,2,1,0:T(8,128)} %base.3), custom_call_target="tpu_custom_call" | custom-call | tf_op jit(solution)/shard_map/pack/pallas_call | solution.py:260
  3.1 3.0 %collective-permute-start = (f32[25,8,8,128]{3,2,1,0:T(8,128)}, f32[25,8,8,128]{3,2,1,0:T(8,128)S(1)}, u32[]{:S(2)}, u32[]{:S(2)}) collective-permute-start(f32[25,8,8,128]{3,2,1,0:T(8,128)} %get-tuple-element.28), channel_id=1, source_target_pairs={{0,2},{2,0},{4,6},{6,4},{8,10},{10,8},{12,14},{14,12},{1,3},{3,1},... | collective-permute-start | bytes 2457608 | tf_op jit(solution)/shard_map/ppermute | solution.py:267
  6.1 3.6 %collective-permute-start.1 = (f32[25,4,8,128]{3,2,1,0:T(8,128)}, f32[25,4,8,128]{3,2,1,0:T(8,128)S(1)}, u32[]{:S(2)}, u32[]{:S(2)}) collective-permute-start(f32[25,4,8,128]{3,2,1,0:T(8,128)} %get-tuple-element.29), channel_id=1, source_target_pairs={{0,12},{2,6},{4,0},{6,10},{8,4},{10,14},{12,8},{14,2},{1,13},{3,7}... | collective-permute-start | bytes 1228808 | tf_op jit(solution)/shard_map/ppermute | solution.py:268
  9.7 10.2 %collective-permute-done.1.own_in = f32[25,4,8,128]{3,2,1,0:T(8,128)S(1)} collective-permute-done((f32[25,4,8,128]{3,2,1,0:T(8,128)}, f32[25,4,8,128]{3,2,1,0:T(8,128)S(1)}, u32[]{:S(2)}, u32[]{:S(2)}) %collective-permute-start.1) | collective-permute-done | bytes 409632 | tf_op jit(solution)/shard_map/ppermute | solution.py:268
  19.9 8.0 %collective-permute-done.2.other_in = f32[25,4,8,128]{3,2,1,0:T(8,128)S(1)} collective-permute-done((f32[25,4,8,128]{3,2,1,0:T(8,128)}, f32[25,4,8,128]{3,2,1,0:T(8,128)S(1)}, u32[]{:S(2)}, u32[]{:S(2)}) %collective-permute-start.2) | collective-permute-done | bytes 409632 | tf_op jit(solution)/shard_map/ppermute | solution.py:269
  27.9 5.4 %collective-permute-done.swap_in = f32[25,8,8,128]{3,2,1,0:T(8,128)S(1)} collective-permute-done((f32[25,8,8,128]{3,2,1,0:T(8,128)}, f32[25,8,8,128]{3,2,1,0:T(8,128)S(1)}, u32[]{:S(2)}, u32[]{:S(2)}) %collective-permute-start) | collective-permute-done | bytes 819232 | tf_op jit(solution)/shard_map/ppermute | solution.py:267
  34.3 3.3 %assemble.1 = (f32[5,24,8,128]{3,2,1,0:T(8,128)}, f32[5,24,8,128]{3,2,1,0:T(8,128)}, f32[15,24,8,128]{3,2,1,0:T(8,128)}) custom-call(s32[2]{0:T(128)} %pad_add_fusion.who, f32[2,5,8,8,128]{4,3,2,1,0:T(8,128)} %pert.3, f32[2,5,8,8,128]{4,3,2,1,0:T(8,128)} %force.3, f32[3,5,8,8,128]{4,3,2,1,0:T(8,128)} %base.3, f32[25,8,8,128]{3,2,1,0:T(8,128)} %copy-done.6, ...), custom_call_target="tpu_custom_call" | custom-call | tf_op jit(solution)/shard_map/assemble/pallas_call | solution.py:272
  38.9 2.1 %collective-permute-done.3.base_there = f32[15,24,8,128]{3,2,1,0:T(8,128)S(1)} collective-permute-done((f32[15,24,8,128]{3,2,1,0:T(8,128)}, f32[15,24,8,128]{3,2,1,0:T(8,128)S(1)}, u32[]{:S(2)}, u32[]{:S(2)}) %collective-permute-start.3) | collective-permute-done | bytes 1474592 | tf_op jit(solution)/shard_map/ppermute | solution.py:279
  41.1 1.4 %copy-done = f32[15,24,8,128]{3,2,1,0:T(8,128)S(1)} copy-done((f32[15,24,8,128]{3,2,1,0:T(8,128)S(1)}, f32[15,24,8,128]{3,2,1,0:T(8,128)}, u32[]{:S(2)}) %copy-start) | copy-done | bytes 1474584
  42.5 1.0 copy-done.2
  44.6 5.4 %advance.6 = (f32[5,16,8,128]{3,2,1,0:T(8,128)S(1)}, f32[5,4,8,128]{3,2,1,0:T(8,128)S(1)}, f32[5,4,8,128]{3,2,1,0:T(8,128)S(1)}) custom-call(s32[2]{0:T(128)S(1)} %copy-done.4, s32[6]{0:T(128)S(1)} %copy-done.5, f32[3,8,128]{2,1,0:T(8,128)S(1)} %broadcast_in_dim.21.waves, f32[5,24,8,128]{3,2,1,0:T(8,128)S(1)} %copy-done.2, f32[15,24,8,128]{3,2,1,0:T(8,128)S(1)} %copy-done, ...), custom_call_target="tpu_custom_call" | custom-call | tf_op jit(solution)/shard_map/advance/pallas_call | solution.py:231
  49.9 1.9 %collective-permute-start.4 = (f32[5,4,8,128]{3,2,1,0:T(8,128)S(1)}, f32[5,4,8,128]{3,2,1,0:T(8,128)S(1)}, u32[]{:S(2)}, u32[]{:S(2)}) collective-permute-start(f32[5,4,8,128]{3,2,1,0:T(8,128)S(1)} %get-tuple-element.35), channel_id=1, source_target_pairs={{0,4},{2,6},{4,8},{6,10},{8,12},{10,14},{12,0},{14,2},{1,5},{3,7},... | collective-permute-start | bytes 245768 | tf_op jit(solution)/shard_map/ppermute | solution.py:296
  51.8 2.1 %collective-permute-start.5 = (f32[5,4,8,128]{3,2,1,0:T(8,128)S(1)}, f32[5,4,8,128]{3,2,1,0:T(8,128)S(1)}, u32[]{:S(2)}, u32[]{:S(2)}) collective-permute-start(f32[5,4,8,128]{3,2,1,0:T(8,128)S(1)} %get-tuple-element.36), channel_id=1, source_target_pairs={{0,12},{2,14},{4,0},{6,2},{8,4},{10,6},{12,8},{14,10},{1,13},{3,15... | collective-permute-start | bytes 245768 | tf_op jit(solution)/shard_map/ppermute | solution.py:296
  53.9 3.0 %collective-permute-done.4.refs_1_ = f32[5,4,8,128]{3,2,1,0:T(8,128)S(1)} collective-permute-done((f32[5,4,8,128]{3,2,1,0:T(8,128)S(1)}, f32[5,4,8,128]{3,2,1,0:T(8,128)S(1)}, u32[]{:S(2)}, u32[]{:S(2)}) %collective-permute-start.4) | collective-permute-done | bytes 81952 | tf_op jit(solution)/shard_map/ppermute | solution.py:296
  57.9 5.4 %advance.7 = (f32[5,16,8,128]{3,2,1,0:T(8,128)S(1)}, f32[5,4,8,128]{3,2,1,0:T(8,128)S(1)}, f32[5,4,8,128]{3,2,1,0:T(8,128)S(1)}) custom-call(s32[2]{0:T(128)S(1)} %copy-done.4, s32[6]{0:T(128)S(1)} %copy-done.5, f32[3,8,128]{2,1,0:T(8,128)S(1)} %broadcast_in_dim.20.waves, f32[5,24,8,128]{3,2,1,0:T(8,128)S(1)} %copy-done.2, f32[15,24,8,128]{3,2,1,0:T(8,128)S(1)} %copy-done.1, ...), custom_call_target="tpu_custom_call" | custom-call | tf_op jit(solution)/shard_map/advance/pallas_call | solution.py:231
  63.2 1.2 %collective-permute-start.6 = (f32[5,4,8,128]{3,2,1,0:T(8,128)S(1)}, f32[5,4,8,128]{3,2,1,0:T(8,128)S(1)}, u32[]{:S(2)}, u32[]{:S(2)}) collective-permute-start(f32[5,4,8,128]{3,2,1,0:T(8,128)S(1)} %get-tuple-element.38), channel_id=1, source_target_pairs={{0,4},{2,6},{4,8},{6,10},{8,12},{10,14},{12,0},{14,2},{1,5},{3,7},... | collective-permute-start | bytes 245768 | tf_op jit(solution)/shard_map/ppermute | solution.py:296
  64.4 2.7 %collective-permute-start.7 = (f32[5,4,8,128]{3,2,1,0:T(8,128)S(1)}, f32[5,4,8,128]{3,2,1,0:T(8,128)S(1)}, u32[]{:S(2)}, u32[]{:S(2)}) collective-permute-start(f32[5,4,8,128]{3,2,1,0:T(8,128)S(1)} %get-tuple-element.39), channel_id=1, source_target_pairs={{0,12},{2,14},{4,0},{6,2},{8,4},{10,6},{12,8},{14,10},{1,13},{3,15... | collective-permute-start | bytes 245768 | tf_op jit(solution)/shard_map/ppermute | solution.py:296
  67.1 2.8 %collective-permute-done.6.refs_1_ = f32[5,4,8,128]{3,2,1,0:T(8,128)S(1)} collective-permute-done((f32[5,4,8,128]{3,2,1,0:T(8,128)S(1)}, f32[5,4,8,128]{3,2,1,0:T(8,128)S(1)}, u32[]{:S(2)}, u32[]{:S(2)}) %collective-permute-start.6) | collective-permute-done | bytes 81952 | tf_op jit(solution)/shard_map/ppermute | solution.py:296
  70.3 5.4 %advance.8 = (f32[5,16,8,128]{3,2,1,0:T(8,128)S(1)}, f32[5,4,8,128]{3,2,1,0:T(8,128)S(1)}, f32[5,4,8,128]{3,2,1,0:T(8,128)S(1)}) custom-call(s32[2]{0:T(128)S(1)} %copy-done.4, s32[6]{0:T(128)S(1)} %copy-done.5, f32[3,8,128]{2,1,0:T(8,128)S(1)} %broadcast_in_dim.19.waves, f32[5,24,8,128]{3,2,1,0:T(8,128)S(1)} %copy-done.2, f32[15,24,8,128]{3,2,1,0:T(8,128)S(1)} %copy-done.1, ...), custom_call_target="tpu_custom_call" | custom-call | tf_op jit(solution)/shard_map/advance/pallas_call | solution.py:231
  76.1 3.5 %collective-permute-start.9 = (f32[5,4,8,128]{3,2,1,0:T(8,128)S(1)}, f32[5,4,8,128]{3,2,1,0:T(8,128)S(1)}, u32[]{:S(2)}, u32[]{:S(2)}) collective-permute-start(f32[5,4,8,128]{3,2,1,0:T(8,128)S(1)} %get-tuple-element.42), channel_id=1, source_target_pairs={{0,12},{2,14},{4,0},{6,2},{8,4},{10,6},{12,8},{14,10},{1,13},{3,15... | collective-permute-start | bytes 245768 | tf_op jit(solution)/shard_map/ppermute | solution.py:296
  79.6 2.5 %collective-permute-done.8.refs_1_ = f32[5,4,8,128]{3,2,1,0:T(8,128)S(1)} collective-permute-done((f32[5,4,8,128]{3,2,1,0:T(8,128)S(1)}, f32[5,4,8,128]{3,2,1,0:T(8,128)S(1)}, u32[]{:S(2)}, u32[]{:S(2)}) %collective-permute-start.8) | collective-permute-done | bytes 81952 | tf_op jit(solution)/shard_map/ppermute | solution.py:296
  82.2 5.4 %advance.9 = (f32[5,16,8,128]{3,2,1,0:T(8,128)S(1)}, f32[5,4,8,128]{3,2,1,0:T(8,128)S(1)}, f32[5,4,8,128]{3,2,1,0:T(8,128)S(1)}) custom-call(s32[2]{0:T(128)S(1)} %copy-done.4, s32[6]{0:T(128)S(1)} %copy-done.5, f32[3,8,128]{2,1,0:T(8,128)S(1)} %broadcast_in_dim.18.waves, f32[5,24,8,128]{3,2,1,0:T(8,128)S(1)} %copy-done.2, f32[15,24,8,128]{3,2,1,0:T(8,128)S(1)} %copy-done.1, ...), custom_call_target="tpu_custom_call" | custom-call | tf_op jit(solution)/shard_map/advance/pallas_call | solution.py:231
  87.5 1.2 %collective-permute-start.10 = (f32[5,4,8,128]{3,2,1,0:T(8,128)S(1)}, f32[5,4,8,128]{3,2,1,0:T(8,128)S(1)}, u32[]{:S(2)}, u32[]{:S(2)}) collective-permute-start(f32[5,4,8,128]{3,2,1,0:T(8,128)S(1)} %get-tuple-element.44), channel_id=1, source_target_pairs={{0,4},{2,6},{4,8},{6,10},{8,12},{10,14},{12,0},{14,2},{1,5},{3,7},... | collective-permute-start | bytes 245768 | tf_op jit(solution)/shard_map/ppermute | solution.py:296
  88.8 2.7 %collective-permute-start.11 = (f32[5,4,8,128]{3,2,1,0:T(8,128)S(1)}, f32[5,4,8,128]{3,2,1,0:T(8,128)S(1)}, u32[]{:S(2)}, u32[]{:S(2)}) collective-permute-start(f32[5,4,8,128]{3,2,1,0:T(8,128)S(1)} %get-tuple-element.45), channel_id=1, source_target_pairs={{0,12},{2,14},{4,0},{6,2},{8,4},{10,6},{12,8},{14,10},{1,13},{3,15... | collective-permute-start | bytes 245768 | tf_op jit(solution)/shard_map/ppermute | solution.py:296
  91.4 2.5 %collective-permute-done.10.refs_1_ = f32[5,4,8,128]{3,2,1,0:T(8,128)S(1)} collective-permute-done((f32[5,4,8,128]{3,2,1,0:T(8,128)S(1)}, f32[5,4,8,128]{3,2,1,0:T(8,128)S(1)}, u32[]{:S(2)}, u32[]{:S(2)}) %collective-permute-start.10) | collective-permute-done | bytes 81952 | tf_op jit(solution)/shard_map/ppermute | solution.py:296
  94.1 5.4 %advance.10 = (f32[5,16,8,128]{3,2,1,0:T(8,128)S(1)}, f32[5,4,8,128]{3,2,1,0:T(8,128)S(1)}, f32[5,4,8,128]{3,2,1,0:T(8,128)S(1)}) custom-call(s32[2]{0:T(128)S(1)} %copy-done.4, s32[6]{0:T(128)S(1)} %copy-done.5, f32[3,8,128]{2,1,0:T(8,128)S(1)} %broadcast_in_dim.17.waves, f32[5,24,8,128]{3,2,1,0:T(8,128)S(1)} %copy-done.2, ...), custom_call_target="tpu_custom_call" | custom-call | tf_op jit(solution)/shard_map/advance/pallas_call | solution.py:231
  99.5 1.2 %collective-permute-start.12 = (f32[5,4,8,128]{3,2,1,0:T(8,128)S(1)}, f32[5,4,8,128]{3,2,1,0:T(8,128)S(1)}, u32[]{:S(2)}, u32[]{:S(2)}) collective-permute-start(f32[5,4,8,128]{3,2,1,0:T(8,128)S(1)} %get-tuple-element.47), channel_id=1, source_target_pairs={{0,4},{2,6},{4,8},{6,10},{8,12},{10,14},{12,0},{14,2},{1,5},{3,7},... | collective-permute-start | bytes 245768 | tf_op jit(solution)/shard_map/ppermute | solution.py:296
  100.8 2.6 %collective-permute-start.13 = (f32[5,4,8,128]{3,2,1,0:T(8,128)S(1)}, f32[5,4,8,128]{3,2,1,0:T(8,128)S(1)}, u32[]{:S(2)}, u32[]{:S(2)}) collective-permute-start(f32[5,4,8,128]{3,2,1,0:T(8,128)S(1)} %get-tuple-element.48), channel_id=1, source_target_pairs={{0,12},{2,14},{4,0},{6,2},{8,4},{10,6},{12,8},{14,10},{1,13},{3,15... | collective-permute-start | bytes 245768 | tf_op jit(solution)/shard_map/ppermute | solution.py:296
  103.4 2.5 %collective-permute-done.12.refs_1_ = f32[5,4,8,128]{3,2,1,0:T(8,128)S(1)} collective-permute-done((f32[5,4,8,128]{3,2,1,0:T(8,128)S(1)}, f32[5,4,8,128]{3,2,1,0:T(8,128)S(1)}, u32[]{:S(2)}, u32[]{:S(2)}) %collective-permute-start.12) | collective-permute-done | bytes 81952 | tf_op jit(solution)/shard_map/ppermute | solution.py:296
  106.2 5.4 %advance.11 = (f32[5,8,8,128]{3,2,1,0:T(8,128)S(1)}, f32[5,8,8,128]{3,2,1,0:T(8,128)S(1)}) custom-call(s32[2]{0:T(128)S(1)} %copy-done.4, s32[6]{0:T(128)S(1)} %copy-done.5, f32[3,8,128]{2,1,0:T(8,128)S(1)} %broadcast_in_dim.16.waves, f32[5,24,8,128]{3,2,1,0:T(8,128)S(1)} %copy-done.2, f32[15,24,8,128]{3,2,1,0:T(8,128)S(1)} %copy-done.1, ...), custom_call_target="tpu_custom_call" | custom-call | tf_op jit(solution)/shard_map/advance/pallas_call | solution.py:231
  111.5 1.6 %collective-permute-start.14 = (f32[5,8,8,128]{3,2,1,0:T(8,128)S(1)}, f32[5,8,8,128]{3,2,1,0:T(8,128)S(1)}, u32[]{:S(2)}, u32[]{:S(2)}) collective-permute-start(f32[5,8,8,128]{3,2,1,0:T(8,128)S(1)} %get-tuple-element.50), channel_id=1, source_target_pairs={{0,2},{2,0},{4,6},{6,4},{8,10},{10,8},{12,14},{14,12},{1,3},{3,1},... | collective-permute-start | bytes 491528 | tf_op jit(solution)/shard_map/ppermute | solution.py:298
  113.1 3.8 %collective-permute-done.14 = f32[5,8,8,128]{3,2,1,0:T(8,128)S(1)} collective-permute-done((f32[5,8,8,128]{3,2,1,0:T(8,128)S(1)}, f32[5,8,8,128]{3,2,1,0:T(8,128)S(1)}, u32[]{:S(2)}, u32[]{:S(2)}) %collective-permute-start.14) | collective-permute-done | bytes 163872 | tf_op jit(solution)/shard_map/ppermute | solution.py:298
  (40 shorter events, 7.0 us)
Async XLA Ops:
  3.1 34.5 %copy-start.9 = (f32[2]{0:T(128)S(1)}, f32[2]{0:T(128)}, u32[]{:S(2)}) copy-start(f32[2]{0:T(128)} %param.8) | copy-start | bytes 28
  3.1 35.1 %copy-start.10 = (f32[18]{0:T(128)S(1)}, f32[18]{0:T(128)}, u32[]{:S(2)}) copy-start(f32[18]{0:T(128)} %constant.21.clone) | copy-start | bytes 220
  3.1 38.1 %copy-start.4 = (s32[2]{0:T(128)S(1)}, s32[2]{0:T(128)}, u32[]{:S(2)}) copy-start(s32[2]{0:T(128)} %pad_add_fusion.who) | copy-start | bytes 28
  3.1 38.1 %copy-start.5 = (s32[6]{0:T(128)S(1)}, s32[6]{0:T(128)}, u32[]{:S(2)}) copy-start(s32[6]{0:T(128)} %phase_slot.11) | copy-start | bytes 76
  3.1 30.2 %collective-permute-start = (f32[25,8,8,128]{3,2,1,0:T(8,128)}, f32[25,8,8,128]{3,2,1,0:T(8,128)S(1)}, u32[]{:S(2)}, u32[]{:S(2)}) collective-permute-start(f32[25,8,8,128]{3,2,1,0:T(8,128)} %get-tuple-element.28), channel_id=1, source_target_pairs={{0,2},{2,0},{4,6},{6,4},{8,10},{10,8},{12,14},{14,12},{1,3},{3,1},... | collective-permute-start | bytes 2457608 | tf_op jit(solution)/shard_map/ppermute | solution.py:267
  6.1 13.8 %collective-permute-start.1 = (f32[25,4,8,128]{3,2,1,0:T(8,128)}, f32[25,4,8,128]{3,2,1,0:T(8,128)S(1)}, u32[]{:S(2)}, u32[]{:S(2)}) collective-permute-start(f32[25,4,8,128]{3,2,1,0:T(8,128)} %get-tuple-element.29), channel_id=1, source_target_pairs={{0,12},{2,6},{4,0},{6,10},{8,4},{10,14},{12,8},{14,2},{1,13},{3,7}... | collective-permute-start | bytes 1228808 | tf_op jit(solution)/shard_map/ppermute | solution.py:268
  9.7 18.2 %collective-permute-start.2 = (f32[25,4,8,128]{3,2,1,0:T(8,128)}, f32[25,4,8,128]{3,2,1,0:T(8,128)S(1)}, u32[]{:S(2)}, u32[]{:S(2)}) collective-permute-start(f32[25,4,8,128]{3,2,1,0:T(8,128)} %get-tuple-element.30), channel_id=1, source_target_pairs={{0,14},{2,4},{4,2},{6,8},{8,6},{10,12},{12,10},{14,0},{1,15},{3,5}... | collective-permute-start | bytes 1228808 | tf_op jit(solution)/shard_map/ppermute | solution.py:269
  19.9 13.4 %copy-start.7 = (f32[25,4,8,128]{3,2,1,0:T(8,128)}, f32[25,4,8,128]{3,2,1,0:T(8,128)S(1)}, u32[]{:S(2)}) copy-start(f32[25,4,8,128]{3,2,1,0:T(8,128)S(1)} %collective-permute-done.1.own_in) | copy-start | bytes 1228804
  27.9 5.4 %copy-start.8 = (f32[25,4,8,128]{3,2,1,0:T(8,128)}, f32[25,4,8,128]{3,2,1,0:T(8,128)S(1)}, u32[]{:S(2)}) copy-start(f32[25,4,8,128]{3,2,1,0:T(8,128)S(1)} %collective-permute-done.2.other_in) | copy-start | bytes 1228804
  33.3 0.9 copy-start.6
  37.6 3.5 %collective-permute-start.3 = (f32[15,24,8,128]{3,2,1,0:T(8,128)}, f32[15,24,8,128]{3,2,1,0:T(8,128)S(1)}, u32[]{:S(2)}, u32[]{:S(2)}) collective-permute-start(f32[15,24,8,128]{3,2,1,0:T(8,128)} %get-tuple-element.32.base_here), channel_id=1, source_target_pairs={{0,1},{1,0},{2,3},{3,2},{4,5},{5,4},{6,7},{7,6},{8,9},{9,8},{10,11... | collective-permute-start | bytes 4423688 | tf_op jit(solution)/shard_map/ppermute | solution.py:279
  41.1 1.4 %copy-start = (f32[15,24,8,128]{3,2,1,0:T(8,128)S(1)}, f32[15,24,8,128]{3,2,1,0:T(8,128)}, u32[]{:S(2)}) copy-start(f32[15,24,8,128]{3,2,1,0:T(8,128)} %get-tuple-element.32.base_here) | copy-start | bytes 4423684
  42.5 1.0 copy-start.2
  43.5 1.0 copy-start.3
  44.6 13.3 %copy-start.1 = (f32[15,24,8,128]{3,2,1,0:T(8,128)S(1)}, f32[15,24,8,128]{3,2,1,0:T(8,128)}, u32[]{:S(2)}) copy-start(f32[15,24,8,128]{3,2,1,0:T(8,128)} %get-tuple-element.32.base_here) | copy-start | bytes 4423684
  49.9 7.0 %collective-permute-start.4 = (f32[5,4,8,128]{3,2,1,0:T(8,128)S(1)}, f32[5,4,8,128]{3,2,1,0:T(8,128)S(1)}, u32[]{:S(2)}, u32[]{:S(2)}) collective-permute-start(f32[5,4,8,128]{3,2,1,0:T(8,128)S(1)} %get-tuple-element.35), channel_id=1, source_target_pairs={{0,4},{2,6},{4,8},{6,10},{8,12},{10,14},{12,0},{14,2},{1,5},{3,7},... | collective-permute-start | bytes 245768 | tf_op jit(solution)/shard_map/ppermute | solution.py:296
  51.8 6.0 %collective-permute-start.5 = (f32[5,4,8,128]{3,2,1,0:T(8,128)S(1)}, f32[5,4,8,128]{3,2,1,0:T(8,128)S(1)}, u32[]{:S(2)}, u32[]{:S(2)}) collective-permute-start(f32[5,4,8,128]{3,2,1,0:T(8,128)S(1)} %get-tuple-element.36), channel_id=1, source_target_pairs={{0,12},{2,14},{4,0},{6,2},{8,4},{10,6},{12,8},{14,10},{1,13},{3,15... | collective-permute-start | bytes 245768 | tf_op jit(solution)/shard_map/ppermute | solution.py:296
  63.2 6.7 %collective-permute-start.6 = (f32[5,4,8,128]{3,2,1,0:T(8,128)S(1)}, f32[5,4,8,128]{3,2,1,0:T(8,128)S(1)}, u32[]{:S(2)}, u32[]{:S(2)}) collective-permute-start(f32[5,4,8,128]{3,2,1,0:T(8,128)S(1)} %get-tuple-element.38), channel_id=1, source_target_pairs={{0,4},{2,6},{4,8},{6,10},{8,12},{10,14},{12,0},{14,2},{1,5},{3,7},... | collective-permute-start | bytes 245768 | tf_op jit(solution)/shard_map/ppermute | solution.py:296
  64.4 5.8 %collective-permute-start.7 = (f32[5,4,8,128]{3,2,1,0:T(8,128)S(1)}, f32[5,4,8,128]{3,2,1,0:T(8,128)S(1)}, u32[]{:S(2)}, u32[]{:S(2)}) collective-permute-start(f32[5,4,8,128]{3,2,1,0:T(8,128)S(1)} %get-tuple-element.39), channel_id=1, source_target_pairs={{0,12},{2,14},{4,0},{6,2},{8,4},{10,6},{12,8},{14,10},{1,13},{3,15... | collective-permute-start | bytes 245768 | tf_op jit(solution)/shard_map/ppermute | solution.py:296
  75.7 6.4 %collective-permute-start.8 = (f32[5,4,8,128]{3,2,1,0:T(8,128)S(1)}, f32[5,4,8,128]{3,2,1,0:T(8,128)S(1)}, u32[]{:S(2)}, u32[]{:S(2)}) collective-permute-start(f32[5,4,8,128]{3,2,1,0:T(8,128)S(1)} %get-tuple-element.41), channel_id=1, source_target_pairs={{0,4},{2,6},{4,8},{6,10},{8,12},{10,14},{12,0},{14,2},{1,5},{3,7},... | collective-permute-start | bytes 245768 | tf_op jit(solution)/shard_map/ppermute | solution.py:296
  76.1 6.0 %collective-permute-start.9 = (f32[5,4,8,128]{3,2,1,0:T(8,128)S(1)}, f32[5,4,8,128]{3,2,1,0:T(8,128)S(1)}, u32[]{:S(2)}, u32[]{:S(2)}) collective-permute-start(f32[5,4,8,128]{3,2,1,0:T(8,128)S(1)} %get-tuple-element.42), channel_id=1, source_target_pairs={{0,12},{2,14},{4,0},{6,2},{8,4},{10,6},{12,8},{14,10},{1,13},{3,15... | collective-permute-start | bytes 245768 | tf_op jit(solution)/shard_map/ppermute | solution.py:296
  87.5 6.4 %collective-permute-start.10 = (f32[5,4,8,128]{3,2,1,0:T(8,128)S(1)}, f32[5,4,8,128]{3,2,1,0:T(8,128)S(1)}, u32[]{:S(2)}, u32[]{:S(2)}) collective-permute-start(f32[5,4,8,128]{3,2,1,0:T(8,128)S(1)} %get-tuple-element.44), channel_id=1, source_target_pairs={{0,4},{2,6},{4,8},{6,10},{8,12},{10,14},{12,0},{14,2},{1,5},{3,7},... | collective-permute-start | bytes 245768 | tf_op jit(solution)/shard_map/ppermute | solution.py:296
  88.8 5.3 %collective-permute-start.11 = (f32[5,4,8,128]{3,2,1,0:T(8,128)S(1)}, f32[5,4,8,128]{3,2,1,0:T(8,128)S(1)}, u32[]{:S(2)}, u32[]{:S(2)}) collective-permute-start(f32[5,4,8,128]{3,2,1,0:T(8,128)S(1)} %get-tuple-element.45), channel_id=1, source_target_pairs={{0,12},{2,14},{4,0},{6,2},{8,4},{10,6},{12,8},{14,10},{1,13},{3,15... | collective-permute-start | bytes 245768 | tf_op jit(solution)/shard_map/ppermute | solution.py:296
  99.5 6.4 %collective-permute-start.12 = (f32[5,4,8,128]{3,2,1,0:T(8,128)S(1)}, f32[5,4,8,128]{3,2,1,0:T(8,128)S(1)}, u32[]{:S(2)}, u32[]{:S(2)}) collective-permute-start(f32[5,4,8,128]{3,2,1,0:T(8,128)S(1)} %get-tuple-element.47), channel_id=1, source_target_pairs={{0,4},{2,6},{4,8},{6,10},{8,12},{10,14},{12,0},{14,2},{1,5},{3,7},... | collective-permute-start | bytes 245768 | tf_op jit(solution)/shard_map/ppermute | solution.py:296
  100.8 5.3 %collective-permute-start.13 = (f32[5,4,8,128]{3,2,1,0:T(8,128)S(1)}, f32[5,4,8,128]{3,2,1,0:T(8,128)S(1)}, u32[]{:S(2)}, u32[]{:S(2)}) collective-permute-start(f32[5,4,8,128]{3,2,1,0:T(8,128)S(1)} %get-tuple-element.48), channel_id=1, source_target_pairs={{0,12},{2,14},{4,0},{6,2},{8,4},{10,6},{12,8},{14,10},{1,13},{3,15... | collective-permute-start | bytes 245768 | tf_op jit(solution)/shard_map/ppermute | solution.py:296
  111.5 5.4 %collective-permute-start.14 = (f32[5,8,8,128]{3,2,1,0:T(8,128)S(1)}, f32[5,8,8,128]{3,2,1,0:T(8,128)S(1)}, u32[]{:S(2)}, u32[]{:S(2)}) collective-permute-start(f32[5,8,8,128]{3,2,1,0:T(8,128)S(1)} %get-tuple-element.50), channel_id=1, source_target_pairs={{0,2},{2,0},{4,6},{6,4},{8,10},{10,8},{12,14},{14,12},{1,3},{3,1},... | collective-permute-start | bytes 491528 | tf_op jit(solution)/shard_map/ppermute | solution.py:298
where the time goes:
time: 118 us
  waiting for transfers between devices  44.5 us (38%)
  Pallas kernels  38 us (32%)
  starting transfers between devices  27.6 us (23%)
  local copies, waits for them, and re-layouts  5.46 us (5%)
  other arithmetic  2.04 us (2%)
    pallas_call x6, Pallas kernels, advance(): pl.pallas_call(functools.partial(advance_kernel, first_step, width, ends)...  32.2 us
    ppermute x5, starting transfers between devices, per_device(): lax.ppermute(left, 'space', behind)  13.6 us
    ppermute x5, waiting for transfers between devices, per_device(): lax.ppermute(right, 'space', ahead)  13.3 us
    ppermute x1, waiting for transfers between devices, per_device(): own_in = lax.ppermute(own_out, 'space', own)  10.2 us
    ppermute x1, waiting for transfers between devices, per_device(): other_in = lax.ppermute(other_out, 'space', other)  8.02 us
    ppermute x5, starting transfers between devices, per_device(): lax.ppermute(right, 'space', ahead)  5.92 us
    ppermute x1, waiting for transfers between devices, per_device(): swap_in = lax.ppermute(swap_out, 'space', swap)  5.38 us
    unnamed x22, local copies, waits for them, and re-layouts  4.38 us
  transfers between devices with their start and end apart: 15, of which 14 were waited for; matrix products, arithmetic and copies ran while one was open for 1% of the time, Pallas kernels for 0%

commit v1 on v0

--- a/solution.py
+++ b/solution.py
@@ -13,7 +13,7 @@
 FIELDS = 5
 TERMS = 26
 STAGES = 4
-UNROLL = 2
+UNROLL = 22
 
 
 VMEM = pl.BlockSpec(memory_space=pltpu.VMEM)
@@ -234,7 +234,7 @@
         in_specs=[SMEM, SMEM] + [VMEM] * (4 + len(carried)),
         out_specs=[VMEM] * len(outs),
         scratch_shapes=[scratch(FIELDS), scratch(FIELDS), scratch(TERMS)] + [scratch(FIELDS)] * 3,
-        compiler_params=pltpu.CompilerParams(vmem_limit_bytes=32 << 20),
+        compiler_params=pltpu.CompilerParams(vmem_limit_bytes=9 << 20),
         name="advance",
     )(who, phase_slot, waves, force, base_here, base_there, *carried)
 
@@ -262,6 +262,7 @@
         out_shape=[block(lead, tile), block(lead, width), block(lead, width)],
         in_specs=[SMEM] + [VMEM] * 3,
         out_specs=[VMEM] * 3,
+        compiler_params=pltpu.CompilerParams(vmem_limit_bytes=6 << 20),
         name="pack",
     )(who, perturbation, forcing, base_flow)
     swap_in = lax.ppermute(swap_out, "space", swap)
@@ -274,6 +275,7 @@
         out_shape=[block(FIELDS, planes), block(FIELDS, planes), block(FIELDS * slots, planes)],
         in_specs=[SMEM] + [VMEM] * 6,
         out_specs=[VMEM] * 3,
+        compiler_params=pltpu.CompilerParams(vmem_limit_bytes=8 << 20),
         name="assemble",
     )(who, perturbation, forcing, base_flow, swap_in, own_in, other_in)
     base_there = lax.ppermute(base_here, "vec", core)

time: 118 us -> 101 us (0.86)
  Pallas kernels: 38 us -> 17.9 us
  local copies, waits for them, and re-layouts: 5.46 us -> 8.49 us
    pallas_call x6, Pallas kernels: 32.2 us -> 16.5 us  [advance(): pl.pallas_call(functools.partial(advance_kernel, first_step, width, ends)...]
    unnamed x22 -> x24, local copies, waits for them, and re-layouts: 4.38 us -> 7.42 us
    pallas_call x1, Pallas kernels: 3.33 us -> 0.7 us  [per_device(): pl.pallas_call(functools.partial(assemble_kernel, width), out_shape=[bloc...]
    pallas_call x1, Pallas kernels: 2.49 us -> 0.65 us  [per_device(): pl.pallas_call(functools.partial(pack_kernel, width), out_shape=[block(le...]
where the time goes in v1:
time: 101 us
  waiting for transfers between devices  44.3 us (44%)
  starting transfers between devices  27.6 us (27%)
  Pallas kernels  17.9 us (18%)
  local copies, waits for them, and re-layouts  8.49 us (8%)
  other arithmetic  2.45 us (2%)
    pallas_call x6, Pallas kernels, advance(): pl.pallas_call(functools.partial(advance_kernel, first_step, width, ends)...  16.5 us
    ppermute x5, starting transfers between devices, per_device(): lax.ppermute(left, 'space', behind)  13.6 us
    ppermute x5, waiting for transfers between devices, per_device(): lax.ppermute(right, 'space', ahead)  13.3 us
    ppermute x1, waiting for transfers between devices, per_device(): own_in = lax.ppermute(own_out, 'space', own)  9.91 us
    ppermute x1, waiting for transfers between devices, per_device(): other_in = lax.ppermute(other_out, 'space', other)  8.13 us
    unnamed x24, local copies, waits for them, and re-layouts  7.42 us
    ppermute x5, starting transfers between devices, per_device(): lax.ppermute(right, 'space', ahead)  5.92 us
    ppermute x1, waiting for transfers between devices, per_device(): swap_in = lax.ppermute(swap_out, 'space', swap)  5.38 us
  transfers between devices with their start and end apart: 15, of which 14 were waited for; matrix products, arithmetic and copies ran while one was open for 1% of the time, Pallas kernels for 0%

profile of v1, /device:TPU:0, one launch (start us, length us, event | category | flops | bytes accessed | tf_op | source)
XLA Modules:
  0.0 100.8 jit_solution(1244904655153433607)
XLA Ops:
  0.1 1.0 %copy-done = f32[3,5,8,8,128]{4,3,2,1,0:T(8,128)S(1)} copy-done((f32[3,5,8,8,128]{4,3,2,1,0:T(8,128)S(1)}, f32[3,5,8,8,128]{4,3,2,1,0:T(8,128)}, u32[]{:S(2)}) %copy-start) | copy-done | bytes 491544
  1.1 1.0 copy-done.2
  3.7 3.0 %collective-permute-start = (f32[25,8,8,128]{3,2,1,0:T(8,128)S(1)}, f32[25,8,8,128]{3,2,1,0:T(8,128)S(1)}, u32[]{:S(2)}, u32[]{:S(2)}) collective-permute-start(f32[25,8,8,128]{3,2,1,0:T(8,128)S(1)} %get-tuple-element.28), channel_id=1, source_target_pairs={{0,2},{2,0},{4,6},{6,4},{8,10},{10,8},{12,14},{14,12},{1,3},{3,1},... | collective-permute-start | bytes 2457608 | tf_op jit(solution)/shard_map/ppermute | solution.py:268
  6.7 3.6 %collective-permute-start.1 = (f32[25,4,8,128]{3,2,1,0:T(8,128)S(1)}, f32[25,4,8,128]{3,2,1,0:T(8,128)S(1)}, u32[]{:S(2)}, u32[]{:S(2)}) collective-permute-start(f32[25,4,8,128]{3,2,1,0:T(8,128)S(1)} %get-tuple-element.29), channel_id=1, source_target_pairs={{0,12},{2,6},{4,0},{6,10},{8,4},{10,14},{12,8},{14,2},{1,13},{3,7}... | collective-permute-start | bytes 1228808 | tf_op jit(solution)/shard_map/ppermute | solution.py:269
  10.4 9.9 %collective-permute-done.1.own_in = f32[25,4,8,128]{3,2,1,0:T(8,128)S(1)} collective-permute-done((f32[25,4,8,128]{3,2,1,0:T(8,128)S(1)}, f32[25,4,8,128]{3,2,1,0:T(8,128)S(1)}, u32[]{:S(2)}, u32[]{:S(2)}) %collective-permute-start.1) | collective-permute-done | bytes 409632 | tf_op jit(solution)/shard_map/ppermute | solution.py:269
  20.3 8.1 %collective-permute-done.2.other_in = f32[25,4,8,128]{3,2,1,0:T(8,128)S(1)} collective-permute-done((f32[25,4,8,128]{3,2,1,0:T(8,128)S(1)}, f32[25,4,8,128]{3,2,1,0:T(8,128)S(1)}, u32[]{:S(2)}, u32[]{:S(2)}) %collective-permute-start.2) | collective-permute-done | bytes 409632 | tf_op jit(solution)/shard_map/ppermute | solution.py:270
  28.4 5.4 %collective-permute-done.swap_in = f32[25,8,8,128]{3,2,1,0:T(8,128)S(1)} collective-permute-done((f32[25,8,8,128]{3,2,1,0:T(8,128)S(1)}, f32[25,8,8,128]{3,2,1,0:T(8,128)S(1)}, u32[]{:S(2)}, u32[]{:S(2)}) %collective-permute-start) | collective-permute-done | bytes 819232 | tf_op jit(solution)/shard_map/ppermute | solution.py:268
  33.8 1.0 copy-done.3
  38.6 1.9 %collective-permute-done.3.base_there = f32[15,24,8,128]{3,2,1,0:T(8,128)S(1)} collective-permute-done((f32[15,24,8,128]{3,2,1,0:T(8,128)S(1)}, f32[15,24,8,128]{3,2,1,0:T(8,128)S(1)}, u32[]{:S(2)}, u32[]{:S(2)}) %collective-permute-start.3) | collective-permute-done | bytes 1474592 | tf_op jit(solution)/shard_map/ppermute | solution.py:281
  40.6 1.0 %copy-done.7 = f32[5,24,8,128]{3,2,1,0:T(8,128)S(1)} copy-done((f32[5,24,8,128]{3,2,1,0:T(8,128)S(1)}, f32[5,24,8,128]{3,2,1,0:T(8,128)}, u32[]{:S(2)}) %copy-start.7) | copy-done | bytes 491544
  41.6 2.6 %advance.6 = (f32[5,16,8,128]{3,2,1,0:T(8,128)S(1)}, f32[5,4,8,128]{3,2,1,0:T(8,128)S(1)}, f32[5,4,8,128]{3,2,1,0:T(8,128)S(1)}) custom-call(s32[2]{0:T(128)S(1)} %pad_add_fusion.who, s32[6]{0:T(128)S(1)} %copy-done.9, f32[3,8,128]{2,1,0:T(8,128)S(1)} %broadcast_in_dim.21.waves, f32[5,24,8,128]{3,2,1,0:T(8,128)S(1)} %get-tuple-element.31.force, ...), custom_call_target="tpu_custom_call" | custom-call | tf_op jit(solution)/shard_map/advance/pallas_call | solution.py:231
  44.2 1.9 %collective-permute-start.4 = (f32[5,4,8,128]{3,2,1,0:T(8,128)S(1)}, f32[5,4,8,128]{3,2,1,0:T(8,128)S(1)}, u32[]{:S(2)}, u32[]{:S(2)}) collective-permute-start(f32[5,4,8,128]{3,2,1,0:T(8,128)S(1)} %get-tuple-element.35), channel_id=1, source_target_pairs={{0,4},{2,6},{4,8},{6,10},{8,12},{10,14},{12,0},{14,2},{1,5},{3,7},... | collective-permute-start | bytes 245768 | tf_op jit(solution)/shard_map/ppermute | solution.py:298
  46.1 2.1 %collective-permute-start.5 = (f32[5,4,8,128]{3,2,1,0:T(8,128)S(1)}, f32[5,4,8,128]{3,2,1,0:T(8,128)S(1)}, u32[]{:S(2)}, u32[]{:S(2)}) collective-permute-start(f32[5,4,8,128]{3,2,1,0:T(8,128)S(1)} %get-tuple-element.36), channel_id=1, source_target_pairs={{0,12},{2,14},{4,0},{6,2},{8,4},{10,6},{12,8},{14,10},{1,13},{3,15... | collective-permute-start | bytes 245768 | tf_op jit(solution)/shard_map/ppermute | solution.py:298
  48.2 3.0 %collective-permute-done.4.refs_1_ = f32[5,4,8,128]{3,2,1,0:T(8,128)S(1)} collective-permute-done((f32[5,4,8,128]{3,2,1,0:T(8,128)S(1)}, f32[5,4,8,128]{3,2,1,0:T(8,128)S(1)}, u32[]{:S(2)}, u32[]{:S(2)}) %collective-permute-start.4) | collective-permute-done | bytes 81952 | tf_op jit(solution)/shard_map/ppermute | solution.py:298
  52.1 2.6 %advance.7 = (f32[5,16,8,128]{3,2,1,0:T(8,128)S(1)}, f32[5,4,8,128]{3,2,1,0:T(8,128)S(1)}, f32[5,4,8,128]{3,2,1,0:T(8,128)S(1)}) custom-call(s32[2]{0:T(128)S(1)} %pad_add_fusion.who, s32[6]{0:T(128)S(1)} %copy-done.9, f32[3,8,128]{2,1,0:T(8,128)S(1)} %broadcast_in_dim.20.waves, f32[5,24,8,128]{3,2,1,0:T(8,128)S(1)} %get-tuple-element.31.force, ...), custom_call_target="tpu_custom_call" | custom-call | tf_op jit(solution)/shard_map/advance/pallas_call | solution.py:231
  54.7 1.2 %collective-permute-start.6 = (f32[5,4,8,128]{3,2,1,0:T(8,128)S(1)}, f32[5,4,8,128]{3,2,1,0:T(8,128)S(1)}, u32[]{:S(2)}, u32[]{:S(2)}) collective-permute-start(f32[5,4,8,128]{3,2,1,0:T(8,128)S(1)} %get-tuple-element.38), channel_id=1, source_target_pairs={{0,4},{2,6},{4,8},{6,10},{8,12},{10,14},{12,0},{14,2},{1,5},{3,7},... | collective-permute-start | bytes 245768 | tf_op jit(solution)/shard_map/ppermute | solution.py:298
  55.9 2.7 %collective-permute-start.7 = (f32[5,4,8,128]{3,2,1,0:T(8,128)S(1)}, f32[5,4,8,128]{3,2,1,0:T(8,128)S(1)}, u32[]{:S(2)}, u32[]{:S(2)}) collective-permute-start(f32[5,4,8,128]{3,2,1,0:T(8,128)S(1)} %get-tuple-element.39), channel_id=1, source_target_pairs={{0,12},{2,14},{4,0},{6,2},{8,4},{10,6},{12,8},{14,10},{1,13},{3,15... | collective-permute-start | bytes 245768 | tf_op jit(solution)/shard_map/ppermute | solution.py:298
  58.6 2.8 %collective-permute-done.6.refs_1_ = f32[5,4,8,128]{3,2,1,0:T(8,128)S(1)} collective-permute-done((f32[5,4,8,128]{3,2,1,0:T(8,128)S(1)}, f32[5,4,8,128]{3,2,1,0:T(8,128)S(1)}, u32[]{:S(2)}, u32[]{:S(2)}) %collective-permute-start.6) | collective-permute-done | bytes 81952 | tf_op jit(solution)/shard_map/ppermute | solution.py:298
  61.8 2.6 %advance.8 = (f32[5,16,8,128]{3,2,1,0:T(8,128)S(1)}, f32[5,4,8,128]{3,2,1,0:T(8,128)S(1)}, f32[5,4,8,128]{3,2,1,0:T(8,128)S(1)}) custom-call(s32[2]{0:T(128)S(1)} %pad_add_fusion.who, s32[6]{0:T(128)S(1)} %copy-done.9, f32[3,8,128]{2,1,0:T(8,128)S(1)} %broadcast_in_dim.19.waves, f32[5,24,8,128]{3,2,1,0:T(8,128)S(1)} %get-tuple-element.31.force, ...), custom_call_target="tpu_custom_call" | custom-call | tf_op jit(solution)/shard_map/advance/pallas_call | solution.py:231
  64.8 3.5 %collective-permute-start.9 = (f32[5,4,8,128]{3,2,1,0:T(8,128)S(1)}, f32[5,4,8,128]{3,2,1,0:T(8,128)S(1)}, u32[]{:S(2)}, u32[]{:S(2)}) collective-permute-start(f32[5,4,8,128]{3,2,1,0:T(8,128)S(1)} %get-tuple-element.42), channel_id=1, source_target_pairs={{0,12},{2,14},{4,0},{6,2},{8,4},{10,6},{12,8},{14,10},{1,13},{3,15... | collective-permute-start | bytes 245768 | tf_op jit(solution)/shard_map/ppermute | solution.py:298
  68.3 2.5 %collective-permute-done.8.refs_1_ = f32[5,4,8,128]{3,2,1,0:T(8,128)S(1)} collective-permute-done((f32[5,4,8,128]{3,2,1,0:T(8,128)S(1)}, f32[5,4,8,128]{3,2,1,0:T(8,128)S(1)}, u32[]{:S(2)}, u32[]{:S(2)}) %collective-permute-start.8) | collective-permute-done | bytes 81952 | tf_op jit(solution)/shard_map/ppermute | solution.py:298
  70.9 2.6 %advance.9 = (f32[5,16,8,128]{3,2,1,0:T(8,128)S(1)}, f32[5,4,8,128]{3,2,1,0:T(8,128)S(1)}, f32[5,4,8,128]{3,2,1,0:T(8,128)S(1)}) custom-call(s32[2]{0:T(128)S(1)} %pad_add_fusion.who, s32[6]{0:T(128)S(1)} %copy-done.9, f32[3,8,128]{2,1,0:T(8,128)S(1)} %broadcast_in_dim.18.waves, f32[5,24,8,128]{3,2,1,0:T(8,128)S(1)} %get-tuple-element.31.force, ...), custom_call_target="tpu_custom_call" | custom-call | tf_op jit(solution)/shard_map/advance/pallas_call | solution.py:231
  73.5 1.2 %collective-permute-start.10 = (f32[5,4,8,128]{3,2,1,0:T(8,128)S(1)}, f32[5,4,8,128]{3,2,1,0:T(8,128)S(1)}, u32[]{:S(2)}, u32[]{:S(2)}) collective-permute-start(f32[5,4,8,128]{3,2,1,0:T(8,128)S(1)} %get-tuple-element.44), channel_id=1, source_target_pairs={{0,4},{2,6},{4,8},{6,10},{8,12},{10,14},{12,0},{14,2},{1,5},{3,7},... | collective-permute-start | bytes 245768 | tf_op jit(solution)/shard_map/ppermute | solution.py:298
  74.7 2.7 %collective-permute-start.11 = (f32[5,4,8,128]{3,2,1,0:T(8,128)S(1)}, f32[5,4,8,128]{3,2,1,0:T(8,128)S(1)}, u32[]{:S(2)}, u32[]{:S(2)}) collective-permute-start(f32[5,4,8,128]{3,2,1,0:T(8,128)S(1)} %get-tuple-element.45), channel_id=1, source_target_pairs={{0,12},{2,14},{4,0},{6,2},{8,4},{10,6},{12,8},{14,10},{1,13},{3,15... | collective-permute-start | bytes 245768 | tf_op jit(solution)/shard_map/ppermute | solution.py:298
  77.4 2.5 %collective-permute-done.10.refs_1_ = f32[5,4,8,128]{3,2,1,0:T(8,128)S(1)} collective-permute-done((f32[5,4,8,128]{3,2,1,0:T(8,128)S(1)}, f32[5,4,8,128]{3,2,1,0:T(8,128)S(1)}, u32[]{:S(2)}, u32[]{:S(2)}) %collective-permute-start.10) | collective-permute-done | bytes 81952 | tf_op jit(solution)/shard_map/ppermute | solution.py:298
  80.1 2.8 %advance.10 = (f32[5,16,8,128]{3,2,1,0:T(8,128)S(1)}, f32[5,4,8,128]{3,2,1,0:T(8,128)S(1)}, f32[5,4,8,128]{3,2,1,0:T(8,128)S(1)}) custom-call(s32[2]{0:T(128)S(1)} %pad_add_fusion.who, s32[6]{0:T(128)S(1)} %copy-done.9, f32[3,8,128]{2,1,0:T(8,128)S(1)} %broadcast_in_dim.17.waves, f32[5,24,8,128]{3,2,1,0:T(8,128)S(1)} %get-tuple-element.31.force, ...), custom_call_target="tpu_custom_call" | custom-call | tf_op jit(solution)/shard_map/advance/pallas_call | solution.py:231
  82.9 1.2 %collective-permute-start.12 = (f32[5,4,8,128]{3,2,1,0:T(8,128)S(1)}, f32[5,4,8,128]{3,2,1,0:T(8,128)S(1)}, u32[]{:S(2)}, u32[]{:S(2)}) collective-permute-start(f32[5,4,8,128]{3,2,1,0:T(8,128)S(1)} %get-tuple-element.47), channel_id=1, source_target_pairs={{0,4},{2,6},{4,8},{6,10},{8,12},{10,14},{12,0},{14,2},{1,5},{3,7},... | collective-permute-start | bytes 245768 | tf_op jit(solution)/shard_map/ppermute | solution.py:298
  84.2 2.6 %collective-permute-start.13 = (f32[5,4,8,128]{3,2,1,0:T(8,128)S(1)}, f32[5,4,8,128]{3,2,1,0:T(8,128)S(1)}, u32[]{:S(2)}, u32[]{:S(2)}) collective-permute-start(f32[5,4,8,128]{3,2,1,0:T(8,128)S(1)} %get-tuple-element.48), channel_id=1, source_target_pairs={{0,12},{2,14},{4,0},{6,2},{8,4},{10,6},{12,8},{14,10},{1,13},{3,15... | collective-permute-start | bytes 245768 | tf_op jit(solution)/shard_map/ppermute | solution.py:298
  86.8 2.5 %collective-permute-done.12.refs_1_ = f32[5,4,8,128]{3,2,1,0:T(8,128)S(1)} collective-permute-done((f32[5,4,8,128]{3,2,1,0:T(8,128)S(1)}, f32[5,4,8,128]{3,2,1,0:T(8,128)S(1)}, u32[]{:S(2)}, u32[]{:S(2)}) %collective-permute-start.12) | collective-permute-done | bytes 81952 | tf_op jit(solution)/shard_map/ppermute | solution.py:298
  89.6 3.3 %advance.11 = (f32[5,8,8,128]{3,2,1,0:T(8,128)S(1)}, f32[5,8,8,128]{3,2,1,0:T(8,128)}) custom-call(s32[2]{0:T(128)S(1)} %pad_add_fusion.who, s32[6]{0:T(128)S(1)} %copy-done.9, f32[3,8,128]{2,1,0:T(8,128)S(1)} %broadcast_in_dim.16.waves, f32[5,24,8,128]{3,2,1,0:T(8,128)S(1)} %get-tuple-element.31.force, f32[15,24,8,128]{3,2,1,0:T(8,128)S(1)} %get-tuple-element.32.base_here, ...), custom_call_target="tpu_custom_call" | custom-call | tf_op jit(solution)/shard_map/advance/pallas_call | solution.py:231
  93.5 1.5 %collective-permute-start.14 = (f32[5,8,8,128]{3,2,1,0:T(8,128)}, f32[5,8,8,128]{3,2,1,0:T(8,128)S(1)}, u32[]{:S(2)}, u32[]{:S(2)}) collective-permute-start(f32[5,8,8,128]{3,2,1,0:T(8,128)} %get-tuple-element.50), channel_id=1, source_target_pairs={{0,2},{2,0},{4,6},{6,4},{8,10},{10,8},{12,14},{14,12},{1,3},{3,1},... | collective-permute-start | bytes 491528 | tf_op jit(solution)/shard_map/ppermute | solution.py:300
  95.0 4.0 %collective-permute-done.14 = f32[5,8,8,128]{3,2,1,0:T(8,128)S(1)} collective-permute-done((f32[5,8,8,128]{3,2,1,0:T(8,128)}, f32[5,8,8,128]{3,2,1,0:T(8,128)S(1)}, u32[]{:S(2)}, u32[]{:S(2)}) %collective-permute-start.14) | collective-permute-done | bytes 163872 | tf_op jit(solution)/shard_map/ppermute | solution.py:300
  (42 shorter events, 10.2 us)
Async XLA Ops:
  0.1 1.0 %copy-start = (f32[3,5,8,8,128]{4,3,2,1,0:T(8,128)S(1)}, f32[3,5,8,8,128]{4,3,2,1,0:T(8,128)}, u32[]{:S(2)}) copy-start(f32[3,5,8,8,128]{4,3,2,1,0:T(8,128)} %base.3) | copy-start | bytes 1474564
  1.1 1.0 copy-start.2
  2.1 1.0 copy-start.4
  3.1 30.7 %copy-start.1 = (f32[3,5,8,8,128]{4,3,2,1,0:T(8,128)S(1)}, f32[3,5,8,8,128]{4,3,2,1,0:T(8,128)}, u32[]{:S(2)}) copy-start(f32[3,5,8,8,128]{4,3,2,1,0:T(8,128)} %base.3) | copy-start | bytes 1474564
  3.7 33.5 %copy-start.10 = (f32[2]{0:T(128)S(1)}, f32[2]{0:T(128)}, u32[]{:S(2)}) copy-start(f32[2]{0:T(128)} %param.8) | copy-start | bytes 28
  3.7 34.1 %copy-start.11 = (f32[18]{0:T(128)S(1)}, f32[18]{0:T(128)}, u32[]{:S(2)}) copy-start(f32[18]{0:T(128)} %constant.21.clone) | copy-start | bytes 220
  3.7 36.8 %copy-start.9 = (s32[6]{0:T(128)S(1)}, s32[6]{0:T(128)}, u32[]{:S(2)}) copy-start(s32[6]{0:T(128)} %phase_slot.11) | copy-start | bytes 76
  3.7 30.0 %collective-permute-start = (f32[25,8,8,128]{3,2,1,0:T(8,128)S(1)}, f32[25,8,8,128]{3,2,1,0:T(8,128)S(1)}, u32[]{:S(2)}, u32[]{:S(2)}) collective-permute-start(f32[25,8,8,128]{3,2,1,0:T(8,128)S(1)} %get-tuple-element.28), channel_id=1, source_target_pairs={{0,2},{2,0},{4,6},{6,4},{8,10},{10,8},{12,14},{14,12},{1,3},{3,1},... | collective-permute-start | bytes 2457608 | tf_op jit(solution)/shard_map/ppermute | solution.py:268
  6.7 13.5 %collective-permute-start.1 = (f32[25,4,8,128]{3,2,1,0:T(8,128)S(1)}, f32[25,4,8,128]{3,2,1,0:T(8,128)S(1)}, u32[]{:S(2)}, u32[]{:S(2)}) collective-permute-start(f32[25,4,8,128]{3,2,1,0:T(8,128)S(1)} %get-tuple-element.29), channel_id=1, source_target_pairs={{0,12},{2,6},{4,0},{6,10},{8,4},{10,14},{12,8},{14,2},{1,13},{3,7}... | collective-permute-start | bytes 1228808 | tf_op jit(solution)/shard_map/ppermute | solution.py:269
  10.4 18.0 %collective-permute-start.2 = (f32[25,4,8,128]{3,2,1,0:T(8,128)S(1)}, f32[25,4,8,128]{3,2,1,0:T(8,128)S(1)}, u32[]{:S(2)}, u32[]{:S(2)}) collective-permute-start(f32[25,4,8,128]{3,2,1,0:T(8,128)S(1)} %get-tuple-element.30), channel_id=1, source_target_pairs={{0,14},{2,4},{4,2},{6,8},{8,6},{10,12},{12,10},{14,0},{1,15},{3,5}... | collective-permute-start | bytes 1228808 | tf_op jit(solution)/shard_map/ppermute | solution.py:270
  33.8 1.0 copy-start.3
  34.7 1.0 copy-start.5
  36.4 0.8 copy-start.6
  37.2 3.3 %collective-permute-start.3 = (f32[15,24,8,128]{3,2,1,0:T(8,128)S(1)}, f32[15,24,8,128]{3,2,1,0:T(8,128)S(1)}, u32[]{:S(2)}, u32[]{:S(2)}) collective-permute-start(f32[15,24,8,128]{3,2,1,0:T(8,128)S(1)} %get-tuple-element.32.base_here), channel_id=1, source_target_pairs={{0,1},{1,0},{2,3},{3,2},{4,5},{5,4},{6,7},{7,6},{8,9},{9,8},{10,11... | collective-permute-start | bytes 4423688 | tf_op jit(solution)/shard_map/ppermute | solution.py:281
  40.6 1.0 %copy-start.7 = (f32[5,24,8,128]{3,2,1,0:T(8,128)S(1)}, f32[5,24,8,128]{3,2,1,0:T(8,128)}, u32[]{:S(2)}) copy-start(f32[5,24,8,128]{3,2,1,0:T(8,128)} %copy-done.6) | copy-start | bytes 1474564
  44.2 7.0 %collective-permute-start.4 = (f32[5,4,8,128]{3,2,1,0:T(8,128)S(1)}, f32[5,4,8,128]{3,2,1,0:T(8,128)S(1)}, u32[]{:S(2)}, u32[]{:S(2)}) collective-permute-start(f32[5,4,8,128]{3,2,1,0:T(8,128)S(1)} %get-tuple-element.35), channel_id=1, source_target_pairs={{0,4},{2,6},{4,8},{6,10},{8,12},{10,14},{12,0},{14,2},{1,5},{3,7},... | collective-permute-start | bytes 245768 | tf_op jit(solution)/shard_map/ppermute | solution.py:298
  46.1 6.0 %collective-permute-start.5 = (f32[5,4,8,128]{3,2,1,0:T(8,128)S(1)}, f32[5,4,8,128]{3,2,1,0:T(8,128)S(1)}, u32[]{:S(2)}, u32[]{:S(2)}) collective-permute-start(f32[5,4,8,128]{3,2,1,0:T(8,128)S(1)} %get-tuple-element.36), channel_id=1, source_target_pairs={{0,12},{2,14},{4,0},{6,2},{8,4},{10,6},{12,8},{14,10},{1,13},{3,15... | collective-permute-start | bytes 245768 | tf_op jit(solution)/shard_map/ppermute | solution.py:298
  54.7 6.7 %collective-permute-start.6 = (f32[5,4,8,128]{3,2,1,0:T(8,128)S(1)}, f32[5,4,8,128]{3,2,1,0:T(8,128)S(1)}, u32[]{:S(2)}, u32[]{:S(2)}) collective-permute-start(f32[5,4,8,128]{3,2,1,0:T(8,128)S(1)} %get-tuple-element.38), channel_id=1, source_target_pairs={{0,4},{2,6},{4,8},{6,10},{8,12},{10,14},{12,0},{14,2},{1,5},{3,7},... | collective-permute-start | bytes 245768 | tf_op jit(solution)/shard_map/ppermute | solution.py:298
  55.9 5.8 %collective-permute-start.7 = (f32[5,4,8,128]{3,2,1,0:T(8,128)S(1)}, f32[5,4,8,128]{3,2,1,0:T(8,128)S(1)}, u32[]{:S(2)}, u32[]{:S(2)}) collective-permute-start(f32[5,4,8,128]{3,2,1,0:T(8,128)S(1)} %get-tuple-element.39), channel_id=1, source_target_pairs={{0,12},{2,14},{4,0},{6,2},{8,4},{10,6},{12,8},{14,10},{1,13},{3,15... | collective-permute-start | bytes 245768 | tf_op jit(solution)/shard_map/ppermute | solution.py:298
  64.4 6.4 %collective-permute-start.8 = (f32[5,4,8,128]{3,2,1,0:T(8,128)S(1)}, f32[5,4,8,128]{3,2,1,0:T(8,128)S(1)}, u32[]{:S(2)}, u32[]{:S(2)}) collective-permute-start(f32[5,4,8,128]{3,2,1,0:T(8,128)S(1)} %get-tuple-element.41), channel_id=1, source_target_pairs={{0,4},{2,6},{4,8},{6,10},{8,12},{10,14},{12,0},{14,2},{1,5},{3,7},... | collective-permute-start | bytes 245768 | tf_op jit(solution)/shard_map/ppermute | solution.py:298
  64.8 6.0 %collective-permute-start.9 = (f32[5,4,8,128]{3,2,1,0:T(8,128)S(1)}, f32[5,4,8,128]{3,2,1,0:T(8,128)S(1)}, u32[]{:S(2)}, u32[]{:S(2)}) collective-permute-start(f32[5,4,8,128]{3,2,1,0:T(8,128)S(1)} %get-tuple-element.42), channel_id=1, source_target_pairs={{0,12},{2,14},{4,0},{6,2},{8,4},{10,6},{12,8},{14,10},{1,13},{3,15... | collective-permute-start | bytes 245768 | tf_op jit(solution)/shard_map/ppermute | solution.py:298
  73.5 6.4 %collective-permute-start.10 = (f32[5,4,8,128]{3,2,1,0:T(8,128)S(1)}, f32[5,4,8,128]{3,2,1,0:T(8,128)S(1)}, u32[]{:S(2)}, u32[]{:S(2)}) collective-permute-start(f32[5,4,8,128]{3,2,1,0:T(8,128)S(1)} %get-tuple-element.44), channel_id=1, source_target_pairs={{0,4},{2,6},{4,8},{6,10},{8,12},{10,14},{12,0},{14,2},{1,5},{3,7},... | collective-permute-start | bytes 245768 | tf_op jit(solution)/shard_map/ppermute | solution.py:298
  74.7 5.3 %collective-permute-start.11 = (f32[5,4,8,128]{3,2,1,0:T(8,128)S(1)}, f32[5,4,8,128]{3,2,1,0:T(8,128)S(1)}, u32[]{:S(2)}, u32[]{:S(2)}) collective-permute-start(f32[5,4,8,128]{3,2,1,0:T(8,128)S(1)} %get-tuple-element.45), channel_id=1, source_target_pairs={{0,12},{2,14},{4,0},{6,2},{8,4},{10,6},{12,8},{14,10},{1,13},{3,15... | collective-permute-start | bytes 245768 | tf_op jit(solution)/shard_map/ppermute | solution.py:298
  82.9 6.4 %collective-permute-start.12 = (f32[5,4,8,128]{3,2,1,0:T(8,128)S(1)}, f32[5,4,8,128]{3,2,1,0:T(8,128)S(1)}, u32[]{:S(2)}, u32[]{:S(2)}) collective-permute-start(f32[5,4,8,128]{3,2,1,0:T(8,128)S(1)} %get-tuple-element.47), channel_id=1, source_target_pairs={{0,4},{2,6},{4,8},{6,10},{8,12},{10,14},{12,0},{14,2},{1,5},{3,7},... | collective-permute-start | bytes 245768 | tf_op jit(solution)/shard_map/ppermute | solution.py:298
  84.2 5.3 %collective-permute-start.13 = (f32[5,4,8,128]{3,2,1,0:T(8,128)S(1)}, f32[5,4,8,128]{3,2,1,0:T(8,128)S(1)}, u32[]{:S(2)}, u32[]{:S(2)}) collective-permute-start(f32[5,4,8,128]{3,2,1,0:T(8,128)S(1)} %get-tuple-element.48), channel_id=1, source_target_pairs={{0,12},{2,14},{4,0},{6,2},{8,4},{10,6},{12,8},{14,10},{1,13},{3,15... | collective-permute-start | bytes 245768 | tf_op jit(solution)/shard_map/ppermute | solution.py:298
  92.9 0.7 copy-start.8
  93.5 5.5 %collective-permute-start.14 = (f32[5,8,8,128]{3,2,1,0:T(8,128)}, f32[5,8,8,128]{3,2,1,0:T(8,128)S(1)}, u32[]{:S(2)}, u32[]{:S(2)}) collective-permute-start(f32[5,8,8,128]{3,2,1,0:T(8,128)} %get-tuple-element.50), channel_id=1, source_target_pairs={{0,2},{2,0},{4,6},{6,4},{8,10},{10,8},{12,14},{14,12},{1,3},{3,1},... | collective-permute-start | bytes 491528 | tf_op jit(solution)/shard_map/ppermute | solution.py:300

commit v2 on v0

v2 whole, which is shorter than its diff:
```python
import functools

import jax
import jax.numpy as jnp
from jax import lax
from jax.experimental import pallas as pl
from jax.experimental.pallas import tpu as pltpu
from jax.sharding import PartitionSpec as P

HEAT_RATIO = 1.4
VISCOSITY = 0.1
TIME_STEP = 0.4
FIELDS = 5
TERMS = 26
STAGES = 4


VMEM = pl.BlockSpec(memory_space=pltpu.VMEM)
SMEM = pl.BlockSpec(memory_space=pltpu.SMEM)
HBM = pl.BlockSpec(memory_space=pltpu.HBM)


def parity():
    return lax.rem(lax.axis_index("space"), 2)


def in_place(*arrays):
    return [pltpu.with_memory_space_constraint(array, pltpu.HBM) for array in arrays]


def after(values, *earlier):
    return lax.optimization_barrier((values, *earlier))[0]


def pallas(kernel, name, outs, in_specs, scratch=(), grant=4):
    return pl.pallas_call(
        kernel,
        out_shape=outs,
        in_specs=in_specs,
        out_specs=[VMEM] * len(outs),
        scratch_shapes=scratch,
        compiler_params=pltpu.CompilerParams(vmem_limit_bytes=grant << 20),
        name=name,
    )


def pack_kernel(sets, widths, reach, which, phase_slot, pert, force, base, base_peer, *refs):
    sends, kept, sem = refs[: 3 * len(which)], refs[3 * len(which) : -1], refs[-1]
    mine = parity()
    core = lax.axis_index("vec")
    other = 1 - mine
    tile = pert.shape[2]
    local = base.shape[0]
    waits = []

    def copy(source, target, at, count):
        into = target.at[:, pl.ds(at, count)]
        waits.append(pltpu.make_async_copy(source(), into, sem.at[len(waits)]))
        waits[-1].start()

    def copy_base(step, cells, target, at, count):
        into = target.at[:, pl.ds(at, count)]
        held = lax.div(phase_slot[step], local) == core
        row = lax.rem(phase_slot[step], local)
        first, second = [
            pltpu.make_async_copy(array.at[row, :, cells], into, sem.at[len(waits)]) for array in (base, base_peer)
        ]
        pl.when(held)(first.start)
        pl.when(jnp.logical_not(held))(second.start)
        waits.append(first)

    for index, chosen in enumerate(which):
        swap_out, own_out, other_out = sends[3 * index : 3 * index + 3]
        at_swap = at_edge = 0
        if chosen == 0:
            for array, width in ((pert, widths[0]), (force, reach)):
                edge = pl.ds(mine * (tile - width), width)
                copy(lambda: array.at[other], swap_out, at_swap, tile)
                copy(lambda: array.at[mine, :, edge], own_out, at_edge, width)
                copy(lambda: array.at[other, :, edge], other_out, at_edge, width)
                at_swap += tile
                at_edge += width
        for step in sets[chosen]:
            half, width = tile // 2, widths[step]
            copy_base(step, pl.ds(core * half, half), swap_out, at_swap, half)
            edge = pl.ds(mine * (tile - width) + core * (width // 2), width // 2)
            for target in (own_out, other_out):
                copy_base(step, edge, target, at_edge, width // 2)
            at_swap += half
            at_edge += width // 2
    if kept:
        held_state, held_base = kept
        copy(lambda: pert.at[mine], held_state, 0, tile)
        copy(lambda: force.at[mine], held_state, tile, tile)
        for step in range(held_base.shape[1] // tile):
            copy_base(step, pl.ds(0, tile), held_base, step * tile, tile)
    for wait in waits:
        wait.wait()


def waves_kernel(moments, frequency, waves):
    shape = waves.shape[1:]
    rows = lax.broadcasted_iota(jnp.int32, shape, 0)
    for first in range(0, len(moments), shape[0]):
        chunk = moments[first : first + shape[0]]
        angle = jnp.zeros(shape, jnp.float32)
        for row, moment in enumerate(chunk):
            angle = jnp.where(rows == row, moment, angle)
        wave = jnp.cos(frequency[parity()] * angle)
        for row in range(len(chunk)):
            waves[first + row] = jnp.broadcast_to(wave[row : row + 1], shape)


def neighbours(ref, field, at, count):
    block = ref[field, pl.ds(at - 1, count + 2)]
    centre = block[1 : count + 1]
    return (
        centre,
        (block[2:], block[:count]),
        (pltpu.roll(centre, centre.shape[1] - 1, 1), pltpu.roll(centre, 1, 1)),
        (pltpu.roll(centre, centre.shape[2] - 1, 2), pltpu.roll(centre, 1, 2)),
    )


def base_terms(base, terms, at, count):
    centre, diff = [], []
    for field in range(FIELDS):
        mid, along_x, along_y, along_z = neighbours(base, field, at, count)
        centre.append(mid)
        diff.append([up - down for up, down in (along_x, along_y, along_z)])
    density, pressure = centre[0], centre[4]
    inverse = 1.0 / density
    square = 0.5 * inverse * inverse
    divergence = diff[1][0] + diff[2][1] + diff[3][2]
    out = [-0.5 * centre[1 + j] for j in range(3)]
    out += [-0.5 * diff[0][j] for j in range(3)]
    out += [-0.5 * density, -0.5 * divergence]
    for j in range(3):
        for k in range(3):
            slope = -0.5 * diff[1 + k][j]
            out.append(slope - 6.0 * VISCOSITY if j == k else slope)
    out += [-0.5 * inverse]
    out += [diff[4][k] * square for k in range(3)]
    out += [-0.5 * diff[4][j] for j in range(3)]
    out += [-0.5 * HEAT_RATIO * pressure, -0.5 * HEAT_RATIO * divergence]
    for index, value in enumerate(out):
        terms[index, pl.ds(at, count)] = value


def terms_kernel(steps, widths, at_held, at_swap, at_edge, reach, held_base, *refs):
    mine_in, peer_in, outs, held = refs[:3], refs[3:6], refs[6:-1], refs[-1]
    mine = parity()
    core = lax.axis_index("vec")
    planes = held.shape[1]
    tile = planes // 2 - reach
    half = tile // 2
    at_peer_swap = at_peer_edge = 0
    for step, terms in zip(steps, outs):
        width = widths[step]
        held[:, pl.ds(reach + mine * tile, tile)] = held_base[:, at_held : at_held + tile]
        partner = reach + (1 - mine) * tile
        near, far = reach - width, reach + 2 * tile
        own_at = near + (1 - mine) * (far - near)
        other_at = near + mine * (far - near)
        for (swap_in, own_in, other_in), who, swap_lo, edge_lo in (
            (mine_in, core, at_swap, at_edge),
            (peer_in, 1 - core, at_peer_swap, at_peer_edge),
        ):
            edge = width // 2
            held[:, pl.ds(partner + who * half, half)] = swap_in[:, swap_lo : swap_lo + half]
            held[:, pl.ds(own_at + who * edge, edge)] = own_in[:, edge_lo : edge_lo + edge]
            held[:, pl.ds(other_at + who * edge, edge)] = other_in[:, edge_lo : edge_lo + edge]
        base_terms(held, terms, near + 1, planes - 2 * near - 2)
        at_held += tile
        at_swap, at_peer_swap = at_swap + half, at_peer_swap + half
        at_edge, at_peer_edge = at_edge + width // 2, at_peer_edge + width // 2


def rates(state, terms, force, wave, at, count):
    here = pl.ds(at, count)
    centre, diff, around = [], [], []
    for field in range(FIELDS):
        mid, along_x, along_y, along_z = neighbours(state, field, at, count)
        centre.append(mid)
        diff.append([up - down for up, down in (along_x, along_y, along_z)])
        if 1 <= field <= 3:
            around.append((along_x[0] + along_x[1]) + (along_y[0] + along_y[1]) + (along_z[0] + along_z[1]))
    term = lambda index: terms[index, here]
    speed = [term(j) for j in range(3)]
    spread = diff[1][0] + diff[2][1] + diff[3][2]

    def carried(field, first, stride):
        total = force[field, here] * wave
        for j in range(3):
            total = total + (speed[j] * diff[field][j] + centre[1 + j] * term(first + stride * j))
        return total

    out = [carried(0, 3, 1) + (term(6) * spread + centre[0] * term(7))]
    inverse = term(17)
    for k in range(3):
        pull = inverse * diff[4][k] + centre[0] * term(18 + k)
        out.append(carried(1 + k, 8 + k, 3) + (pull + VISCOSITY * around[k]))
    out.append(carried(4, 21, 1) + (term(24) * spread + centre[4] * term(25)))
    return out


def one_step(inset, state, force, terms, waves, second, third, fourth):
    planes = state.shape[1]

    def stage(number, source, size, wave, target):
        at, count = inset + number, planes - 2 * (inset + number)
        here = pl.ds(at, count)
        for field, rate in enumerate(rates(source, terms, force, wave[None], at, count)):
            target[field, here] = state[field, here] + size * rate

    stage(1, state, 0.5 * TIME_STEP, waves[0], second)
    stage(2, second, 0.5 * TIME_STEP, waves[1], third)
    stage(3, third, TIME_STEP, waves[1], fourth)
    at, count = inset + STAGES, planes - 2 * (inset + STAGES)
    here = pl.ds(at, count)
    for field, rate in enumerate(rates(fourth, terms, force, waves[2][None], at, count)):
        mixed = second[field, here] + fourth[field, here] + 2.0 * third[field, here] - state[field, here]
        state[field, here] = mixed * (1.0 / 3.0) + (TIME_STEP / 6.0) * rate


def advance_kernel(steps, widths, reach, first, last, next_width, waves, *refs):
    terms, refs = refs[: len(steps)], refs[len(steps) :]
    width = widths[steps[0]]
    state, second, third, fourth = refs[-4:]
    refs = refs[:-4]
    planes = state.shape[1]
    tile = planes // 2 - reach
    mine = parity()
    near, far = reach - width, reach + 2 * tile
    if first:
        held_state, swap_in, own_in, other_in, force, *outs = refs
        here, there = pl.ds(reach + mine * tile, tile), pl.ds(reach + (1 - mine) * tile, tile)
        state[:, here] = held_state[:, 0:tile]
        state[:, there] = swap_in[:, 0:tile]
        state[:, pl.ds(near + (1 - mine) * (far - near), width)] = own_in[:, 0:width]
        state[:, pl.ds(near + mine * (far - near), width)] = other_in[:, 0:width]
        force[:, here] = held_state[:, tile : 2 * tile]
        force[:, there] = swap_in[:, tile : 2 * tile]
        force[:, pl.ds((1 - mine) * far, reach)] = own_in[:, width : width + reach]
        force[:, pl.ds(mine * far, reach)] = other_in[:, width : width + reach]
    else:
        force, slab_in, left_in, right_in, *outs = refs
        state[:, near:reach] = left_in[...]
        state[:, reach:far] = slab_in[...]
        state[:, far : far + width] = right_in[...]
    for index, step in enumerate(steps):
        wave = [waves[3 * step + which] for which in range(3)]
        one_step(reach - widths[step], state, force, terms[index], wave, second, third, fourth)
    if last:
        keep, give = outs
        keep[...] = state[:, pl.ds(reach + mine * tile, tile)]
        give[...] = state[:, pl.ds(reach + (1 - mine) * tile, tile)]
    else:
        slab, left, right = outs
        slab[...] = state[:, reach:far]
        left[...] = state[:, reach : reach + next_width]
        right[...] = state[:, far - next_width : far]


def per_device(perturbation, forcing, frequency, base_flow, phase_slot):
    _, _, tile, rows, lanes = perturbation.shape
    count = lax.axis_size("space")
    steps = phase_slot.shape[0]
    block = lambda *lead: jax.ShapeDtypeStruct((*lead, rows, lanes), jnp.float32)
    scratch = lambda *lead: pltpu.VMEM((*lead, rows, lanes), jnp.float32)

    rounds = [list(range(start, min(start + 2, steps))) for start in range(0, steps, 2)]
    sets = [each for each in (rounds[0], sum(rounds[1:], [])) if each]
    widths = {step: STAGES * (each[-1] - step + 1) for each in rounds for step in each}
    reach = max(widths.values())
    planes = 2 * (tile + reach)

    swap = [(i, i ^ 1) for i in range(count)]
    own = [(i, (i + 2 * (1 if i % 2 else -1)) % count) for i in range(count)]
    other = [(i, (i + (1 if i % 2 else -1)) % count) for i in range(count)]
    ahead = [(i, (i + 2) % count) for i in range(count)]
    behind = [(i, (i - 2) % count) for i in range(count)]
    core = [(0, 1), (1, 0)]

    base_peer = lax.ppermute(base_flow, "vec", core)
    moments = [step * TIME_STEP + part for step in range(steps) for part in (0.0, 0.5 * TIME_STEP, TIME_STEP)]

    def pack(which, keep):
        sends, copies = [], 0
        for chosen in which:
            group, start = sets[chosen], chosen == 0
            swapped = len(group) * (tile // 2) + (2 * tile if start else 0)
            edges = sum(widths[step] // 2 for step in group) + (widths[0] + reach if start else 0)
            sends += [block(FIELDS, swapped), block(FIELDS, edges), block(FIELDS, edges)]
            copies += 3 * len(group) + (6 if start else 0)
        kept = [block(FIELDS, 2 * tile), block(FIELDS, steps * tile)] if keep else []
        return pallas(
            functools.partial(pack_kernel, sets, widths, reach, which),
            "pack",
            sends + kept,
            [SMEM] + [HBM] * 4,
            [pltpu.SemaphoreType.DMA((copies + (2 + steps if keep else 0),))],
        )(*in_place(phase_slot, perturbation, forcing, base_flow), base_peer)

    def exchange(packed):
        return [lax.ppermute(part, "space", perm) for part, perm in zip(packed, (swap, own, other))]

    def factors(which, arrived):
        group = sets[which]
        at_swap, at_edge = (2 * tile, widths[0] + reach) if which == 0 else (0, 0)
        crossed = [
            lax.ppermute(part[:, at:] if at else part, "vec", core)
            for part, at in zip(arrived, (at_swap, at_edge, at_edge))
        ]
        return pallas(
            functools.partial(terms_kernel, group, widths, group[0] * tile, at_swap, at_edge, reach),
            "terms",
            [block(TERMS, planes)] * len(group),
            [VMEM] * 7,
            [scratch(FIELDS, planes)],
            grant=2,
        )(held_base, *arrived, *crossed)

    def advance(which, operands):
        group = rounds[which]
        first, last = which == 0, which == len(rounds) - 1
        next_width = 0 if last else widths[rounds[which + 1][0]]
        if last:
            outs = [block(FIELDS, tile)] * 2
        else:
            outs = [block(FIELDS, 2 * tile), block(FIELDS, next_width), block(FIELDS, next_width)]
        if first:
            outs = [block(FIELDS, planes)] + outs
        return pallas(
            functools.partial(advance_kernel, group, widths, reach, first, last, next_width),
            "advance",
            outs,
            [VMEM] * (1 + len(operands)),
            [scratch(FIELDS, planes)] * 4,
            grant=8,
        )(waves, *operands)

    first = exchange(pack([0], False))
    *later, held_state, held_base = pack(range(1, len(sets)), True)
    (waves,) = pallas(functools.partial(waves_kernel, moments), "waves", [block(3 * steps)], [SMEM])(*in_place(frequency))
    packed = [None] + [later[3 * which : 3 * which + 3] for which in range(len(sets) - 1)]
    arrived = exchange(after(packed[1], first[1])) if len(sets) > 1 else None
    first, held_state, held_base, waves = lax.optimization_barrier((first, held_state, held_base, waves))
    terms = dict(zip(sets[0], factors(0, first)))
    force, *outs = advance(0, [*[terms[step] for step in rounds[0]], held_state, *first])
    for which in range(1, len(rounds)):
        slab, left, right = outs
        left_in = lax.ppermute(right, "space", ahead)
        right_in = lax.ppermute(left, "space", behind)
        if which < len(sets):
            arrived = after(arrived, slab)
            following = exchange(after(packed[which + 1], arrived)) if which + 1 < len(sets) else None
            terms |= zip(sets[which], factors(which, arrived))
            arrived = following
        outs = advance(which, [*[terms[step] for step in rounds[which]], force, slab, left_in, right_in])
    keep, give = outs
    given = lax.ppermute(give, "space", swap)
    mine = parity()
    low, high = jnp.where(mine == 0, keep, given), jnp.where(mine == 0, given, keep)
    return jnp.stack([low, high])


def solution(mesh):
    return jax.shard_map(
        per_device,
        mesh=mesh,
        in_specs=(
            P(("groups", "vec"), None, "space", None, None),
            P(("groups", "vec"), None, "space", None, None),
            P(("groups", "vec")),
            P("vec", None, "space", None, None),
            P(),
        ),
        out_specs=P(("groups", "vec"), None, "space", None, None),
        check_vma=False,
    )
```

time: 118 us -> 84.3 us (0.71)
  Pallas kernels: 38 us -> 21.1 us
  starting transfers between devices: 27.6 us -> 22.1 us
  local copies, waits for them, and re-layouts: 5.46 us -> 0.03 us
  waiting for transfers between devices: 44.5 us -> 40 us
  other arithmetic: 2.04 us -> 0.77 us
    pallas_call x8, Pallas kernels: 38 us -> 21.1 us  [the longest x3 13.6 us: advance(): pallas(functools.partial(advance_kernel, group, widths, reach, first, las...]
    ppermute x14 -> x17, waiting for transfers between devices: 40.6 us -> 34.9 us  [the longest x6 21 us: exchange(): lax.ppermute(part, 'space', perm)]
    unnamed x22 -> x0, local copies, waits for them, and re-layouts: 4.38 us -> none
    ppermute x14 -> x17, starting transfers between devices: 26.1 us -> 21.7 us  [the longest x6 12.4 us: exchange(): lax.ppermute(part, 'space', perm)]
    ppermute x1, starting transfers between devices: 1.55 us -> 0.33 us  [per_device(): given = lax.ppermute(give, 'space', swap)]
    ppermute x1, waiting for transfers between devices: 3.83 us -> 5.05 us  [per_device(): given = lax.ppermute(give, 'space', swap)]
  transfers between devices with their start and end apart: 15 -> 18, of which waited for: 14 -> 11; matrix products, arithmetic and copies ran while one was open for 1% -> 0% of each run, Pallas kernels for 0% -> 12%
where the time goes in v2:
time: 84.3 us; the launch traced here: 84.1 us
  waiting for transfers between devices  40 us (47%)
  starting transfers between devices  22.1 us (26%)
  Pallas kernels  21.1 us (25%)
    ppermute x6, waiting for transfers between devices, exchange(): lax.ppermute(part, 'space', perm)  21 us
    pallas_call x3, Pallas kernels, advance(): pallas(functools.partial(advance_kernel, group, widths, reach, first, las...  13.6 us
    ppermute x6, starting transfers between devices, exchange(): lax.ppermute(part, 'space', perm)  12.4 us
    ppermute x2, waiting for transfers between devices, per_device(): left_in = lax.ppermute(right, 'space', ahead)  8.56 us
    ppermute x2, starting transfers between devices, per_device(): right_in = lax.ppermute(left, 'space', behind)  7.07 us
    ppermute x1, waiting for transfers between devices, per_device(): given = lax.ppermute(give, 'space', swap)  5.05 us
    pallas_call x2, Pallas kernels, pack(): pallas(functools.partial(pack_kernel, sets, widths, reach, which), 'pack'...  4.44 us
    ppermute x2, waiting for transfers between devices, per_device(): right_in = lax.ppermute(left, 'space', behind)  2.62 us
  transfers between devices with their start and end apart: 18, of which 11 were waited for; matrix products, arithmetic and copies ran while one was open for 0% of the time, Pallas kernels for 12%

profile of v2, /device:TPU:0, one launch (start us, length us, event | category | flops | bytes accessed | tf_op | source)
XLA Modules:
  0.0 84.1 jit_solution(11014050703997296866)
XLA Ops:
  0.0 0.5 collective-permute-start
  0.5 1.7 %collective-permute-done.base_peer = f32[3,5,8,8,128]{4,3,2,1,0:T(8,128)S(1)} collective-permute-done((f32[3,5,8,8,128]{4,3,2,1,0:T(8,128)}, f32[3,5,8,8,128]{4,3,2,1,0:T(8,128)S(1)}, u32[]{:S(2)}, u32[]{:S(2)}) %collective-permute-start) | collective-permute-done | bytes 491552 | tf_op jit(solution)/shard_map/ppermute | solution.py:285
  2.2 2.1 %pack.2 = (f32[5,24,8,128]{3,2,1,0:T(8,128)S(1)}, f32[5,22,8,128]{3,2,1,0:T(8,128)S(1)}, f32[5,22,8,128]{3,2,1,0:T(8,128)S(1)}) custom-call(s32[6]{0:T(128)} %phase_slot.3, f32[2,5,8,8,128]{4,3,2,1,0:T(8,128)} %pert.3, f32[2,5,8,8,128]{4,3,2,1,0:T(8,128)} %force.3, f32[3,5,8,8,128]{4,3,2,1,0:T(8,128)} %base.3, ...), custom_call_target="tpu_custom_call" | custom-call | tf_op jit(solution)/shard_map/pack/pallas_call | solution.py:297
  4.3 5.0 %collective-permute-start.2 = (f32[5,22,8,128]{3,2,1,0:T(8,128)S(1)}, f32[5,22,8,128]{3,2,1,0:T(8,128)S(1)}, u32[]{:S(2)}, u32[]{:S(2)}) collective-permute-start(f32[5,22,8,128]{3,2,1,0:T(8,128)S(1)} %get-tuple-element.41), channel_id=1, source_target_pairs={{0,12},{2,6},{4,0},{6,10},{8,4},{10,14},{12,8},{14,2},{1,13},{3,7}... | collective-permute-start | bytes 1351688 | tf_op jit(solution)/shard_map/ppermute | solution.py:306
  9.3 1.9 %collective-permute-start.3 = (f32[5,22,8,128]{3,2,1,0:T(8,128)S(1)}, f32[5,22,8,128]{3,2,1,0:T(8,128)S(1)}, u32[]{:S(2)}, u32[]{:S(2)}) collective-permute-start(f32[5,22,8,128]{3,2,1,0:T(8,128)S(1)} %get-tuple-element.42), channel_id=1, source_target_pairs={{0,14},{2,4},{4,2},{6,8},{8,6},{10,12},{12,10},{14,0},{1,15},{3,5}... | collective-permute-start | bytes 1351688 | tf_op jit(solution)/shard_map/ppermute | solution.py:306
  11.2 2.3 %pack.3 = (f32[5,16,8,128]{3,2,1,0:T(8,128)S(1)}, f32[5,12,8,128]{3,2,1,0:T(8,128)S(1)}, f32[5,12,8,128]{3,2,1,0:T(8,128)S(1)}, f32[5,16,8,128]{3,2,1,0:T(8,128)S(1)}, f32[5,48,8,128]{3,2,1,0:T(8,128)S(1)}) custom-call(s32[6]{0:T(128)} %phase_slot.3, f32[2,5,8,8,128]{4,3,2,1,0:T(8,128)} %pert.3, f32[2,5,8,8,128]{4,3,2,1,0:T(8,128)} %force.3, ...), custom_call_target="tpu_custom_call" | custom-call | tf_op jit(solution)/shard_map/pack/pallas_call | solution.py:297
  13.5 6.5 %collective-permute-done.2.refs_1_.refs_4_ = f32[5,22,8,128]{3,2,1,0:T(8,128)S(1)} collective-permute-done((f32[5,22,8,128]{3,2,1,0:T(8,128)S(1)}, f32[5,22,8,128]{3,2,1,0:T(8,128)S(1)}, u32[]{:S(2)}, u32[]{:S(2)}) %collective-permute-start.2) | collective-permute-done | bytes 450592 | tf_op jit(solution)/shard_map/ppermute | solution.py:306
  20.0 2.2 %collective-permute-start.4 = (f32[5,16,8,128]{3,2,1,0:T(8,128)S(1)}, f32[5,16,8,128]{3,2,1,0:T(8,128)S(1)}, u32[]{:S(2)}, u32[]{:S(2)}) collective-permute-start(f32[5,16,8,128]{3,2,1,0:T(8,128)S(1)} %get-tuple-element.50), channel_id=1, source_target_pairs={{0,2},{2,0},{4,6},{6,4},{8,10},{10,8},{12,14},{14,12},{1,3},{3,1},... | collective-permute-start | bytes 983048 | tf_op jit(solution)/shard_map/ppermute | solution.py:306
  22.2 0.7 waves.1
  22.9 7.8 %collective-permute-done.3.refs_2_.refs_5_ = f32[5,22,8,128]{3,2,1,0:T(8,128)S(1)} collective-permute-done((f32[5,22,8,128]{3,2,1,0:T(8,128)S(1)}, f32[5,22,8,128]{3,2,1,0:T(8,128)S(1)}, u32[]{:S(2)}, u32[]{:S(2)}) %collective-permute-start.3) | collective-permute-done | bytes 450592 | tf_op jit(solution)/shard_map/ppermute | solution.py:306
  30.7 2.4 %collective-permute-done.1.refs_0_.refs_3_ = f32[5,24,8,128]{3,2,1,0:T(8,128)S(1)} collective-permute-done((f32[5,24,8,128]{3,2,1,0:T(8,128)S(1)}, f32[5,24,8,128]{3,2,1,0:T(8,128)S(1)}, u32[]{:S(2)}, u32[]{:S(2)}) %collective-permute-start.1) | collective-permute-done | bytes 491552 | tf_op jit(solution)/shard_map/ppermute | solution.py:306
  33.2 3.2 %collective-permute-start.6 = (f32[5,12,8,128]{3,2,1,0:T(8,128)S(1)}, f32[5,12,8,128]{3,2,1,0:T(8,128)S(1)}, u32[]{:S(2)}, u32[]{:S(2)}) collective-permute-start(f32[5,12,8,128]{3,2,1,0:T(8,128)S(1)} %get-tuple-element.52), channel_id=1, source_target_pairs={{0,14},{2,4},{4,2},{6,8},{8,6},{10,12},{12,10},{14,0},{1,15},{3,5}... | collective-permute-start | bytes 737288 | tf_op jit(solution)/shard_map/ppermute | solution.py:306
  36.4 0.1 collective-permute-start.7
  36.6 0.6 collective-permute-start.9
  37.1 1.0 %collective-permute-done.9.refs_5_ = f32[5,6,8,128]{3,2,1,0:T(8,128)S(1)} collective-permute-done((f32[5,6,8,128]{3,2,1,0:T(8,128)S(1)}, f32[5,6,8,128]{3,2,1,0:T(8,128)S(1)}, u32[]{:S(2)}, u32[]{:S(2)}) %collective-permute-start.9) | collective-permute-done | bytes 122912 | tf_op jit(solution)/shard_map/ppermute | solution.py:312
  38.1 0.8 terms.2
  38.9 4.7 %advance.3 = (f32[5,32,8,128]{3,2,1,0:T(8,128)S(1)}, f32[5,16,8,128]{3,2,1,0:T(8,128)S(1)}, f32[5,8,8,128]{3,2,1,0:T(8,128)S(1)}, f32[5,8,8,128]{3,2,1,0:T(8,128)S(1)}) custom-call(f32[18,8,128]{2,1,0:T(8,128)S(1)} %waves.1, f32[26,32,8,128]{3,2,1,0:T(8,128)S(1)} %get-tuple-element.56.refs_0_, f32[26,32,8,128]{3,2,1,0:T(8,128)S(1)} %get-tuple-element.57.refs_1_, ...), custom_call_target="tpu_custom_call" | custom-call | tf_op jit(solution)/shard_map/advance/pallas_call | solution.py:334
  43.6 4.4 %collective-permute-done.6.refs_2_ = f32[5,12,8,128]{3,2,1,0:T(8,128)S(1)} collective-permute-done((f32[5,12,8,128]{3,2,1,0:T(8,128)S(1)}, f32[5,12,8,128]{3,2,1,0:T(8,128)S(1)}, u32[]{:S(2)}, u32[]{:S(2)}) %collective-permute-start.6) | collective-permute-done | bytes 245792 | tf_op jit(solution)/shard_map/ppermute | solution.py:306
  48.0 0.5 collective-permute-start.11
  48.5 3.8 %collective-permute-start.14 = (f32[5,8,8,128]{3,2,1,0:T(8,128)S(1)}, f32[5,8,8,128]{3,2,1,0:T(8,128)S(1)}, u32[]{:S(2)}, u32[]{:S(2)}) collective-permute-start(f32[5,8,8,128]{3,2,1,0:T(8,128)S(1)} %get-tuple-element.69), channel_id=1, source_target_pairs={{0,12},{2,14},{4,0},{6,2},{8,4},{10,6},{12,8},{14,10},{1,13},{3,15... | collective-permute-start | bytes 491528 | tf_op jit(solution)/shard_map/ppermute | solution.py:354
  52.3 1.6 %terms.3 = (f32[26,32,8,128]{3,2,1,0:T(8,128)S(1)}, f32[26,32,8,128]{3,2,1,0:T(8,128)S(1)}, f32[26,32,8,128]{3,2,1,0:T(8,128)S(1)}, f32[26,32,8,128]{3,2,1,0:T(8,128)S(1)}) custom-call(f32[5,48,8,128]{3,2,1,0:T(8,128)S(1)} %get-tuple-element.46.held_base, f32[5,16,8,128]{3,2,1,0:T(8,128)S(1)} %collective-permute-done.4.refs_0_, ...), custom_call_target="tpu_custom_call" | custom-call | tf_op jit(solution)/shard_map/terms/pallas_call | solution.py:315
  53.9 3.4 %collective-permute-done.13.refs_4_ = f32[5,8,8,128]{3,2,1,0:T(8,128)S(1)} collective-permute-done((f32[5,8,8,128]{3,2,1,0:T(8,128)S(1)}, f32[5,8,8,128]{3,2,1,0:T(8,128)S(1)}, u32[]{:S(2)}, u32[]{:S(2)}) %collective-permute-start.13) | collective-permute-done | bytes 163872 | tf_op jit(solution)/shard_map/ppermute | solution.py:353
  57.3 1.3 %collective-permute-done.14.refs_5_ = f32[5,8,8,128]{3,2,1,0:T(8,128)S(1)} collective-permute-done((f32[5,8,8,128]{3,2,1,0:T(8,128)S(1)}, f32[5,8,8,128]{3,2,1,0:T(8,128)S(1)}, u32[]{:S(2)}, u32[]{:S(2)}) %collective-permute-start.14) | collective-permute-done | bytes 163872 | tf_op jit(solution)/shard_map/ppermute | solution.py:354
  58.6 4.7 %advance.4 = (f32[5,16,8,128]{3,2,1,0:T(8,128)S(1)}, f32[5,8,8,128]{3,2,1,0:T(8,128)S(1)}, f32[5,8,8,128]{3,2,1,0:T(8,128)S(1)}) custom-call(f32[18,8,128]{2,1,0:T(8,128)S(1)} %waves.1, f32[26,32,8,128]{3,2,1,0:T(8,128)S(1)} %get-tuple-element.66.refs_0_, f32[26,32,8,128]{3,2,1,0:T(8,128)S(1)} %get-tuple-element.67.refs_1_, ...), custom_call_target="tpu_custom_call" | custom-call | tf_op jit(solution)/shard_map/advance/pallas_call | solution.py:334
  63.3 0.6 collective-permute-start.15
  63.9 3.3 %collective-permute-start.16 = (f32[5,8,8,128]{3,2,1,0:T(8,128)S(1)}, f32[5,8,8,128]{3,2,1,0:T(8,128)S(1)}, u32[]{:S(2)}, u32[]{:S(2)}) collective-permute-start(f32[5,8,8,128]{3,2,1,0:T(8,128)S(1)} %get-tuple-element.72), channel_id=1, source_target_pairs={{0,12},{2,14},{4,0},{6,2},{8,4},{10,6},{12,8},{14,10},{1,13},{3,15... | collective-permute-start | bytes 491528 | tf_op jit(solution)/shard_map/ppermute | solution.py:354
  67.2 5.1 %collective-permute-done.15.refs_4_ = f32[5,8,8,128]{3,2,1,0:T(8,128)S(1)} collective-permute-done((f32[5,8,8,128]{3,2,1,0:T(8,128)S(1)}, f32[5,8,8,128]{3,2,1,0:T(8,128)S(1)}, u32[]{:S(2)}, u32[]{:S(2)}) %collective-permute-start.15) | collective-permute-done | bytes 163872 | tf_op jit(solution)/shard_map/ppermute | solution.py:353
  72.3 1.3 %collective-permute-done.16.refs_5_ = f32[5,8,8,128]{3,2,1,0:T(8,128)S(1)} collective-permute-done((f32[5,8,8,128]{3,2,1,0:T(8,128)S(1)}, f32[5,8,8,128]{3,2,1,0:T(8,128)S(1)}, u32[]{:S(2)}, u32[]{:S(2)}) %collective-permute-start.16) | collective-permute-done | bytes 163872 | tf_op jit(solution)/shard_map/ppermute | solution.py:354
  73.6 4.3 %advance.5 = (f32[5,8,8,128]{3,2,1,0:T(8,128)S(1)}, f32[5,8,8,128]{3,2,1,0:T(8,128)S(1)}) custom-call(f32[18,8,128]{2,1,0:T(8,128)S(1)} %waves.1, f32[26,32,8,128]{3,2,1,0:T(8,128)S(1)} %get-tuple-element.63.refs_0_, f32[26,32,8,128]{3,2,1,0:T(8,128)S(1)} %get-tuple-element.64.refs_1_, f32[5,32,8,128]{3,2,1,0:T(8,128)S(1)} %get-tuple-element.65.refs_2_, ...), custom_call_target="tpu_custom_call" | custom-call | tf_op jit(solution)/shard_map/advance/pallas_call | solution.py:334
  77.9 0.3 collective-permute-start.17
  78.3 5.1 %collective-permute-done.17 = f32[5,8,8,128]{3,2,1,0:T(8,128)S(1)} collective-permute-done((f32[5,8,8,128]{3,2,1,0:T(8,128)S(1)}, f32[5,8,8,128]{3,2,1,0:T(8,128)S(1)}, u32[]{:S(2)}, u32[]{:S(2)}) %collective-permute-start.17) | collective-permute-done | bytes 163872 | tf_op jit(solution)/shard_map/ppermute | solution.py:362
  83.3 0.7 pad_maximum_fusion
  (17 shorter events, 0.2 us)
Async XLA Ops:
  0.0 2.2 %collective-permute-start = (f32[3,5,8,8,128]{4,3,2,1,0:T(8,128)}, f32[3,5,8,8,128]{4,3,2,1,0:T(8,128)S(1)}, u32[]{:S(2)}, u32[]{:S(2)}) collective-permute-start(f32[3,5,8,8,128]{4,3,2,1,0:T(8,128)} %base.3), channel_id=1, source_target_pairs={{0,1},{1,0},{2,3},{3,2},{4,5},{5,4},{6,7},{7,6},{8,9},{9,8},{10,11... | collective-permute-start | bytes 1474568 | tf_op jit(solution)/shard_map/ppermute | solution.py:285
  4.3 15.7 %collective-permute-start.2 = (f32[5,22,8,128]{3,2,1,0:T(8,128)S(1)}, f32[5,22,8,128]{3,2,1,0:T(8,128)S(1)}, u32[]{:S(2)}, u32[]{:S(2)}) collective-permute-start(f32[5,22,8,128]{3,2,1,0:T(8,128)S(1)} %get-tuple-element.41), channel_id=1, source_target_pairs={{0,12},{2,6},{4,0},{6,10},{8,4},{10,14},{12,8},{14,2},{1,13},{3,7}... | collective-permute-start | bytes 1351688 | tf_op jit(solution)/shard_map/ppermute | solution.py:306
  9.3 23.8 %collective-permute-start.1 = (f32[5,24,8,128]{3,2,1,0:T(8,128)S(1)}, f32[5,24,8,128]{3,2,1,0:T(8,128)S(1)}, u32[]{:S(2)}, u32[]{:S(2)}) collective-permute-start(f32[5,24,8,128]{3,2,1,0:T(8,128)S(1)} %get-tuple-element.40), channel_id=1, source_target_pairs={{0,2},{2,0},{4,6},{6,4},{8,10},{10,8},{12,14},{14,12},{1,3},{3,1},... | collective-permute-start | bytes 1474568 | tf_op jit(solution)/shard_map/ppermute | solution.py:306
  9.3 21.4 %collective-permute-start.3 = (f32[5,22,8,128]{3,2,1,0:T(8,128)S(1)}, f32[5,22,8,128]{3,2,1,0:T(8,128)S(1)}, u32[]{:S(2)}, u32[]{:S(2)}) collective-permute-start(f32[5,22,8,128]{3,2,1,0:T(8,128)S(1)} %get-tuple-element.42), channel_id=1, source_target_pairs={{0,14},{2,4},{4,2},{6,8},{8,6},{10,12},{12,10},{14,0},{1,15},{3,5}... | collective-permute-start | bytes 1351688 | tf_op jit(solution)/shard_map/ppermute | solution.py:306
  20.0 28.0 %collective-permute-start.4 = (f32[5,16,8,128]{3,2,1,0:T(8,128)S(1)}, f32[5,16,8,128]{3,2,1,0:T(8,128)S(1)}, u32[]{:S(2)}, u32[]{:S(2)}) collective-permute-start(f32[5,16,8,128]{3,2,1,0:T(8,128)S(1)} %get-tuple-element.50), channel_id=1, source_target_pairs={{0,2},{2,0},{4,6},{6,4},{8,10},{10,8},{12,14},{14,12},{1,3},{3,1},... | collective-permute-start | bytes 983048 | tf_op jit(solution)/shard_map/ppermute | solution.py:306
  33.1 3.5 %collective-permute-start.8 = (f32[5,6,8,128]{3,2,1,0:T(8,128)S(1)}, f32[5,6,8,128]{3,2,1,0:T(8,128)S(1)}, u32[]{:S(2)}, u32[]{:S(2)}) collective-permute-start(f32[5,6,8,128]{3,2,1,0:T(8,128)S(1)} %slice.10), channel_id=1, source_target_pairs={{0,1},{1,0},{2,3},{3,2},{4,5},{5,4},{6,7},{7,6},{8,9},{9,8},{10,11... | collective-permute-start | bytes 368648 | tf_op jit(solution)/shard_map/ppermute | solution.py:312
  33.2 10.4 %collective-permute-start.5 = (f32[5,12,8,128]{3,2,1,0:T(8,128)S(1)}, f32[5,12,8,128]{3,2,1,0:T(8,128)S(1)}, u32[]{:S(2)}, u32[]{:S(2)}) collective-permute-start(f32[5,12,8,128]{3,2,1,0:T(8,128)S(1)} %get-tuple-element.51), channel_id=1, source_target_pairs={{0,12},{2,6},{4,0},{6,10},{8,4},{10,14},{12,8},{14,2},{1,13},{3,7}... | collective-permute-start | bytes 737288 | tf_op jit(solution)/shard_map/ppermute | solution.py:306
  33.2 14.8 %collective-permute-start.6 = (f32[5,12,8,128]{3,2,1,0:T(8,128)S(1)}, f32[5,12,8,128]{3,2,1,0:T(8,128)S(1)}, u32[]{:S(2)}, u32[]{:S(2)}) collective-permute-start(f32[5,12,8,128]{3,2,1,0:T(8,128)S(1)} %get-tuple-element.52), channel_id=1, source_target_pairs={{0,14},{2,4},{4,2},{6,8},{8,6},{10,12},{12,10},{14,0},{1,15},{3,5}... | collective-permute-start | bytes 737288 | tf_op jit(solution)/shard_map/ppermute | solution.py:306
  36.4 1.6 %collective-permute-start.7 = (f32[5,8,8,128]{3,2,1,0:T(8,128)S(1)}, f32[5,8,8,128]{3,2,1,0:T(8,128)S(1)}, u32[]{:S(2)}, u32[]{:S(2)}) collective-permute-start(f32[5,8,8,128]{3,2,1,0:T(8,128)S(1)} %slice.9), channel_id=1, source_target_pairs={{0,1},{1,0},{2,3},{3,2},{4,5},{5,4},{6,7},{7,6},{8,9},{9,8},{10,11... | collective-permute-start | bytes 491528 | tf_op jit(solution)/shard_map/ppermute | solution.py:312
  36.6 1.5 %collective-permute-start.9 = (f32[5,6,8,128]{3,2,1,0:T(8,128)S(1)}, f32[5,6,8,128]{3,2,1,0:T(8,128)S(1)}, u32[]{:S(2)}, u32[]{:S(2)}) collective-permute-start(f32[5,6,8,128]{3,2,1,0:T(8,128)S(1)} %slice.11), channel_id=1, source_target_pairs={{0,1},{1,0},{2,3},{3,2},{4,5},{5,4},{6,7},{7,6},{8,9},{9,8},{10,11... | collective-permute-start | bytes 368648 | tf_op jit(solution)/shard_map/ppermute | solution.py:312
  48.0 4.3 %collective-permute-start.10 = (f32[5,16,8,128]{3,2,1,0:T(8,128)S(1)}, f32[5,16,8,128]{3,2,1,0:T(8,128)S(1)}, u32[]{:S(2)}, u32[]{:S(2)}) collective-permute-start(f32[5,16,8,128]{3,2,1,0:T(8,128)S(1)} %collective-permute-done.4.refs_0_), channel_id=1, source_target_pairs={{0,1},{1,0},{2,3},{3,2},{4,5},{5,4},{6,7},{7,6},{8,9},{9,8},{10,11... | collective-permute-start | bytes 983048 | tf_op jit(solution)/shard_map/ppermute | solution.py:312
  48.0 4.3 %collective-permute-start.11 = (f32[5,12,8,128]{3,2,1,0:T(8,128)S(1)}, f32[5,12,8,128]{3,2,1,0:T(8,128)S(1)}, u32[]{:S(2)}, u32[]{:S(2)}) collective-permute-start(f32[5,12,8,128]{3,2,1,0:T(8,128)S(1)} %collective-permute-done.5.refs_1_), channel_id=1, source_target_pairs={{0,1},{1,0},{2,3},{3,2},{4,5},{5,4},{6,7},{7,6},{8,9},{9,8},{10,11... | collective-permute-start | bytes 737288 | tf_op jit(solution)/shard_map/ppermute | solution.py:312
  48.5 3.8 %collective-permute-start.12 = (f32[5,12,8,128]{3,2,1,0:T(8,128)S(1)}, f32[5,12,8,128]{3,2,1,0:T(8,128)S(1)}, u32[]{:S(2)}, u32[]{:S(2)}) collective-permute-start(f32[5,12,8,128]{3,2,1,0:T(8,128)S(1)} %collective-permute-done.6.refs_2_), channel_id=1, source_target_pairs={{0,1},{1,0},{2,3},{3,2},{4,5},{5,4},{6,7},{7,6},{8,9},{9,8},{10,11... | collective-permute-start | bytes 737288 | tf_op jit(solution)/shard_map/ppermute | solution.py:312
  48.5 8.8 %collective-permute-start.13 = (f32[5,8,8,128]{3,2,1,0:T(8,128)S(1)}, f32[5,8,8,128]{3,2,1,0:T(8,128)S(1)}, u32[]{:S(2)}, u32[]{:S(2)}) collective-permute-start(f32[5,8,8,128]{3,2,1,0:T(8,128)S(1)} %get-tuple-element.68), channel_id=1, source_target_pairs={{0,4},{2,6},{4,8},{6,10},{8,12},{10,14},{12,0},{14,2},{1,5},{3,7},... | collective-permute-start | bytes 491528 | tf_op jit(solution)/shard_map/ppermute | solution.py:353
  48.5 10.1 %collective-permute-start.14 = (f32[5,8,8,128]{3,2,1,0:T(8,128)S(1)}, f32[5,8,8,128]{3,2,1,0:T(8,128)S(1)}, u32[]{:S(2)}, u32[]{:S(2)}) collective-permute-start(f32[5,8,8,128]{3,2,1,0:T(8,128)S(1)} %get-tuple-element.69), channel_id=1, source_target_pairs={{0,12},{2,14},{4,0},{6,2},{8,4},{10,6},{12,8},{14,10},{1,13},{3,15... | collective-permute-start | bytes 491528 | tf_op jit(solution)/shard_map/ppermute | solution.py:354
  63.3 9.0 %collective-permute-start.15 = (f32[5,8,8,128]{3,2,1,0:T(8,128)S(1)}, f32[5,8,8,128]{3,2,1,0:T(8,128)S(1)}, u32[]{:S(2)}, u32[]{:S(2)}) collective-permute-start(f32[5,8,8,128]{3,2,1,0:T(8,128)S(1)} %get-tuple-element.71), channel_id=1, source_target_pairs={{0,4},{2,6},{4,8},{6,10},{8,12},{10,14},{12,0},{14,2},{1,5},{3,7},... | collective-permute-start | bytes 491528 | tf_op jit(solution)/shard_map/ppermute | solution.py:353
  63.9 9.7 %collective-permute-start.16 = (f32[5,8,8,128]{3,2,1,0:T(8,128)S(1)}, f32[5,8,8,128]{3,2,1,0:T(8,128)S(1)}, u32[]{:S(2)}, u32[]{:S(2)}) collective-permute-start(f32[5,8,8,128]{3,2,1,0:T(8,128)S(1)} %get-tuple-element.72), channel_id=1, source_target_pairs={{0,12},{2,14},{4,0},{6,2},{8,4},{10,6},{12,8},{14,10},{1,13},{3,15... | collective-permute-start | bytes 491528 | tf_op jit(solution)/shard_map/ppermute | solution.py:354
  77.9 5.4 %collective-permute-start.17 = (f32[5,8,8,128]{3,2,1,0:T(8,128)S(1)}, f32[5,8,8,128]{3,2,1,0:T(8,128)S(1)}, u32[]{:S(2)}, u32[]{:S(2)}) collective-permute-start(f32[5,8,8,128]{3,2,1,0:T(8,128)S(1)} %get-tuple-element.74), channel_id=1, source_target_pairs={{0,2},{2,0},{4,6},{6,4},{8,10},{10,8},{12,14},{14,12},{1,3},{3,1},... | collective-permute-start | bytes 491528 | tf_op jit(solution)/shard_map/ppermute | solution.py:362

commit v3 on v2

--- a/solution.py
+++ b/solution.py
@@ -45,7 +45,8 @@
 
 
 def pack_kernel(sets, widths, reach, which, phase_slot, pert, force, base, base_peer, *refs):
-    sends, kept, sem = refs[: 3 * len(which)], refs[3 * len(which) : -1], refs[-1]
+    count = sum(3 if chosen == 0 else 2 for chosen in which)
+    sends, kept, sem = refs[:count], refs[count:-1], refs[-1]
     mine = parity()
     core = lax.axis_index("vec")
     other = 1 - mine
@@ -69,25 +70,32 @@
         pl.when(jnp.logical_not(held))(second.start)
         waits.append(first)
 
-    for index, chosen in enumerate(which):
-        swap_out, own_out, other_out = sends[3 * index : 3 * index + 3]
-        at_swap = at_edge = 0
+    for chosen in which:
+        if chosen == 0:
+            swap_out, own_out, other_out, *sends = sends
+        else:
+            swap_out, other_out, *sends = sends
+        at_swap = at_other = at_own = 0
         if chosen == 0:
             for array, width in ((pert, widths[0]), (force, reach)):
                 edge = pl.ds(mine * (tile - width), width)
                 copy(lambda: array.at[other], swap_out, at_swap, tile)
-                copy(lambda: array.at[mine, :, edge], own_out, at_edge, width)
-                copy(lambda: array.at[other, :, edge], other_out, at_edge, width)
+                copy(lambda: array.at[mine, :, edge], own_out, at_own, width)
+                copy(lambda: array.at[other, :, edge], other_out, at_other, width)
                 at_swap += tile
-                at_edge += width
+                at_own += width
+                at_other += width
+        half = tile // 2
+        layers = lambda step: pl.ds(mine * (tile - widths[step]) + core * (widths[step] // 2), widths[step] // 2)
         for step in sets[chosen]:
-            half, width = tile // 2, widths[step]
             copy_base(step, pl.ds(core * half, half), swap_out, at_swap, half)
-            edge = pl.ds(mine * (tile - width) + core * (width // 2), width // 2)
-            for target in (own_out, other_out):
-                copy_base(step, edge, target, at_edge, width // 2)
+            copy_base(step, layers(step), other_out, at_other, widths[step] // 2)
             at_swap += half
-            at_edge += width // 2
+            at_other += widths[step] // 2
+        if chosen == 0:
+            for step in sum(sets, []):
+                copy_base(step, layers(step), own_out, at_own, widths[step] // 2)
+                at_own += widths[step] // 2
     if kept:
         held_state, held_base = kept
         copy(lambda: pert.at[mine], held_state, 0, tile)
@@ -147,14 +155,14 @@
         terms[index, pl.ds(at, count)] = value
 
 
-def terms_kernel(steps, widths, at_held, at_swap, at_edge, reach, held_base, *refs):
+def terms_kernel(steps, widths, at_held, starts, reach, held_base, *refs):
     mine_in, peer_in, outs, held = refs[:3], refs[3:6], refs[6:-1], refs[-1]
     mine = parity()
     core = lax.axis_index("vec")
     planes = held.shape[1]
     tile = planes // 2 - reach
     half = tile // 2
-    at_peer_swap = at_peer_edge = 0
+    starts = [list(starts), [0, 0, 0]]
     for step, terms in zip(steps, outs):
         width = widths[step]
         held[:, pl.ds(reach + mine * tile, tile)] = held_base[:, at_held : at_held + tile]
@@ -162,18 +170,16 @@
         near, far = reach - width, reach + 2 * tile
         own_at = near + (1 - mine) * (far - near)
         other_at = near + mine * (far - near)
-        for (swap_in, own_in, other_in), who, swap_lo, edge_lo in (
-            (mine_in, core, at_swap, at_edge),
-            (peer_in, 1 - core, at_peer_swap, at_peer_edge),
-        ):
+        for (swap_in, own_in, other_in), who, start in zip((mine_in, peer_in), (core, 1 - core), starts):
             edge = width // 2
-            held[:, pl.ds(partner + who * half, half)] = swap_in[:, swap_lo : swap_lo + half]
-            held[:, pl.ds(own_at + who * edge, edge)] = own_in[:, edge_lo : edge_lo + edge]
-            held[:, pl.ds(other_at + who * edge, edge)] = other_in[:, edge_lo : edge_lo + edge]
-        base_terms(held, terms, near + 1, planes - 2 * near - 2)
+            at_swap, at_own, at_other = start
+            held[:, pl.ds(partner + who * half, half)] = swap_in[:, at_swap : at_swap + half]
+            held[:, pl.ds(own_at + who * edge, edge)] = own_in[:, at_own : at_own + edge]
+            held[:, pl.ds(other_at + who * edge, edge)] = other_in[:, at_other : at_other + edge]
+            start[:] = [at_swap + half, at_own + edge, at_other + edge]
+        for at, count in singly([(near + 1, planes - 2 * near - 2)]):
+            base_terms(held, terms, at, count)
         at_held += tile
-        at_swap, at_peer_swap = at_swap + half, at_peer_swap + half
-        at_edge, at_peer_edge = at_edge + width // 2, at_peer_edge + width // 2
 
 
 def rates(state, terms, force, wave, at, count):
@@ -204,23 +210,52 @@
     return out
 
 
-def one_step(inset, state, force, terms, waves, second, third, fourth):
-    planes = state.shape[1]
-
+def singly(ranges):
+    return [(at, 1) for first, count in ranges for at in range(first, first + count)]
+
+
+def one_step(cover, depth, state, force, terms, waves, second, third, fourth):
     def stage(number, source, size, wave, target):
-        at, count = inset + number, planes - 2 * (inset + number)
-        here = pl.ds(at, count)
-        for field, rate in enumerate(rates(source, terms, force, wave[None], at, count)):
-            target[field, here] = state[field, here] + size * rate
+        for at, count in singly(cover(depth + number)):
+            here = pl.ds(at, count)
+            for field, rate in enumerate(rates(source, terms, force, wave[None], at, count)):
+                target[field, here] = state[field, here] + size * rate
 
     stage(1, state, 0.5 * TIME_STEP, waves[0], second)
     stage(2, second, 0.5 * TIME_STEP, waves[1], third)
     stage(3, third, TIME_STEP, waves[1], fourth)
-    at, count = inset + STAGES, planes - 2 * (inset + STAGES)
-    here = pl.ds(at, count)
-    for field, rate in enumerate(rates(fourth, terms, force, waves[2][None], at, count)):
-        mixed = second[field, here] + fourth[field, here] + 2.0 * third[field, here] - state[field, here]
-        state[field, here] = mixed * (1.0 / 3.0) + (TIME_STEP / 6.0) * rate
+    for at, count in singly(cover(depth + STAGES)):
+        here = pl.ds(at, count)
+        for field, rate in enumerate(rates(fourth, terms, force, waves[2][None], at, count)):
+            mixed = second[field, here] + fourth[field, here] + 2.0 * third[field, here] - state[field, here]
+            state[field, here] = mixed * (1.0 / 3.0) + (TIME_STEP / 6.0) * rate
+
+
+def several(steps, cover, waves, state, force, terms, *stages):
+    for index, step in enumerate(steps):
+        wave = [waves[3 * step + which] for which in range(3)]
+        one_step(cover, STAGES * index, state, force, terms[index], wave, *stages)
+
+
+def inner(reach, slab, depth):
+    return [(reach + depth, slab - 2 * depth)] if slab > 2 * depth else []
+
+
+def outer(reach, slab, width, depth):
+    low, high = reach - width + depth, reach + slab + width - depth
+    if not inner(reach, slab, depth):
+        return [(low, high - low)]
+    return [(low, width), (high - width, width)]
+
+
+def interior_kernel(steps, reach, waves, *refs):
+    terms, (force, slab, *refs) = refs[: len(steps)], refs[len(steps) :]
+    outs, scratch = refs[:4], refs[4:]
+    planes = slab.shape[1]
+    scratch[0][:, reach : reach + planes] = slab[...]
+    several(steps, functools.partial(inner, reach, planes), waves, scratch[0], force, terms, *scratch[1:])
+    for index, (out, held) in enumerate(zip(outs, scratch)):
+        out[:, index : planes - index] = held[:, reach + index : reach + planes - index]
 
 
 def advance_kernel(steps, widths, reach, first, last, next_width, waves, *refs):
@@ -243,14 +278,16 @@
         force[:, there] = swap_in[:, tile : 2 * tile]
         force[:, pl.ds((1 - mine) * far, reach)] = own_in[:, width : width + reach]
         force[:, pl.ds(mine * far, reach)] = other_in[:, width : width + reach]
+        cover = lambda depth: [(near + depth, planes - 2 * (near + depth))]
     else:
-        force, slab_in, left_in, right_in, *outs = refs
+        force, left_in, right_in, *refs = refs
+        begun, outs = refs[:4], refs[4:]
+        for index, (source, held) in enumerate(zip(begun, (state, second, third, fourth))):
+            held[:, reach + index : far - index] = source[:, index : 2 * tile - index]
         state[:, near:reach] = left_in[...]
-        state[:, reach:far] = slab_in[...]
         state[:, far : far + width] = right_in[...]
-    for index, step in enumerate(steps):
-        wave = [waves[3 * step + which] for which in range(3)]
-        one_step(reach - widths[step], state, force, terms[index], wave, second, third, fourth)
+        cover = functools.partial(outer, reach, 2 * tile, width)
+    several(steps, cover, waves, state, force, terms, second, third, fourth)
     if last:
         keep, give = outs
         keep[...] = state[:, pl.ds(reach + mine * tile, tile)]
@@ -291,8 +328,9 @@
             group, start = sets[chosen], chosen == 0
             swapped = len(group) * (tile // 2) + (2 * tile if start else 0)
             edges = sum(widths[step] // 2 for step in group) + (widths[0] + reach if start else 0)
-            sends += [block(FIELDS, swapped), block(FIELDS, edges), block(FIELDS, edges)]
-            copies += 3 * len(group) + (6 if start else 0)
+            every = sum(widths.values()) // 2 + widths[0] + reach
+            sends += [block(FIELDS, swapped)] + ([block(FIELDS, every)] if start else []) + [block(FIELDS, edges)]
+            copies += 2 * len(group) + (6 + steps if start else 0)
         kept = [block(FIELDS, 2 * tile), block(FIELDS, steps * tile)] if keep else []
         return pallas(
             functools.partial(pack_kernel, sets, widths, reach, which),
@@ -302,18 +340,21 @@
             [pltpu.SemaphoreType.DMA((copies + (2 + steps if keep else 0),))],
         )(*in_place(phase_slot, perturbation, forcing, base_flow), base_peer)
 
-    def exchange(packed):
-        return [lax.ppermute(part, "space", perm) for part, perm in zip(packed, (swap, own, other))]
+    def exchange(packed, perms):
+        return [lax.ppermute(part, "space", perm) for part, perm in zip(packed, perms)]
 
     def factors(which, arrived):
         group = sets[which]
-        at_swap, at_edge = (2 * tile, widths[0] + reach) if which == 0 else (0, 0)
+        edges = sum(widths[step] // 2 for step in group)
+        starts = [2 * tile, widths[0] + reach, widths[0] + reach] if which == 0 else [0, 0, 0]
+        if which > 0:
+            starts[1] = widths[0] + reach + sum(widths[step] // 2 for each in sets[:which] for step in each)
+        sizes = (len(group) * tile // 2, edges, edges)
         crossed = [
-            lax.ppermute(part[:, at:] if at else part, "vec", core)
-            for part, at in zip(arrived, (at_swap, at_edge, at_edge))
+            lax.ppermute(part[:, at : at + size], "vec", core) for part, at, size in zip(arrived, starts, sizes)
         ]
         return pallas(
-            functools.partial(terms_kernel, group, widths, group[0] * tile, at_swap, at_edge, reach),
+            functools.partial(terms_kernel, group, widths, group[0] * tile, starts, reach),
             "terms",
             [block(TERMS, planes)] * len(group),
             [VMEM] * 7,
@@ -340,11 +381,10 @@
             grant=8,
         )(waves, *operands)
 
-    first = exchange(pack([0], False))
+    first = exchange(pack([0], False), (swap, own, other))
     *later, held_state, held_base = pack(range(1, len(sets)), True)
     (waves,) = pallas(functools.partial(waves_kernel, moments), "waves", [block(3 * steps)], [SMEM])(*in_place(frequency))
-    packed = [None] + [later[3 * which : 3 * which + 3] for which in range(len(sets) - 1)]
-    arrived = exchange(after(packed[1], first[1])) if len(sets) > 1 else None
+    arrived = exchange(later, (swap, other))
     first, held_state, held_base, waves = lax.optimization_barrier((first, held_state, held_base, waves))
     terms = dict(zip(sets[0], factors(0, first)))
     force, *outs = advance(0, [*[terms[step] for step in rounds[0]], held_state, *first])
@@ -353,11 +393,18 @@
         left_in = lax.ppermute(right, "space", ahead)
         right_in = lax.ppermute(left, "space", behind)
         if which < len(sets):
-            arrived = after(arrived, slab)
-            following = exchange(after(packed[which + 1], arrived)) if which + 1 < len(sets) else None
-            terms |= zip(sets[which], factors(which, arrived))
-            arrived = following
-        outs = advance(which, [*[terms[step] for step in rounds[which]], force, slab, left_in, right_in])
+            swap_in, other_in = after(arrived, slab)
+            terms |= zip(sets[which], factors(which, [swap_in, first[1], other_in]))
+        factors_here = [terms[step] for step in rounds[which]]
+        begun = pallas(
+            functools.partial(interior_kernel, rounds[which], reach),
+            "interior",
+            [block(FIELDS, 2 * tile)] * 4,
+            [VMEM] * (3 + len(factors_here)),
+            [scratch(FIELDS, planes)] * 4,
+            grant=8,
+        )(waves, *factors_here, force, slab)
+        outs = advance(which, [*factors_here, force, left_in, right_in, *begun])
     keep, give = outs
     given = lax.ppermute(give, "space", swap)
     mine = parity()

time: 84.3 us -> 77.8 us (0.923)
  waiting for transfers between devices: 40 us -> 35.9 us
  starting transfers between devices: 22.1 us -> 20.8 us
  Pallas kernels: 21.1 us -> 20 us
    pallas_call x3, Pallas kernels: 13.6 us -> 10.1 us  [advance(): pallas(functools.partial(advance_kernel, group, widths, reach, first, las...]
    ppermute x6 -> x5, starting transfers between devices: 12.4 us -> 9.89 us  [exchange(): lax.ppermute(part, 'space', perm)]
    ppermute x2, waiting for transfers between devices: 8.56 us -> 6.3 us  [per_device(): left_in = lax.ppermute(right, 'space', ahead)]
    pallas_call x2 -> x4, Pallas kernels: 2.32 us -> 4.58 us  [the longest x2 2.3 us: per_device(): pallas(functools.partial(interior_kernel, rounds[which], reach), 'interio...]
    ppermute x6 -> x5, waiting for transfers between devices: 21 us -> 19.7 us  [exchange(): lax.ppermute(part, 'space', perm)]
    ppermute x1, starting transfers between devices: 0.33 us -> 1.38 us  [per_device(): given = lax.ppermute(give, 'space', swap)]
  transfers between devices with their start and end apart: 18 -> 17, of which waited for: 11 -> 10; matrix products, arithmetic and copies ran while one was open for 0% -> 0% of each run, Pallas kernels for 12% -> 15%
where the time goes in v3:
time: 77.8 us; the launch traced here: 77.6 us
  waiting for transfers between devices  35.9 us (46%)
  starting transfers between devices  20.8 us (27%)
  Pallas kernels  20 us (26%)
    ppermute x5, waiting for transfers between devices, exchange(): lax.ppermute(part, 'space', perm)  19.7 us
    pallas_call x3, Pallas kernels, advance(): pallas(functools.partial(advance_kernel, group, widths, reach, first, las...  10.1 us
    ppermute x5, starting transfers between devices, exchange(): lax.ppermute(part, 'space', perm)  9.89 us
    ppermute x2, starting transfers between devices, per_device(): right_in = lax.ppermute(left, 'space', behind)  6.72 us
    ppermute x2, waiting for transfers between devices, per_device(): left_in = lax.ppermute(right, 'space', ahead)  6.3 us
    pallas_call x2, Pallas kernels, pack(): pallas(functools.partial(pack_kernel, sets, widths, reach, which), 'pack'...  4.53 us
    ppermute x1, waiting for transfers between devices, per_device(): given = lax.ppermute(give, 'space', swap)  4.36 us
    ppermute x2, waiting for transfers between devices, per_device(): right_in = lax.ppermute(left, 'space', behind)  2.48 us
  transfers between devices with their start and end apart: 17, of which 10 were waited for; matrix products, arithmetic and copies ran while one was open for 0% of the time, Pallas kernels for 15%

profile of v3, /device:TPU:0, one launch (start us, length us, event | category | flops | bytes accessed | tf_op | source)
XLA Modules:
  0.0 77.6 jit_solution(10402808981027360367)
XLA Ops:
  0.0 0.5 collective-permute-start
  0.5 1.7 %collective-permute-done.base_peer = f32[3,5,8,8,128]{4,3,2,1,0:T(8,128)S(1)} collective-permute-done((f32[3,5,8,8,128]{4,3,2,1,0:T(8,128)}, f32[3,5,8,8,128]{4,3,2,1,0:T(8,128)S(1)}, u32[]{:S(2)}, u32[]{:S(2)}) %collective-permute-start) | collective-permute-done | bytes 491552 | tf_op jit(solution)/shard_map/ppermute | solution.py:322
  2.2 2.3 %pack.2 = (f32[5,24,8,128]{3,2,1,0:T(8,128)S(1)}, f32[5,34,8,128]{3,2,1,0:T(8,128)S(1)}, f32[5,22,8,128]{3,2,1,0:T(8,128)S(1)}) custom-call(s32[6]{0:T(128)} %phase_slot.3, f32[2,5,8,8,128]{4,3,2,1,0:T(8,128)} %pert.3, f32[2,5,8,8,128]{4,3,2,1,0:T(8,128)} %force.3, f32[3,5,8,8,128]{4,3,2,1,0:T(8,128)} %base.3, ...), custom_call_target="tpu_custom_call" | custom-call | tf_op jit(solution)/shard_map/pack/pallas_call | solution.py:335
  4.4 5.0 %collective-permute-start.2 = (f32[5,34,8,128]{3,2,1,0:T(8,128)S(1)}, f32[5,34,8,128]{3,2,1,0:T(8,128)S(1)}, u32[]{:S(2)}, u32[]{:S(2)}) collective-permute-start(f32[5,34,8,128]{3,2,1,0:T(8,128)S(1)} %get-tuple-element.44), channel_id=1, source_target_pairs={{0,12},{2,6},{4,0},{6,10},{8,4},{10,14},{12,8},{14,2},{1,13},{3,7}... | collective-permute-start | bytes 2088968 | tf_op jit(solution)/shard_map/ppermute | solution.py:344
  9.5 1.9 %collective-permute-start.3 = (f32[5,22,8,128]{3,2,1,0:T(8,128)S(1)}, f32[5,22,8,128]{3,2,1,0:T(8,128)S(1)}, u32[]{:S(2)}, u32[]{:S(2)}) collective-permute-start(f32[5,22,8,128]{3,2,1,0:T(8,128)S(1)} %get-tuple-element.45), channel_id=1, source_target_pairs={{0,14},{2,4},{4,2},{6,8},{8,6},{10,12},{12,10},{14,0},{1,15},{3,5}... | collective-permute-start | bytes 1351688 | tf_op jit(solution)/shard_map/ppermute | solution.py:344
  11.4 2.3 %pack.3 = (f32[5,16,8,128]{3,2,1,0:T(8,128)S(1)}, f32[5,12,8,128]{3,2,1,0:T(8,128)S(1)}, f32[5,16,8,128]{3,2,1,0:T(8,128)S(1)}, f32[5,48,8,128]{3,2,1,0:T(8,128)S(1)}) custom-call(s32[6]{0:T(128)} %phase_slot.3, f32[2,5,8,8,128]{4,3,2,1,0:T(8,128)} %pert.3, f32[2,5,8,8,128]{4,3,2,1,0:T(8,128)} %force.3, f32[3,5,8,8,128]{4,3,2,1,0:T(8,128)} %base.3, ...), custom_call_target="tpu_custom_call" | custom-call | tf_op jit(solution)/shard_map/pack/pallas_call | solution.py:335
  13.6 0.7 collective-permute-start.4
  14.3 2.3 %collective-permute-start.5 = (f32[5,12,8,128]{3,2,1,0:T(8,128)S(1)}, f32[5,12,8,128]{3,2,1,0:T(8,128)S(1)}, u32[]{:S(2)}, u32[]{:S(2)}) collective-permute-start(f32[5,12,8,128]{3,2,1,0:T(8,128)S(1)} %get-tuple-element.51), channel_id=1, source_target_pairs={{0,14},{2,4},{4,2},{6,8},{8,6},{10,12},{12,10},{14,0},{1,15},{3,5}... | collective-permute-start | bytes 737288 | tf_op jit(solution)/shard_map/ppermute | solution.py:344
  16.6 0.7 waves.1
  17.3 19.5 %collective-permute-done.3.refs_2_.refs_5_ = f32[5,22,8,128]{3,2,1,0:T(8,128)S(1)} collective-permute-done((f32[5,22,8,128]{3,2,1,0:T(8,128)S(1)}, f32[5,22,8,128]{3,2,1,0:T(8,128)S(1)}, u32[]{:S(2)}, u32[]{:S(2)}) %collective-permute-start.3) | collective-permute-done | bytes 450592 | tf_op jit(solution)/shard_map/ppermute | solution.py:344
  36.9 0.6 collective-permute-start.7
  37.6 0.9 %collective-permute-done.7.refs_4_ = f32[5,6,8,128]{3,2,1,0:T(8,128)S(1)} collective-permute-done((f32[5,6,8,128]{3,2,1,0:T(8,128)S(1)}, f32[5,6,8,128]{3,2,1,0:T(8,128)S(1)}, u32[]{:S(2)}, u32[]{:S(2)}) %collective-permute-start.7) | collective-permute-done | bytes 122912 | tf_op jit(solution)/shard_map/ppermute | solution.py:354
  38.5 0.4 collective-permute-done.8.refs_5_
  38.9 0.8 terms.2
  39.7 4.4 %advance.3 = (f32[5,32,8,128]{3,2,1,0:T(8,128)S(1)}, f32[5,16,8,128]{3,2,1,0:T(8,128)S(1)}, f32[5,8,8,128]{3,2,1,0:T(8,128)S(1)}, f32[5,8,8,128]{3,2,1,0:T(8,128)S(1)}) custom-call(f32[18,8,128]{2,1,0:T(8,128)S(1)} %waves.1, f32[26,32,8,128]{3,2,1,0:T(8,128)S(1)} %get-tuple-element.55.refs_0_, f32[26,32,8,128]{3,2,1,0:T(8,128)S(1)} %get-tuple-element.56.refs_1_, ...), custom_call_target="tpu_custom_call" | custom-call | tf_op jit(solution)/shard_map/advance/pallas_call | solution.py:375
  44.1 0.2 collective-permute-done.4.refs_0_
  44.3 0.6 collective-permute-start.10
  45.0 3.8 %collective-permute-start.13 = (f32[5,8,8,128]{3,2,1,0:T(8,128)S(1)}, f32[5,8,8,128]{3,2,1,0:T(8,128)S(1)}, u32[]{:S(2)}, u32[]{:S(2)}) collective-permute-start(f32[5,8,8,128]{3,2,1,0:T(8,128)S(1)} %get-tuple-element.67), channel_id=1, source_target_pairs={{0,12},{2,14},{4,0},{6,2},{8,4},{10,6},{12,8},{14,10},{1,13},{3,15... | collective-permute-start | bytes 491528 | tf_op jit(solution)/shard_map/ppermute | solution.py:394
  48.8 1.5 %terms.3 = (f32[26,32,8,128]{3,2,1,0:T(8,128)S(1)}, f32[26,32,8,128]{3,2,1,0:T(8,128)S(1)}, f32[26,32,8,128]{3,2,1,0:T(8,128)S(1)}, f32[26,32,8,128]{3,2,1,0:T(8,128)S(1)}) custom-call(f32[5,48,8,128]{3,2,1,0:T(8,128)S(1)} %get-tuple-element.49.held_base, f32[5,16,8,128]{3,2,1,0:T(8,128)S(1)} %collective-permute-done.4.refs_0_, ...), custom_call_target="tpu_custom_call" | custom-call | tf_op jit(solution)/shard_map/terms/pallas_call | solution.py:356
  50.4 1.2 %interior.2 = (f32[5,16,8,128]{3,2,1,0:T(8,128)S(1)}, f32[5,16,8,128]{3,2,1,0:T(8,128)S(1)}, f32[5,16,8,128]{3,2,1,0:T(8,128)S(1)}, f32[5,16,8,128]{3,2,1,0:T(8,128)S(1)}) custom-call(f32[18,8,128]{2,1,0:T(8,128)S(1)} %waves.1, f32[26,32,8,128]{3,2,1,0:T(8,128)S(1)} %get-tuple-element.64.refs_0_, f32[26,32,8,128]{3,2,1,0:T(8,128)S(1)} %get-tuple-element.65.refs_1_, ...), custom_call_target="tpu_custom_call" | custom-call | tf_op jit(solution)/shard_map/interior/pallas_call | solution.py:399
  51.5 2.3 %collective-permute-done.12.refs_3_ = f32[5,8,8,128]{3,2,1,0:T(8,128)S(1)} collective-permute-done((f32[5,8,8,128]{3,2,1,0:T(8,128)S(1)}, f32[5,8,8,128]{3,2,1,0:T(8,128)S(1)}, u32[]{:S(2)}, u32[]{:S(2)}) %collective-permute-start.12) | collective-permute-done | bytes 163872 | tf_op jit(solution)/shard_map/ppermute | solution.py:393
  53.8 1.2 %collective-permute-done.13.refs_4_ = f32[5,8,8,128]{3,2,1,0:T(8,128)S(1)} collective-permute-done((f32[5,8,8,128]{3,2,1,0:T(8,128)S(1)}, f32[5,8,8,128]{3,2,1,0:T(8,128)S(1)}, u32[]{:S(2)}, u32[]{:S(2)}) %collective-permute-start.13) | collective-permute-done | bytes 163872 | tf_op jit(solution)/shard_map/ppermute | solution.py:394
  55.1 2.8 %advance.4 = (f32[5,16,8,128]{3,2,1,0:T(8,128)S(1)}, f32[5,8,8,128]{3,2,1,0:T(8,128)S(1)}, f32[5,8,8,128]{3,2,1,0:T(8,128)S(1)}) custom-call(f32[18,8,128]{2,1,0:T(8,128)S(1)} %waves.1, f32[26,32,8,128]{3,2,1,0:T(8,128)S(1)} %get-tuple-element.64.refs_0_, f32[26,32,8,128]{3,2,1,0:T(8,128)S(1)} %get-tuple-element.65.refs_1_, ...), custom_call_target="tpu_custom_call" | custom-call | tf_op jit(solution)/shard_map/advance/pallas_call | solution.py:375
  57.9 1.0 %collective-permute-start.14 = (f32[5,8,8,128]{3,2,1,0:T(8,128)S(1)}, f32[5,8,8,128]{3,2,1,0:T(8,128)S(1)}, u32[]{:S(2)}, u32[]{:S(2)}) collective-permute-start(f32[5,8,8,128]{3,2,1,0:T(8,128)S(1)} %get-tuple-element.72), channel_id=1, source_target_pairs={{0,4},{2,6},{4,8},{6,10},{8,12},{10,14},{12,0},{14,2},{1,5},{3,7},... | collective-permute-start | bytes 491528 | tf_op jit(solution)/shard_map/ppermute | solution.py:393
  58.8 2.9 %collective-permute-start.15 = (f32[5,8,8,128]{3,2,1,0:T(8,128)S(1)}, f32[5,8,8,128]{3,2,1,0:T(8,128)S(1)}, u32[]{:S(2)}, u32[]{:S(2)}) collective-permute-start(f32[5,8,8,128]{3,2,1,0:T(8,128)S(1)} %get-tuple-element.73), channel_id=1, source_target_pairs={{0,12},{2,14},{4,0},{6,2},{8,4},{10,6},{12,8},{14,10},{1,13},{3,15... | collective-permute-start | bytes 491528 | tf_op jit(solution)/shard_map/ppermute | solution.py:394
  61.7 1.1 %interior.3 = (f32[5,16,8,128]{3,2,1,0:T(8,128)S(1)}, f32[5,16,8,128]{3,2,1,0:T(8,128)S(1)}, f32[5,16,8,128]{3,2,1,0:T(8,128)S(1)}, f32[5,16,8,128]{3,2,1,0:T(8,128)S(1)}) custom-call(f32[18,8,128]{2,1,0:T(8,128)S(1)} %waves.1, f32[26,32,8,128]{3,2,1,0:T(8,128)S(1)} %get-tuple-element.61.refs_0_, f32[26,32,8,128]{3,2,1,0:T(8,128)S(1)} %get-tuple-element.62.refs_1_, ...), custom_call_target="tpu_custom_call" | custom-call | tf_op jit(solution)/shard_map/interior/pallas_call | solution.py:399
  62.9 4.0 %collective-permute-done.14.refs_3_ = f32[5,8,8,128]{3,2,1,0:T(8,128)S(1)} collective-permute-done((f32[5,8,8,128]{3,2,1,0:T(8,128)S(1)}, f32[5,8,8,128]{3,2,1,0:T(8,128)S(1)}, u32[]{:S(2)}, u32[]{:S(2)}) %collective-permute-start.14) | collective-permute-done | bytes 163872 | tf_op jit(solution)/shard_map/ppermute | solution.py:393
  66.9 1.3 %collective-permute-done.15.refs_4_ = f32[5,8,8,128]{3,2,1,0:T(8,128)S(1)} collective-permute-done((f32[5,8,8,128]{3,2,1,0:T(8,128)S(1)}, f32[5,8,8,128]{3,2,1,0:T(8,128)S(1)}, u32[]{:S(2)}, u32[]{:S(2)}) %collective-permute-start.15) | collective-permute-done | bytes 163872 | tf_op jit(solution)/shard_map/ppermute | solution.py:394
  68.1 2.9 %advance.5 = (f32[5,8,8,128]{3,2,1,0:T(8,128)S(1)}, f32[5,8,8,128]{3,2,1,0:T(8,128)S(1)}) custom-call(f32[18,8,128]{2,1,0:T(8,128)S(1)} %waves.1, f32[26,32,8,128]{3,2,1,0:T(8,128)S(1)} %get-tuple-element.61.refs_0_, f32[26,32,8,128]{3,2,1,0:T(8,128)S(1)} %get-tuple-element.62.refs_1_, f32[5,32,8,128]{3,2,1,0:T(8,128)S(1)} %get-tuple-element.63.refs_2_, ...), custom_call_target="tpu_custom_call" | custom-call | tf_op jit(solution)/shard_map/advance/pallas_call | solution.py:375
  71.1 1.4 %collective-permute-start.16 = (f32[5,8,8,128]{3,2,1,0:T(8,128)S(1)}, f32[5,8,8,128]{3,2,1,0:T(8,128)S(1)}, u32[]{:S(2)}, u32[]{:S(2)}) collective-permute-start(f32[5,8,8,128]{3,2,1,0:T(8,128)S(1)} %get-tuple-element.80), channel_id=1, source_target_pairs={{0,2},{2,0},{4,6},{6,4},{8,10},{10,8},{12,14},{14,12},{1,3},{3,1},... | collective-permute-start | bytes 491528 | tf_op jit(solution)/shard_map/ppermute | solution.py:409
  72.4 4.4 %collective-permute-done.16 = f32[5,8,8,128]{3,2,1,0:T(8,128)S(1)} collective-permute-done((f32[5,8,8,128]{3,2,1,0:T(8,128)S(1)}, f32[5,8,8,128]{3,2,1,0:T(8,128)S(1)}, u32[]{:S(2)}, u32[]{:S(2)}) %collective-permute-start.16) | collective-permute-done | bytes 163872 | tf_op jit(solution)/shard_map/ppermute | solution.py:409
  76.8 0.7 pad_maximum_fusion
  (18 shorter events, 0.3 us)
Async XLA Ops:
  0.0 2.2 %collective-permute-start = (f32[3,5,8,8,128]{4,3,2,1,0:T(8,128)}, f32[3,5,8,8,128]{4,3,2,1,0:T(8,128)S(1)}, u32[]{:S(2)}, u32[]{:S(2)}) collective-permute-start(f32[3,5,8,8,128]{4,3,2,1,0:T(8,128)} %base.3), channel_id=1, source_target_pairs={{0,1},{1,0},{2,3},{3,2},{4,5},{5,4},{6,7},{7,6},{8,9},{9,8},{10,11... | collective-permute-start | bytes 1474568 | tf_op jit(solution)/shard_map/ppermute | solution.py:322
  4.4 32.4 %collective-permute-start.2 = (f32[5,34,8,128]{3,2,1,0:T(8,128)S(1)}, f32[5,34,8,128]{3,2,1,0:T(8,128)S(1)}, u32[]{:S(2)}, u32[]{:S(2)}) collective-permute-start(f32[5,34,8,128]{3,2,1,0:T(8,128)S(1)} %get-tuple-element.44), channel_id=1, source_target_pairs={{0,12},{2,6},{4,0},{6,10},{8,4},{10,14},{12,8},{14,2},{1,13},{3,7}... | collective-permute-start | bytes 2088968 | tf_op jit(solution)/shard_map/ppermute | solution.py:344
  9.5 27.3 %collective-permute-start.1 = (f32[5,24,8,128]{3,2,1,0:T(8,128)S(1)}, f32[5,24,8,128]{3,2,1,0:T(8,128)S(1)}, u32[]{:S(2)}, u32[]{:S(2)}) collective-permute-start(f32[5,24,8,128]{3,2,1,0:T(8,128)S(1)} %get-tuple-element.43), channel_id=1, source_target_pairs={{0,2},{2,0},{4,6},{6,4},{8,10},{10,8},{12,14},{14,12},{1,3},{3,1},... | collective-permute-start | bytes 1474568 | tf_op jit(solution)/shard_map/ppermute | solution.py:344
  9.5 27.3 %collective-permute-start.3 = (f32[5,22,8,128]{3,2,1,0:T(8,128)S(1)}, f32[5,22,8,128]{3,2,1,0:T(8,128)S(1)}, u32[]{:S(2)}, u32[]{:S(2)}) collective-permute-start(f32[5,22,8,128]{3,2,1,0:T(8,128)S(1)} %get-tuple-element.45), channel_id=1, source_target_pairs={{0,14},{2,4},{4,2},{6,8},{8,6},{10,12},{12,10},{14,0},{1,15},{3,5}... | collective-permute-start | bytes 1351688 | tf_op jit(solution)/shard_map/ppermute | solution.py:344
  13.6 30.7 %collective-permute-start.4 = (f32[5,16,8,128]{3,2,1,0:T(8,128)S(1)}, f32[5,16,8,128]{3,2,1,0:T(8,128)S(1)}, u32[]{:S(2)}, u32[]{:S(2)}) collective-permute-start(f32[5,16,8,128]{3,2,1,0:T(8,128)S(1)} %get-tuple-element.50), channel_id=1, source_target_pairs={{0,2},{2,0},{4,6},{6,4},{8,10},{10,8},{12,14},{14,12},{1,3},{3,1},... | collective-permute-start | bytes 983048 | tf_op jit(solution)/shard_map/ppermute | solution.py:344
  14.3 29.8 %collective-permute-start.5 = (f32[5,12,8,128]{3,2,1,0:T(8,128)S(1)}, f32[5,12,8,128]{3,2,1,0:T(8,128)S(1)}, u32[]{:S(2)}, u32[]{:S(2)}) collective-permute-start(f32[5,12,8,128]{3,2,1,0:T(8,128)S(1)} %get-tuple-element.51), channel_id=1, source_target_pairs={{0,14},{2,4},{4,2},{6,8},{8,6},{10,12},{12,10},{14,0},{1,15},{3,5}... | collective-permute-start | bytes 737288 | tf_op jit(solution)/shard_map/ppermute | solution.py:344
  36.8 2.1 %collective-permute-start.6 = (f32[5,8,8,128]{3,2,1,0:T(8,128)S(1)}, f32[5,8,8,128]{3,2,1,0:T(8,128)S(1)}, u32[]{:S(2)}, u32[]{:S(2)}) collective-permute-start(f32[5,8,8,128]{3,2,1,0:T(8,128)S(1)} %slice.12), channel_id=1, source_target_pairs={{0,1},{1,0},{2,3},{3,2},{4,5},{5,4},{6,7},{7,6},{8,9},{9,8},{10,11... | collective-permute-start | bytes 491528 | tf_op jit(solution)/shard_map/ppermute | solution.py:354
  36.9 1.5 %collective-permute-start.7 = (f32[5,6,8,128]{3,2,1,0:T(8,128)S(1)}, f32[5,6,8,128]{3,2,1,0:T(8,128)S(1)}, u32[]{:S(2)}, u32[]{:S(2)}) collective-permute-start(f32[5,6,8,128]{3,2,1,0:T(8,128)S(1)} %slice.13), channel_id=1, source_target_pairs={{0,1},{1,0},{2,3},{3,2},{4,5},{5,4},{6,7},{7,6},{8,9},{9,8},{10,11... | collective-permute-start | bytes 368648 | tf_op jit(solution)/shard_map/ppermute | solution.py:354
  37.5 1.4 %collective-permute-start.8 = (f32[5,6,8,128]{3,2,1,0:T(8,128)S(1)}, f32[5,6,8,128]{3,2,1,0:T(8,128)S(1)}, u32[]{:S(2)}, u32[]{:S(2)}) collective-permute-start(f32[5,6,8,128]{3,2,1,0:T(8,128)S(1)} %slice.14), channel_id=1, source_target_pairs={{0,1},{1,0},{2,3},{3,2},{4,5},{5,4},{6,7},{7,6},{8,9},{9,8},{10,11... | collective-permute-start | bytes 368648 | tf_op jit(solution)/shard_map/ppermute | solution.py:354
  44.3 4.5 %collective-permute-start.9 = (f32[5,16,8,128]{3,2,1,0:T(8,128)S(1)}, f32[5,16,8,128]{3,2,1,0:T(8,128)S(1)}, u32[]{:S(2)}, u32[]{:S(2)}) collective-permute-start(f32[5,16,8,128]{3,2,1,0:T(8,128)S(1)} %collective-permute-done.4.refs_0_), channel_id=1, source_target_pairs={{0,1},{1,0},{2,3},{3,2},{4,5},{5,4},{6,7},{7,6},{8,9},{9,8},{10,11... | collective-permute-start | bytes 983048 | tf_op jit(solution)/shard_map/ppermute | solution.py:354
  44.3 4.5 %collective-permute-start.10 = (f32[5,12,8,128]{3,2,1,0:T(8,128)S(1)}, f32[5,12,8,128]{3,2,1,0:T(8,128)S(1)}, u32[]{:S(2)}, u32[]{:S(2)}) collective-permute-start(f32[5,12,8,128]{3,2,1,0:T(8,128)S(1)} %slice.15), channel_id=1, source_target_pairs={{0,1},{1,0},{2,3},{3,2},{4,5},{5,4},{6,7},{7,6},{8,9},{9,8},{10,11... | collective-permute-start | bytes 737288 | tf_op jit(solution)/shard_map/ppermute | solution.py:354
  44.9 3.9 %collective-permute-start.11 = (f32[5,12,8,128]{3,2,1,0:T(8,128)S(1)}, f32[5,12,8,128]{3,2,1,0:T(8,128)S(1)}, u32[]{:S(2)}, u32[]{:S(2)}) collective-permute-start(f32[5,12,8,128]{3,2,1,0:T(8,128)S(1)} %collective-permute-done.5.refs_2_), channel_id=1, source_target_pairs={{0,1},{1,0},{2,3},{3,2},{4,5},{5,4},{6,7},{7,6},{8,9},{9,8},{10,11... | collective-permute-start | bytes 737288 | tf_op jit(solution)/shard_map/ppermute | solution.py:354
  45.0 8.8 %collective-permute-start.12 = (f32[5,8,8,128]{3,2,1,0:T(8,128)S(1)}, f32[5,8,8,128]{3,2,1,0:T(8,128)S(1)}, u32[]{:S(2)}, u32[]{:S(2)}) collective-permute-start(f32[5,8,8,128]{3,2,1,0:T(8,128)S(1)} %get-tuple-element.66), channel_id=1, source_target_pairs={{0,4},{2,6},{4,8},{6,10},{8,12},{10,14},{12,0},{14,2},{1,5},{3,7},... | collective-permute-start | bytes 491528 | tf_op jit(solution)/shard_map/ppermute | solution.py:393
  45.0 10.1 %collective-permute-start.13 = (f32[5,8,8,128]{3,2,1,0:T(8,128)S(1)}, f32[5,8,8,128]{3,2,1,0:T(8,128)S(1)}, u32[]{:S(2)}, u32[]{:S(2)}) collective-permute-start(f32[5,8,8,128]{3,2,1,0:T(8,128)S(1)} %get-tuple-element.67), channel_id=1, source_target_pairs={{0,12},{2,14},{4,0},{6,2},{8,4},{10,6},{12,8},{14,10},{1,13},{3,15... | collective-permute-start | bytes 491528 | tf_op jit(solution)/shard_map/ppermute | solution.py:394
  57.9 9.0 %collective-permute-start.14 = (f32[5,8,8,128]{3,2,1,0:T(8,128)S(1)}, f32[5,8,8,128]{3,2,1,0:T(8,128)S(1)}, u32[]{:S(2)}, u32[]{:S(2)}) collective-permute-start(f32[5,8,8,128]{3,2,1,0:T(8,128)S(1)} %get-tuple-element.72), channel_id=1, source_target_pairs={{0,4},{2,6},{4,8},{6,10},{8,12},{10,14},{12,0},{14,2},{1,5},{3,7},... | collective-permute-start | bytes 491528 | tf_op jit(solution)/shard_map/ppermute | solution.py:393
  58.8 9.3 %collective-permute-start.15 = (f32[5,8,8,128]{3,2,1,0:T(8,128)S(1)}, f32[5,8,8,128]{3,2,1,0:T(8,128)S(1)}, u32[]{:S(2)}, u32[]{:S(2)}) collective-permute-start(f32[5,8,8,128]{3,2,1,0:T(8,128)S(1)} %get-tuple-element.73), channel_id=1, source_target_pairs={{0,12},{2,14},{4,0},{6,2},{8,4},{10,6},{12,8},{14,10},{1,13},{3,15... | collective-permute-start | bytes 491528 | tf_op jit(solution)/shard_map/ppermute | solution.py:394
  71.1 5.7 %collective-permute-start.16 = (f32[5,8,8,128]{3,2,1,0:T(8,128)S(1)}, f32[5,8,8,128]{3,2,1,0:T(8,128)S(1)}, u32[]{:S(2)}, u32[]{:S(2)}) collective-permute-start(f32[5,8,8,128]{3,2,1,0:T(8,128)S(1)} %get-tuple-element.80), channel_id=1, source_target_pairs={{0,2},{2,0},{4,6},{6,4},{8,10},{10,8},{12,14},{14,12},{1,3},{3,1},... | collective-permute-start | bytes 491528 | tf_op jit(solution)/shard_map/ppermute | solution.py:409

commit v4 on v3

--- a/solution.py
+++ b/solution.py
@@ -77,7 +77,7 @@
             swap_out, other_out, *sends = sends
         at_swap = at_other = at_own = 0
         if chosen == 0:
-            for array, width in ((pert, widths[0]), (force, reach)):
+            for array, width in ((pert, widths[0]), (force, reach - 1)):
                 edge = pl.ds(mine * (tile - width), width)
                 copy(lambda: array.at[other], swap_out, at_swap, tile)
                 copy(lambda: array.at[mine, :, edge], own_out, at_own, width)
@@ -162,7 +162,7 @@
     planes = held.shape[1]
     tile = planes // 2 - reach
     half = tile // 2
-    starts = [list(starts), [0, 0, 0]]
+    starts = [list(start) for start in starts]
     for step, terms in zip(steps, outs):
         width = widths[step]
         held[:, pl.ds(reach + mine * tile, tile)] = held_base[:, at_held : at_held + tile]
@@ -276,8 +276,9 @@
         state[:, pl.ds(near + mine * (far - near), width)] = other_in[:, 0:width]
         force[:, here] = held_state[:, tile : 2 * tile]
         force[:, there] = swap_in[:, tile : 2 * tile]
-        force[:, pl.ds((1 - mine) * far, reach)] = own_in[:, width : width + reach]
-        force[:, pl.ds(mine * far, reach)] = other_in[:, width : width + reach]
+        layers = reach - 1
+        force[:, pl.ds(1 + (1 - mine) * (far - 1), layers)] = own_in[:, width : width + layers]
+        force[:, pl.ds(1 + mine * (far - 1), layers)] = other_in[:, width : width + layers]
         cover = lambda depth: [(near + depth, planes - 2 * (near + depth))]
     else:
         force, left_in, right_in, *refs = refs
@@ -310,6 +311,7 @@
     sets = [each for each in (rounds[0], sum(rounds[1:], [])) if each]
     widths = {step: STAGES * (each[-1] - step + 1) for each in rounds for step in each}
     reach = max(widths.values())
+    state_edge = widths[0] + reach - 1
     planes = 2 * (tile + reach)
 
     swap = [(i, i ^ 1) for i in range(count)]
@@ -327,8 +329,8 @@
         for chosen in which:
             group, start = sets[chosen], chosen == 0
             swapped = len(group) * (tile // 2) + (2 * tile if start else 0)
-            edges = sum(widths[step] // 2 for step in group) + (widths[0] + reach if start else 0)
-            every = sum(widths.values()) // 2 + widths[0] + reach
+            edges = sum(widths[step] // 2 for step in group) + (state_edge if start else 0)
+            every = sum(widths.values()) // 2 + state_edge
             sends += [block(FIELDS, swapped)] + ([block(FIELDS, every)] if start else []) + [block(FIELDS, edges)]
             copies += 2 * len(group) + (6 + steps if start else 0)
         kept = [block(FIELDS, 2 * tile), block(FIELDS, steps * tile)] if keep else []
@@ -346,15 +348,18 @@
     def factors(which, arrived):
         group = sets[which]
         edges = sum(widths[step] // 2 for step in group)
-        starts = [2 * tile, widths[0] + reach, widths[0] + reach] if which == 0 else [0, 0, 0]
+        starts = [2 * tile, state_edge, state_edge] if which == 0 else [0, 0, 0]
         if which > 0:
-            starts[1] = widths[0] + reach + sum(widths[step] // 2 for each in sets[:which] for step in each)
+            starts[1] = state_edge + sum(widths[step] // 2 for each in sets[:which] for step in each)
         sizes = (len(group) * tile // 2, edges, edges)
-        crossed = [
-            lax.ppermute(part[:, at : at + size], "vec", core) for part, at, size in zip(arrived, starts, sizes)
-        ]
+        parts = [part[:, at : at + size] for part, at, size in zip(arrived, starts, sizes)]
+        if which == 0:
+            crossed, others = [lax.ppermute(part, "vec", core) for part in parts], (0, 0, 0)
+        else:
+            crossed = [lax.ppermute(jnp.concatenate(parts, axis=1), "vec", core)] * 3
+            others = (0, sizes[0], sizes[0] + edges)
         return pallas(
-            functools.partial(terms_kernel, group, widths, group[0] * tile, starts, reach),
+            functools.partial(terms_kernel, group, widths, group[0] * tile, (starts, others), reach),
             "terms",
             [block(TERMS, planes)] * len(group),
             [VMEM] * 7,

time: 77.8 us -> 76.8 us (0.987)
  transfers between devices with their start and end apart: 17 -> 15, of which waited for: 10 -> 10; matrix products, arithmetic and copies ran while one was open for 0% -> 0% of each run, Pallas kernels for 15% -> 15%
where the time goes in v4:
time: 76.8 us; the launch traced here: 76.6 us
  waiting for transfers between devices  35.6 us (46%)
  starting transfers between devices  20.1 us (26%)
  Pallas kernels  19.9 us (26%)
  other arithmetic  0.83 us (1%)
    ppermute x5, waiting for transfers between devices, exchange(): lax.ppermute(part, 'space', perm)  19.6 us
    pallas_call x3, Pallas kernels, advance(): pallas(functools.partial(advance_kernel, group, widths, reach, first, las...  9.94 us
    ppermute x5, starting transfers between devices, exchange(): lax.ppermute(part, 'space', perm)  9.89 us
    ppermute x2, starting transfers between devices, per_device(): right_in = lax.ppermute(left, 'space', behind)  7.04 us
    ppermute x2, waiting for transfers between devices, per_device(): left_in = lax.ppermute(right, 'space', ahead)  6.14 us
    pallas_call x2, Pallas kernels, pack(): pallas(functools.partial(pack_kernel, sets, widths, reach, which), 'pack'...  4.5 us
    ppermute x1, waiting for transfers between devices, per_device(): given = lax.ppermute(give, 'space', swap)  4.31 us
    ppermute x2, waiting for transfers between devices, per_device(): right_in = lax.ppermute(left, 'space', behind)  2.5 us
  transfers between devices with their start and end apart: 15, of which 10 were waited for; matrix products, arithmetic and copies ran while one was open for 0% of the time, Pallas kernels for 15%

profile of v4, /device:TPU:0, one launch (start us, length us, event | category | flops | bytes accessed | tf_op | source)
XLA Modules:
  0.0 76.6 jit_solution(5474545541011485309)
XLA Ops:
  0.0 0.5 collective-permute-start
  0.5 1.7 %collective-permute-done.base_peer = f32[3,5,8,8,128]{4,3,2,1,0:T(8,128)S(1)} collective-permute-done((f32[3,5,8,8,128]{4,3,2,1,0:T(8,128)}, f32[3,5,8,8,128]{4,3,2,1,0:T(8,128)S(1)}, u32[]{:S(2)}, u32[]{:S(2)}) %collective-permute-start) | collective-permute-done | bytes 491552 | tf_op jit(solution)/shard_map/ppermute | solution.py:324
  2.2 2.2 %pack.2 = (f32[5,24,8,128]{3,2,1,0:T(8,128)S(1)}, f32[5,33,8,128]{3,2,1,0:T(8,128)S(1)}, f32[5,21,8,128]{3,2,1,0:T(8,128)S(1)}) custom-call(s32[6]{0:T(128)} %phase_slot.3, f32[2,5,8,8,128]{4,3,2,1,0:T(8,128)} %pert.3, f32[2,5,8,8,128]{4,3,2,1,0:T(8,128)} %force.3, f32[3,5,8,8,128]{4,3,2,1,0:T(8,128)} %base.3, ...), custom_call_target="tpu_custom_call" | custom-call | tf_op jit(solution)/shard_map/pack/pallas_call | solution.py:337
  4.4 5.0 %collective-permute-start.2 = (f32[5,33,8,128]{3,2,1,0:T(8,128)S(1)}, f32[5,33,8,128]{3,2,1,0:T(8,128)S(1)}, u32[]{:S(2)}, u32[]{:S(2)}) collective-permute-start(f32[5,33,8,128]{3,2,1,0:T(8,128)S(1)} %get-tuple-element.44), channel_id=1, source_target_pairs={{0,12},{2,6},{4,0},{6,10},{8,4},{10,14},{12,8},{14,2},{1,13},{3,7}... | collective-permute-start | bytes 2027528 | tf_op jit(solution)/shard_map/ppermute | solution.py:346
  9.4 1.9 %collective-permute-start.3 = (f32[5,21,8,128]{3,2,1,0:T(8,128)S(1)}, f32[5,21,8,128]{3,2,1,0:T(8,128)S(1)}, u32[]{:S(2)}, u32[]{:S(2)}) collective-permute-start(f32[5,21,8,128]{3,2,1,0:T(8,128)S(1)} %get-tuple-element.45), channel_id=1, source_target_pairs={{0,14},{2,4},{4,2},{6,8},{8,6},{10,12},{12,10},{14,0},{1,15},{3,5}... | collective-permute-start | bytes 1290248 | tf_op jit(solution)/shard_map/ppermute | solution.py:346
  11.3 2.3 %pack.3 = (f32[5,16,8,128]{3,2,1,0:T(8,128)S(1)}, f32[5,12,8,128]{3,2,1,0:T(8,128)S(1)}, f32[5,16,8,128]{3,2,1,0:T(8,128)S(1)}, f32[5,48,8,128]{3,2,1,0:T(8,128)S(1)}) custom-call(s32[6]{0:T(128)} %phase_slot.3, f32[2,5,8,8,128]{4,3,2,1,0:T(8,128)} %pert.3, f32[2,5,8,8,128]{4,3,2,1,0:T(8,128)} %force.3, f32[3,5,8,8,128]{4,3,2,1,0:T(8,128)} %base.3, ...), custom_call_target="tpu_custom_call" | custom-call | tf_op jit(solution)/shard_map/pack/pallas_call | solution.py:337
  13.6 0.7 collective-permute-start.4
  14.3 2.3 %collective-permute-start.5 = (f32[5,12,8,128]{3,2,1,0:T(8,128)S(1)}, f32[5,12,8,128]{3,2,1,0:T(8,128)S(1)}, u32[]{:S(2)}, u32[]{:S(2)}) collective-permute-start(f32[5,12,8,128]{3,2,1,0:T(8,128)S(1)} %get-tuple-element.51), channel_id=1, source_target_pairs={{0,14},{2,4},{4,2},{6,8},{8,6},{10,12},{12,10},{14,0},{1,15},{3,5}... | collective-permute-start | bytes 737288 | tf_op jit(solution)/shard_map/ppermute | solution.py:346
  16.6 0.7 waves.1
  17.3 18.6 %collective-permute-done.3.refs_2_.refs_5_ = f32[5,21,8,128]{3,2,1,0:T(8,128)S(1)} collective-permute-done((f32[5,21,8,128]{3,2,1,0:T(8,128)S(1)}, f32[5,21,8,128]{3,2,1,0:T(8,128)S(1)}, u32[]{:S(2)}, u32[]{:S(2)}) %collective-permute-start.3) | collective-permute-done | bytes 430112 | tf_op jit(solution)/shard_map/ppermute | solution.py:346
  36.0 0.6 collective-permute-start.7
  36.5 0.1 collective-permute-start.8
  36.7 0.9 %collective-permute-done.7.refs_4_ = f32[5,6,8,128]{3,2,1,0:T(8,128)S(1)} collective-permute-done((f32[5,6,8,128]{3,2,1,0:T(8,128)S(1)}, f32[5,6,8,128]{3,2,1,0:T(8,128)S(1)}, u32[]{:S(2)}, u32[]{:S(2)}) %collective-permute-start.7) | collective-permute-done | bytes 122912 | tf_op jit(solution)/shard_map/ppermute | solution.py:357
  37.5 0.4 collective-permute-done.8.refs_5_
  38.0 0.8 terms.2
  38.7 4.1 %advance.3 = (f32[5,32,8,128]{3,2,1,0:T(8,128)S(1)}, f32[5,16,8,128]{3,2,1,0:T(8,128)S(1)}, f32[5,8,8,128]{3,2,1,0:T(8,128)S(1)}, f32[5,8,8,128]{3,2,1,0:T(8,128)S(1)}) custom-call(f32[18,8,128]{2,1,0:T(8,128)S(1)} %waves.1, f32[26,32,8,128]{3,2,1,0:T(8,128)S(1)} %get-tuple-element.55.refs_0_, f32[26,32,8,128]{3,2,1,0:T(8,128)S(1)} %get-tuple-element.56.refs_1_, ...), custom_call_target="tpu_custom_call" | custom-call | tf_op jit(solution)/shard_map/advance/pallas_call | solution.py:380
  42.8 1.1 %collective-permute-done.4.refs_0_ = f32[5,16,8,128]{3,2,1,0:T(8,128)S(1)} collective-permute-done((f32[5,16,8,128]{3,2,1,0:T(8,128)S(1)}, f32[5,16,8,128]{3,2,1,0:T(8,128)S(1)}, u32[]{:S(2)}, u32[]{:S(2)}) %collective-permute-start.4) | collective-permute-done | bytes 327712 | tf_op jit(solution)/shard_map/ppermute | solution.py:346
  44.1 3.8 %collective-permute-start.11 = (f32[5,8,8,128]{3,2,1,0:T(8,128)S(1)}, f32[5,8,8,128]{3,2,1,0:T(8,128)S(1)}, u32[]{:S(2)}, u32[]{:S(2)}) collective-permute-start(f32[5,8,8,128]{3,2,1,0:T(8,128)S(1)} %get-tuple-element.67), channel_id=1, source_target_pairs={{0,12},{2,14},{4,0},{6,2},{8,4},{10,6},{12,8},{14,10},{1,13},{3,15... | collective-permute-start | bytes 491528 | tf_op jit(solution)/shard_map/ppermute | solution.py:399
  47.9 1.5 %terms.3 = (f32[26,32,8,128]{3,2,1,0:T(8,128)S(1)}, f32[26,32,8,128]{3,2,1,0:T(8,128)S(1)}, f32[26,32,8,128]{3,2,1,0:T(8,128)S(1)}, f32[26,32,8,128]{3,2,1,0:T(8,128)S(1)}) custom-call(f32[5,48,8,128]{3,2,1,0:T(8,128)S(1)} %get-tuple-element.49.held_base, f32[5,16,8,128]{3,2,1,0:T(8,128)S(1)} %collective-permute-done.4.refs_0_, ...), custom_call_target="tpu_custom_call" | custom-call | tf_op jit(solution)/shard_map/terms/pallas_call | solution.py:361
  49.4 1.2 %interior.2 = (f32[5,16,8,128]{3,2,1,0:T(8,128)S(1)}, f32[5,16,8,128]{3,2,1,0:T(8,128)S(1)}, f32[5,16,8,128]{3,2,1,0:T(8,128)S(1)}, f32[5,16,8,128]{3,2,1,0:T(8,128)S(1)}) custom-call(f32[18,8,128]{2,1,0:T(8,128)S(1)} %waves.1, f32[26,32,8,128]{3,2,1,0:T(8,128)S(1)} %get-tuple-element.64.refs_0_, f32[26,32,8,128]{3,2,1,0:T(8,128)S(1)} %get-tuple-element.65.refs_1_, ...), custom_call_target="tpu_custom_call" | custom-call | tf_op jit(solution)/shard_map/interior/pallas_call | solution.py:404
  50.7 2.2 %collective-permute-done.10.refs_3_ = f32[5,8,8,128]{3,2,1,0:T(8,128)S(1)} collective-permute-done((f32[5,8,8,128]{3,2,1,0:T(8,128)S(1)}, f32[5,8,8,128]{3,2,1,0:T(8,128)S(1)}, u32[]{:S(2)}, u32[]{:S(2)}) %collective-permute-start.10) | collective-permute-done | bytes 163872 | tf_op jit(solution)/shard_map/ppermute | solution.py:398
  52.9 1.2 %collective-permute-done.11.refs_4_ = f32[5,8,8,128]{3,2,1,0:T(8,128)S(1)} collective-permute-done((f32[5,8,8,128]{3,2,1,0:T(8,128)S(1)}, f32[5,8,8,128]{3,2,1,0:T(8,128)S(1)}, u32[]{:S(2)}, u32[]{:S(2)}) %collective-permute-start.11) | collective-permute-done | bytes 163872 | tf_op jit(solution)/shard_map/ppermute | solution.py:399
  54.1 2.9 %advance.4 = (f32[5,16,8,128]{3,2,1,0:T(8,128)S(1)}, f32[5,8,8,128]{3,2,1,0:T(8,128)S(1)}, f32[5,8,8,128]{3,2,1,0:T(8,128)S(1)}) custom-call(f32[18,8,128]{2,1,0:T(8,128)S(1)} %waves.1, f32[26,32,8,128]{3,2,1,0:T(8,128)S(1)} %get-tuple-element.64.refs_0_, f32[26,32,8,128]{3,2,1,0:T(8,128)S(1)} %get-tuple-element.65.refs_1_, ...), custom_call_target="tpu_custom_call" | custom-call | tf_op jit(solution)/shard_map/advance/pallas_call | solution.py:380
  57.0 0.6 collective-permute-start.12
  57.7 3.2 %collective-permute-start.13 = (f32[5,8,8,128]{3,2,1,0:T(8,128)S(1)}, f32[5,8,8,128]{3,2,1,0:T(8,128)S(1)}, u32[]{:S(2)}, u32[]{:S(2)}) collective-permute-start(f32[5,8,8,128]{3,2,1,0:T(8,128)S(1)} %get-tuple-element.73), channel_id=1, source_target_pairs={{0,12},{2,14},{4,0},{6,2},{8,4},{10,6},{12,8},{14,10},{1,13},{3,15... | collective-permute-start | bytes 491528 | tf_op jit(solution)/shard_map/ppermute | solution.py:399
  60.9 1.2 %interior.3 = (f32[5,16,8,128]{3,2,1,0:T(8,128)S(1)}, f32[5,16,8,128]{3,2,1,0:T(8,128)S(1)}, f32[5,16,8,128]{3,2,1,0:T(8,128)S(1)}, f32[5,16,8,128]{3,2,1,0:T(8,128)S(1)}) custom-call(f32[18,8,128]{2,1,0:T(8,128)S(1)} %waves.1, f32[26,32,8,128]{3,2,1,0:T(8,128)S(1)} %get-tuple-element.61.refs_0_, f32[26,32,8,128]{3,2,1,0:T(8,128)S(1)} %get-tuple-element.62.refs_1_, ...), custom_call_target="tpu_custom_call" | custom-call | tf_op jit(solution)/shard_map/interior/pallas_call | solution.py:404
  62.1 3.9 %collective-permute-done.12.refs_3_ = f32[5,8,8,128]{3,2,1,0:T(8,128)S(1)} collective-permute-done((f32[5,8,8,128]{3,2,1,0:T(8,128)S(1)}, f32[5,8,8,128]{3,2,1,0:T(8,128)S(1)}, u32[]{:S(2)}, u32[]{:S(2)}) %collective-permute-start.12) | collective-permute-done | bytes 163872 | tf_op jit(solution)/shard_map/ppermute | solution.py:398
  66.0 1.3 %collective-permute-done.13.refs_4_ = f32[5,8,8,128]{3,2,1,0:T(8,128)S(1)} collective-permute-done((f32[5,8,8,128]{3,2,1,0:T(8,128)S(1)}, f32[5,8,8,128]{3,2,1,0:T(8,128)S(1)}, u32[]{:S(2)}, u32[]{:S(2)}) %collective-permute-start.13) | collective-permute-done | bytes 163872 | tf_op jit(solution)/shard_map/ppermute | solution.py:399
  67.3 3.0 %advance.5 = (f32[5,8,8,128]{3,2,1,0:T(8,128)S(1)}, f32[5,8,8,128]{3,2,1,0:T(8,128)S(1)}) custom-call(f32[18,8,128]{2,1,0:T(8,128)S(1)} %waves.1, f32[26,32,8,128]{3,2,1,0:T(8,128)S(1)} %get-tuple-element.61.refs_0_, f32[26,32,8,128]{3,2,1,0:T(8,128)S(1)} %get-tuple-element.62.refs_1_, f32[5,32,8,128]{3,2,1,0:T(8,128)S(1)} %get-tuple-element.63.refs_2_, ...), custom_call_target="tpu_custom_call" | custom-call | tf_op jit(solution)/shard_map/advance/pallas_call | solution.py:380
  70.3 1.3 %collective-permute-start.14 = (f32[5,8,8,128]{3,2,1,0:T(8,128)S(1)}, f32[5,8,8,128]{3,2,1,0:T(8,128)S(1)}, u32[]{:S(2)}, u32[]{:S(2)}) collective-permute-start(f32[5,8,8,128]{3,2,1,0:T(8,128)S(1)} %get-tuple-element.80), channel_id=1, source_target_pairs={{0,2},{2,0},{4,6},{6,4},{8,10},{10,8},{12,14},{14,12},{1,3},{3,1},... | collective-permute-start | bytes 491528 | tf_op jit(solution)/shard_map/ppermute | solution.py:414
  71.5 4.3 %collective-permute-done.14 = f32[5,8,8,128]{3,2,1,0:T(8,128)S(1)} collective-permute-done((f32[5,8,8,128]{3,2,1,0:T(8,128)S(1)}, f32[5,8,8,128]{3,2,1,0:T(8,128)S(1)}, u32[]{:S(2)}, u32[]{:S(2)}) %collective-permute-start.14) | collective-permute-done | bytes 163872 | tf_op jit(solution)/shard_map/ppermute | solution.py:414
  75.9 0.7 pad_maximum_fusion.1
  (15 shorter events, 0.3 us)
Async XLA Ops:
  0.0 2.2 %collective-permute-start = (f32[3,5,8,8,128]{4,3,2,1,0:T(8,128)}, f32[3,5,8,8,128]{4,3,2,1,0:T(8,128)S(1)}, u32[]{:S(2)}, u32[]{:S(2)}) collective-permute-start(f32[3,5,8,8,128]{4,3,2,1,0:T(8,128)} %base.3), channel_id=1, source_target_pairs={{0,1},{1,0},{2,3},{3,2},{4,5},{5,4},{6,7},{7,6},{8,9},{9,8},{10,11... | collective-permute-start | bytes 1474568 | tf_op jit(solution)/shard_map/ppermute | solution.py:324
  4.4 31.5 %collective-permute-start.2 = (f32[5,33,8,128]{3,2,1,0:T(8,128)S(1)}, f32[5,33,8,128]{3,2,1,0:T(8,128)S(1)}, u32[]{:S(2)}, u32[]{:S(2)}) collective-permute-start(f32[5,33,8,128]{3,2,1,0:T(8,128)S(1)} %get-tuple-element.44), channel_id=1, source_target_pairs={{0,12},{2,6},{4,0},{6,10},{8,4},{10,14},{12,8},{14,2},{1,13},{3,7}... | collective-permute-start | bytes 2027528 | tf_op jit(solution)/shard_map/ppermute | solution.py:346
  9.4 26.5 %collective-permute-start.1 = (f32[5,24,8,128]{3,2,1,0:T(8,128)S(1)}, f32[5,24,8,128]{3,2,1,0:T(8,128)S(1)}, u32[]{:S(2)}, u32[]{:S(2)}) collective-permute-start(f32[5,24,8,128]{3,2,1,0:T(8,128)S(1)} %get-tuple-element.43), channel_id=1, source_target_pairs={{0,2},{2,0},{4,6},{6,4},{8,10},{10,8},{12,14},{14,12},{1,3},{3,1},... | collective-permute-start | bytes 1474568 | tf_op jit(solution)/shard_map/ppermute | solution.py:346
  9.4 26.4 %collective-permute-start.3 = (f32[5,21,8,128]{3,2,1,0:T(8,128)S(1)}, f32[5,21,8,128]{3,2,1,0:T(8,128)S(1)}, u32[]{:S(2)}, u32[]{:S(2)}) collective-permute-start(f32[5,21,8,128]{3,2,1,0:T(8,128)S(1)} %get-tuple-element.45), channel_id=1, source_target_pairs={{0,14},{2,4},{4,2},{6,8},{8,6},{10,12},{12,10},{14,0},{1,15},{3,5}... | collective-permute-start | bytes 1290248 | tf_op jit(solution)/shard_map/ppermute | solution.py:346
  13.6 30.3 %collective-permute-start.4 = (f32[5,16,8,128]{3,2,1,0:T(8,128)S(1)}, f32[5,16,8,128]{3,2,1,0:T(8,128)S(1)}, u32[]{:S(2)}, u32[]{:S(2)}) collective-permute-start(f32[5,16,8,128]{3,2,1,0:T(8,128)S(1)} %get-tuple-element.50), channel_id=1, source_target_pairs={{0,2},{2,0},{4,6},{6,4},{8,10},{10,8},{12,14},{14,12},{1,3},{3,1},... | collective-permute-start | bytes 983048 | tf_op jit(solution)/shard_map/ppermute | solution.py:346
  14.3 28.5 %collective-permute-start.5 = (f32[5,12,8,128]{3,2,1,0:T(8,128)S(1)}, f32[5,12,8,128]{3,2,1,0:T(8,128)S(1)}, u32[]{:S(2)}, u32[]{:S(2)}) collective-permute-start(f32[5,12,8,128]{3,2,1,0:T(8,128)S(1)} %get-tuple-element.51), channel_id=1, source_target_pairs={{0,14},{2,4},{4,2},{6,8},{8,6},{10,12},{12,10},{14,0},{1,15},{3,5}... | collective-permute-start | bytes 737288 | tf_op jit(solution)/shard_map/ppermute | solution.py:346
  35.9 2.1 %collective-permute-start.6 = (f32[5,8,8,128]{3,2,1,0:T(8,128)S(1)}, f32[5,8,8,128]{3,2,1,0:T(8,128)S(1)}, u32[]{:S(2)}, u32[]{:S(2)}) collective-permute-start(f32[5,8,8,128]{3,2,1,0:T(8,128)S(1)} %slice.12), channel_id=1, source_target_pairs={{0,1},{1,0},{2,3},{3,2},{4,5},{5,4},{6,7},{7,6},{8,9},{9,8},{10,11... | collective-permute-start | bytes 491528 | tf_op jit(solution)/shard_map/ppermute | solution.py:357
  36.0 1.5 %collective-permute-start.7 = (f32[5,6,8,128]{3,2,1,0:T(8,128)S(1)}, f32[5,6,8,128]{3,2,1,0:T(8,128)S(1)}, u32[]{:S(2)}, u32[]{:S(2)}) collective-permute-start(f32[5,6,8,128]{3,2,1,0:T(8,128)S(1)} %slice.13), channel_id=1, source_target_pairs={{0,1},{1,0},{2,3},{3,2},{4,5},{5,4},{6,7},{7,6},{8,9},{9,8},{10,11... | collective-permute-start | bytes 368648 | tf_op jit(solution)/shard_map/ppermute | solution.py:357
  36.5 1.4 %collective-permute-start.8 = (f32[5,6,8,128]{3,2,1,0:T(8,128)S(1)}, f32[5,6,8,128]{3,2,1,0:T(8,128)S(1)}, u32[]{:S(2)}, u32[]{:S(2)}) collective-permute-start(f32[5,6,8,128]{3,2,1,0:T(8,128)S(1)} %slice.14), channel_id=1, source_target_pairs={{0,1},{1,0},{2,3},{3,2},{4,5},{5,4},{6,7},{7,6},{8,9},{9,8},{10,11... | collective-permute-start | bytes 368648 | tf_op jit(solution)/shard_map/ppermute | solution.py:357
  43.9 4.0 %collective-permute-start.9 = (f32[5,40,8,128]{3,2,1,0:T(8,128)S(1)}, f32[5,40,8,128]{3,2,1,0:T(8,128)S(1)}, u32[]{:S(2)}, u32[]{:S(2)}) collective-permute-start(f32[5,40,8,128]{3,2,1,0:T(8,128)S(1)} %pad_maximum_fusion), channel_id=1, source_target_pairs={{0,1},{1,0},{2,3},{3,2},{4,5},{5,4},{6,7},{7,6},{8,9},{9,8},{10,11... | collective-permute-start | bytes 2457608 | tf_op jit(solution)/shard_map/ppermute | solution.py:359
  44.0 8.9 %collective-permute-start.10 = (f32[5,8,8,128]{3,2,1,0:T(8,128)S(1)}, f32[5,8,8,128]{3,2,1,0:T(8,128)S(1)}, u32[]{:S(2)}, u32[]{:S(2)}) collective-permute-start(f32[5,8,8,128]{3,2,1,0:T(8,128)S(1)} %get-tuple-element.66), channel_id=1, source_target_pairs={{0,4},{2,6},{4,8},{6,10},{8,12},{10,14},{12,0},{14,2},{1,5},{3,7},... | collective-permute-start | bytes 491528 | tf_op jit(solution)/shard_map/ppermute | solution.py:398
  44.1 10.1 %collective-permute-start.11 = (f32[5,8,8,128]{3,2,1,0:T(8,128)S(1)}, f32[5,8,8,128]{3,2,1,0:T(8,128)S(1)}, u32[]{:S(2)}, u32[]{:S(2)}) collective-permute-start(f32[5,8,8,128]{3,2,1,0:T(8,128)S(1)} %get-tuple-element.67), channel_id=1, source_target_pairs={{0,12},{2,14},{4,0},{6,2},{8,4},{10,6},{12,8},{14,10},{1,13},{3,15... | collective-permute-start | bytes 491528 | tf_op jit(solution)/shard_map/ppermute | solution.py:399
  57.0 9.0 %collective-permute-start.12 = (f32[5,8,8,128]{3,2,1,0:T(8,128)S(1)}, f32[5,8,8,128]{3,2,1,0:T(8,128)S(1)}, u32[]{:S(2)}, u32[]{:S(2)}) collective-permute-start(f32[5,8,8,128]{3,2,1,0:T(8,128)S(1)} %get-tuple-element.72), channel_id=1, source_target_pairs={{0,4},{2,6},{4,8},{6,10},{8,12},{10,14},{12,0},{14,2},{1,5},{3,7},... | collective-permute-start | bytes 491528 | tf_op jit(solution)/shard_map/ppermute | solution.py:398
  57.7 9.6 %collective-permute-start.13 = (f32[5,8,8,128]{3,2,1,0:T(8,128)S(1)}, f32[5,8,8,128]{3,2,1,0:T(8,128)S(1)}, u32[]{:S(2)}, u32[]{:S(2)}) collective-permute-start(f32[5,8,8,128]{3,2,1,0:T(8,128)S(1)} %get-tuple-element.73), channel_id=1, source_target_pairs={{0,12},{2,14},{4,0},{6,2},{8,4},{10,6},{12,8},{14,10},{1,13},{3,15... | collective-permute-start | bytes 491528 | tf_op jit(solution)/shard_map/ppermute | solution.py:399
  70.3 5.6 %collective-permute-start.14 = (f32[5,8,8,128]{3,2,1,0:T(8,128)S(1)}, f32[5,8,8,128]{3,2,1,0:T(8,128)S(1)}, u32[]{:S(2)}, u32[]{:S(2)}) collective-permute-start(f32[5,8,8,128]{3,2,1,0:T(8,128)S(1)} %get-tuple-element.80), channel_id=1, source_target_pairs={{0,2},{2,0},{4,6},{6,4},{8,10},{10,8},{12,14},{14,12},{1,3},{3,1},... | collective-permute-start | bytes 491528 | tf_op jit(solution)/shard_map/ppermute | solution.py:414

commit v5 on v4

--- a/solution.py
+++ b/solution.py
@@ -46,7 +46,10 @@
 
 def pack_kernel(sets, widths, reach, which, phase_slot, pert, force, base, base_peer, *refs):
     count = sum(3 if chosen == 0 else 2 for chosen in which)
-    sends, kept, sem = refs[:count], refs[count:-1], refs[-1]
+    sends, kept, (slots, sem) = refs[:count], refs[count:-2], refs[-2:]
+    fetched = pltpu.make_async_copy(phase_slot, slots, sem.at[sem.shape[0] - 1])
+    fetched.start()
+    waiting = [fetched]
     mine = parity()
     core = lax.axis_index("vec")
     other = 1 - mine
@@ -60,9 +63,11 @@
         waits[-1].start()
 
     def copy_base(step, cells, target, at, count):
+        if waiting:
+            waiting.pop().wait()
         into = target.at[:, pl.ds(at, count)]
-        held = lax.div(phase_slot[step], local) == core
-        row = lax.rem(phase_slot[step], local)
+        held = lax.div(slots[step], local) == core
+        row = lax.rem(slots[step], local)
         first, second = [
             pltpu.make_async_copy(array.at[row, :, cells], into, sem.at[len(waits)]) for array in (base, base_peer)
         ]
@@ -338,8 +343,8 @@
             functools.partial(pack_kernel, sets, widths, reach, which),
             "pack",
             sends + kept,
-            [SMEM] + [HBM] * 4,
-            [pltpu.SemaphoreType.DMA((copies + (2 + steps if keep else 0),))],
+            [HBM] * 5,
+            [pltpu.SMEM(phase_slot.shape, jnp.int32), pltpu.SemaphoreType.DMA((copies + (3 + steps if keep else 1),))],
         )(*in_place(phase_slot, perturbation, forcing, base_flow), base_peer)
 
     def exchange(packed, perms):

time: 76.8 us -> 76.6 us (level)
  no operation moved by 1% of the time
where the time goes in v5:
time: 76.6 us; the launch traced here: 76.4 us
  waiting for transfers between devices  35.6 us (46%)
  starting transfers between devices  20.1 us (26%)
  Pallas kernels  19.7 us (26%)
  other arithmetic  0.83 us (1%)
    ppermute x5, waiting for transfers between devices, exchange(): lax.ppermute(part, 'space', perm)  19.6 us
    pallas_call x3, Pallas kernels, advance(): pallas(functools.partial(advance_kernel, group, widths, reach, first, las...  9.94 us
    ppermute x5, starting transfers between devices, exchange(): lax.ppermute(part, 'space', perm)  9.89 us
    ppermute x2, starting transfers between devices, per_device(): right_in = lax.ppermute(left, 'space', behind)  7.04 us
    ppermute x2, waiting for transfers between devices, per_device(): left_in = lax.ppermute(right, 'space', ahead)  6.13 us
    ppermute x1, waiting for transfers between devices, per_device(): given = lax.ppermute(give, 'space', swap)  4.32 us
    pallas_call x2, Pallas kernels, pack(): pallas(functools.partial(pack_kernel, sets, widths, reach, which), 'pack'...  4.29 us
    ppermute x2, waiting for transfers between devices, per_device(): right_in = lax.ppermute(left, 'space', behind)  2.5 us
  transfers between devices with their start and end apart: 15, of which 10 were waited for; matrix products, arithmetic and copies ran while one was open for 0% of the time, Pallas kernels for 15%

profile of v5, /device:TPU:0, one launch (start us, length us, event | category | flops | bytes accessed | tf_op | source)
XLA Modules:
  0.0 76.4 jit_solution(18040958188677417788)
XLA Ops:
  0.0 0.5 collective-permute-start
  0.5 1.7 %collective-permute-done.base_peer = f32[3,5,8,8,128]{4,3,2,1,0:T(8,128)S(1)} collective-permute-done((f32[3,5,8,8,128]{4,3,2,1,0:T(8,128)}, f32[3,5,8,8,128]{4,3,2,1,0:T(8,128)S(1)}, u32[]{:S(2)}, u32[]{:S(2)}) %collective-permute-start) | collective-permute-done | bytes 491552 | tf_op jit(solution)/shard_map/ppermute | solution.py:329
  2.2 2.0 %pack.2 = (f32[5,24,8,128]{3,2,1,0:T(8,128)S(1)}, f32[5,33,8,128]{3,2,1,0:T(8,128)S(1)}, f32[5,21,8,128]{3,2,1,0:T(8,128)S(1)}) custom-call(s32[6]{0:T(128)} %phase_slot.3, f32[2,5,8,8,128]{4,3,2,1,0:T(8,128)} %pert.3, f32[2,5,8,8,128]{4,3,2,1,0:T(8,128)} %force.3, f32[3,5,8,8,128]{4,3,2,1,0:T(8,128)} %base.3, ...), custom_call_target="tpu_custom_call" | custom-call | tf_op jit(solution)/shard_map/pack/pallas_call | solution.py:342
  4.2 5.0 %collective-permute-start.2 = (f32[5,33,8,128]{3,2,1,0:T(8,128)S(1)}, f32[5,33,8,128]{3,2,1,0:T(8,128)S(1)}, u32[]{:S(2)}, u32[]{:S(2)}) collective-permute-start(f32[5,33,8,128]{3,2,1,0:T(8,128)S(1)} %get-tuple-element.44), channel_id=1, source_target_pairs={{0,12},{2,6},{4,0},{6,10},{8,4},{10,14},{12,8},{14,2},{1,13},{3,7}... | collective-permute-start | bytes 2027528 | tf_op jit(solution)/shard_map/ppermute | solution.py:351
  9.2 1.9 %collective-permute-start.3 = (f32[5,21,8,128]{3,2,1,0:T(8,128)S(1)}, f32[5,21,8,128]{3,2,1,0:T(8,128)S(1)}, u32[]{:S(2)}, u32[]{:S(2)}) collective-permute-start(f32[5,21,8,128]{3,2,1,0:T(8,128)S(1)} %get-tuple-element.45), channel_id=1, source_target_pairs={{0,14},{2,4},{4,2},{6,8},{8,6},{10,12},{12,10},{14,0},{1,15},{3,5}... | collective-permute-start | bytes 1290248 | tf_op jit(solution)/shard_map/ppermute | solution.py:351
  11.1 2.3 %pack.3 = (f32[5,16,8,128]{3,2,1,0:T(8,128)S(1)}, f32[5,12,8,128]{3,2,1,0:T(8,128)S(1)}, f32[5,16,8,128]{3,2,1,0:T(8,128)S(1)}, f32[5,48,8,128]{3,2,1,0:T(8,128)S(1)}) custom-call(s32[6]{0:T(128)} %phase_slot.3, f32[2,5,8,8,128]{4,3,2,1,0:T(8,128)} %pert.3, f32[2,5,8,8,128]{4,3,2,1,0:T(8,128)} %force.3, f32[3,5,8,8,128]{4,3,2,1,0:T(8,128)} %base.3, ...), custom_call_target="tpu_custom_call" | custom-call | tf_op jit(solution)/shard_map/pack/pallas_call | solution.py:342
  13.4 0.7 collective-permute-start.4
  14.1 2.3 %collective-permute-start.5 = (f32[5,12,8,128]{3,2,1,0:T(8,128)S(1)}, f32[5,12,8,128]{3,2,1,0:T(8,128)S(1)}, u32[]{:S(2)}, u32[]{:S(2)}) collective-permute-start(f32[5,12,8,128]{3,2,1,0:T(8,128)S(1)} %get-tuple-element.51), channel_id=1, source_target_pairs={{0,14},{2,4},{4,2},{6,8},{8,6},{10,12},{12,10},{14,0},{1,15},{3,5}... | collective-permute-start | bytes 737288 | tf_op jit(solution)/shard_map/ppermute | solution.py:351
  16.4 0.7 waves.1
  17.1 18.6 %collective-permute-done.3.refs_2_.refs_5_ = f32[5,21,8,128]{3,2,1,0:T(8,128)S(1)} collective-permute-done((f32[5,21,8,128]{3,2,1,0:T(8,128)S(1)}, f32[5,21,8,128]{3,2,1,0:T(8,128)S(1)}, u32[]{:S(2)}, u32[]{:S(2)}) %collective-permute-start.3) | collective-permute-done | bytes 430112 | tf_op jit(solution)/shard_map/ppermute | solution.py:351
  35.8 0.6 collective-permute-start.7
  36.4 0.1 collective-permute-start.8
  36.5 0.9 %collective-permute-done.7.refs_4_ = f32[5,6,8,128]{3,2,1,0:T(8,128)S(1)} collective-permute-done((f32[5,6,8,128]{3,2,1,0:T(8,128)S(1)}, f32[5,6,8,128]{3,2,1,0:T(8,128)S(1)}, u32[]{:S(2)}, u32[]{:S(2)}) %collective-permute-start.7) | collective-permute-done | bytes 122912 | tf_op jit(solution)/shard_map/ppermute | solution.py:362
  37.3 0.4 collective-permute-done.8.refs_5_
  37.8 0.8 terms.2
  38.5 4.1 %advance.3 = (f32[5,32,8,128]{3,2,1,0:T(8,128)S(1)}, f32[5,16,8,128]{3,2,1,0:T(8,128)S(1)}, f32[5,8,8,128]{3,2,1,0:T(8,128)S(1)}, f32[5,8,8,128]{3,2,1,0:T(8,128)S(1)}) custom-call(f32[18,8,128]{2,1,0:T(8,128)S(1)} %waves.1, f32[26,32,8,128]{3,2,1,0:T(8,128)S(1)} %get-tuple-element.55.refs_0_, f32[26,32,8,128]{3,2,1,0:T(8,128)S(1)} %get-tuple-element.56.refs_1_, ...), custom_call_target="tpu_custom_call" | custom-call | tf_op jit(solution)/shard_map/advance/pallas_call | solution.py:385
  42.6 1.0 %collective-permute-done.4.refs_0_ = f32[5,16,8,128]{3,2,1,0:T(8,128)S(1)} collective-permute-done((f32[5,16,8,128]{3,2,1,0:T(8,128)S(1)}, f32[5,16,8,128]{3,2,1,0:T(8,128)S(1)}, u32[]{:S(2)}, u32[]{:S(2)}) %collective-permute-start.4) | collective-permute-done | bytes 327712 | tf_op jit(solution)/shard_map/ppermute | solution.py:351
  43.8 3.8 %collective-permute-start.11 = (f32[5,8,8,128]{3,2,1,0:T(8,128)S(1)}, f32[5,8,8,128]{3,2,1,0:T(8,128)S(1)}, u32[]{:S(2)}, u32[]{:S(2)}) collective-permute-start(f32[5,8,8,128]{3,2,1,0:T(8,128)S(1)} %get-tuple-element.67), channel_id=1, source_target_pairs={{0,12},{2,14},{4,0},{6,2},{8,4},{10,6},{12,8},{14,10},{1,13},{3,15... | collective-permute-start | bytes 491528 | tf_op jit(solution)/shard_map/ppermute | solution.py:404
  47.7 1.5 %terms.3 = (f32[26,32,8,128]{3,2,1,0:T(8,128)S(1)}, f32[26,32,8,128]{3,2,1,0:T(8,128)S(1)}, f32[26,32,8,128]{3,2,1,0:T(8,128)S(1)}, f32[26,32,8,128]{3,2,1,0:T(8,128)S(1)}) custom-call(f32[5,48,8,128]{3,2,1,0:T(8,128)S(1)} %get-tuple-element.49.held_base, f32[5,16,8,128]{3,2,1,0:T(8,128)S(1)} %collective-permute-done.4.refs_0_, ...), custom_call_target="tpu_custom_call" | custom-call | tf_op jit(solution)/shard_map/terms/pallas_call | solution.py:366
  49.2 1.2 %interior.2 = (f32[5,16,8,128]{3,2,1,0:T(8,128)S(1)}, f32[5,16,8,128]{3,2,1,0:T(8,128)S(1)}, f32[5,16,8,128]{3,2,1,0:T(8,128)S(1)}, f32[5,16,8,128]{3,2,1,0:T(8,128)S(1)}) custom-call(f32[18,8,128]{2,1,0:T(8,128)S(1)} %waves.1, f32[26,32,8,128]{3,2,1,0:T(8,128)S(1)} %get-tuple-element.64.refs_0_, f32[26,32,8,128]{3,2,1,0:T(8,128)S(1)} %get-tuple-element.65.refs_1_, ...), custom_call_target="tpu_custom_call" | custom-call | tf_op jit(solution)/shard_map/interior/pallas_call | solution.py:409
  50.4 2.2 %collective-permute-done.10.refs_3_ = f32[5,8,8,128]{3,2,1,0:T(8,128)S(1)} collective-permute-done((f32[5,8,8,128]{3,2,1,0:T(8,128)S(1)}, f32[5,8,8,128]{3,2,1,0:T(8,128)S(1)}, u32[]{:S(2)}, u32[]{:S(2)}) %collective-permute-start.10) | collective-permute-done | bytes 163872 | tf_op jit(solution)/shard_map/ppermute | solution.py:403
  52.7 1.2 %collective-permute-done.11.refs_4_ = f32[5,8,8,128]{3,2,1,0:T(8,128)S(1)} collective-permute-done((f32[5,8,8,128]{3,2,1,0:T(8,128)S(1)}, f32[5,8,8,128]{3,2,1,0:T(8,128)S(1)}, u32[]{:S(2)}, u32[]{:S(2)}) %collective-permute-start.11) | collective-permute-done | bytes 163872 | tf_op jit(solution)/shard_map/ppermute | solution.py:404
  53.9 2.9 %advance.4 = (f32[5,16,8,128]{3,2,1,0:T(8,128)S(1)}, f32[5,8,8,128]{3,2,1,0:T(8,128)S(1)}, f32[5,8,8,128]{3,2,1,0:T(8,128)S(1)}) custom-call(f32[18,8,128]{2,1,0:T(8,128)S(1)} %waves.1, f32[26,32,8,128]{3,2,1,0:T(8,128)S(1)} %get-tuple-element.64.refs_0_, f32[26,32,8,128]{3,2,1,0:T(8,128)S(1)} %get-tuple-element.65.refs_1_, ...), custom_call_target="tpu_custom_call" | custom-call | tf_op jit(solution)/shard_map/advance/pallas_call | solution.py:385
  56.8 0.6 collective-permute-start.12
  57.4 3.2 %collective-permute-start.13 = (f32[5,8,8,128]{3,2,1,0:T(8,128)S(1)}, f32[5,8,8,128]{3,2,1,0:T(8,128)S(1)}, u32[]{:S(2)}, u32[]{:S(2)}) collective-permute-start(f32[5,8,8,128]{3,2,1,0:T(8,128)S(1)} %get-tuple-element.73), channel_id=1, source_target_pairs={{0,12},{2,14},{4,0},{6,2},{8,4},{10,6},{12,8},{14,10},{1,13},{3,15... | collective-permute-start | bytes 491528 | tf_op jit(solution)/shard_map/ppermute | solution.py:404
  60.7 1.2 %interior.3 = (f32[5,16,8,128]{3,2,1,0:T(8,128)S(1)}, f32[5,16,8,128]{3,2,1,0:T(8,128)S(1)}, f32[5,16,8,128]{3,2,1,0:T(8,128)S(1)}, f32[5,16,8,128]{3,2,1,0:T(8,128)S(1)}) custom-call(f32[18,8,128]{2,1,0:T(8,128)S(1)} %waves.1, f32[26,32,8,128]{3,2,1,0:T(8,128)S(1)} %get-tuple-element.61.refs_0_, f32[26,32,8,128]{3,2,1,0:T(8,128)S(1)} %get-tuple-element.62.refs_1_, ...), custom_call_target="tpu_custom_call" | custom-call | tf_op jit(solution)/shard_map/interior/pallas_call | solution.py:409
  61.9 3.9 %collective-permute-done.12.refs_3_ = f32[5,8,8,128]{3,2,1,0:T(8,128)S(1)} collective-permute-done((f32[5,8,8,128]{3,2,1,0:T(8,128)S(1)}, f32[5,8,8,128]{3,2,1,0:T(8,128)S(1)}, u32[]{:S(2)}, u32[]{:S(2)}) %collective-permute-start.12) | collective-permute-done | bytes 163872 | tf_op jit(solution)/shard_map/ppermute | solution.py:403
  65.8 1.3 %collective-permute-done.13.refs_4_ = f32[5,8,8,128]{3,2,1,0:T(8,128)S(1)} collective-permute-done((f32[5,8,8,128]{3,2,1,0:T(8,128)S(1)}, f32[5,8,8,128]{3,2,1,0:T(8,128)S(1)}, u32[]{:S(2)}, u32[]{:S(2)}) %collective-permute-start.13) | collective-permute-done | bytes 163872 | tf_op jit(solution)/shard_map/ppermute | solution.py:404
  67.1 3.0 %advance.5 = (f32[5,8,8,128]{3,2,1,0:T(8,128)S(1)}, f32[5,8,8,128]{3,2,1,0:T(8,128)S(1)}) custom-call(f32[18,8,128]{2,1,0:T(8,128)S(1)} %waves.1, f32[26,32,8,128]{3,2,1,0:T(8,128)S(1)} %get-tuple-element.61.refs_0_, f32[26,32,8,128]{3,2,1,0:T(8,128)S(1)} %get-tuple-element.62.refs_1_, f32[5,32,8,128]{3,2,1,0:T(8,128)S(1)} %get-tuple-element.63.refs_2_, ...), custom_call_target="tpu_custom_call" | custom-call | tf_op jit(solution)/shard_map/advance/pallas_call | solution.py:385
  70.0 1.3 %collective-permute-start.14 = (f32[5,8,8,128]{3,2,1,0:T(8,128)S(1)}, f32[5,8,8,128]{3,2,1,0:T(8,128)S(1)}, u32[]{:S(2)}, u32[]{:S(2)}) collective-permute-start(f32[5,8,8,128]{3,2,1,0:T(8,128)S(1)} %get-tuple-element.80), channel_id=1, source_target_pairs={{0,2},{2,0},{4,6},{6,4},{8,10},{10,8},{12,14},{14,12},{1,3},{3,1},... | collective-permute-start | bytes 491528 | tf_op jit(solution)/shard_map/ppermute | solution.py:419
  71.3 4.3 %collective-permute-done.14 = f32[5,8,8,128]{3,2,1,0:T(8,128)S(1)} collective-permute-done((f32[5,8,8,128]{3,2,1,0:T(8,128)S(1)}, f32[5,8,8,128]{3,2,1,0:T(8,128)S(1)}, u32[]{:S(2)}, u32[]{:S(2)}) %collective-permute-start.14) | collective-permute-done | bytes 163872 | tf_op jit(solution)/shard_map/ppermute | solution.py:419
  75.6 0.7 pad_maximum_fusion.1
  (15 shorter events, 0.3 us)
Async XLA Ops:
  0.0 2.2 %collective-permute-start = (f32[3,5,8,8,128]{4,3,2,1,0:T(8,128)}, f32[3,5,8,8,128]{4,3,2,1,0:T(8,128)S(1)}, u32[]{:S(2)}, u32[]{:S(2)}) collective-permute-start(f32[3,5,8,8,128]{4,3,2,1,0:T(8,128)} %base.3), channel_id=1, source_target_pairs={{0,1},{1,0},{2,3},{3,2},{4,5},{5,4},{6,7},{7,6},{8,9},{9,8},{10,11... | collective-permute-start | bytes 1474568 | tf_op jit(solution)/shard_map/ppermute | solution.py:329
  4.2 31.5 %collective-permute-start.2 = (f32[5,33,8,128]{3,2,1,0:T(8,128)S(1)}, f32[5,33,8,128]{3,2,1,0:T(8,128)S(1)}, u32[]{:S(2)}, u32[]{:S(2)}) collective-permute-start(f32[5,33,8,128]{3,2,1,0:T(8,128)S(1)} %get-tuple-element.44), channel_id=1, source_target_pairs={{0,12},{2,6},{4,0},{6,10},{8,4},{10,14},{12,8},{14,2},{1,13},{3,7}... | collective-permute-start | bytes 2027528 | tf_op jit(solution)/shard_map/ppermute | solution.py:351
  9.2 26.5 %collective-permute-start.1 = (f32[5,24,8,128]{3,2,1,0:T(8,128)S(1)}, f32[5,24,8,128]{3,2,1,0:T(8,128)S(1)}, u32[]{:S(2)}, u32[]{:S(2)}) collective-permute-start(f32[5,24,8,128]{3,2,1,0:T(8,128)S(1)} %get-tuple-element.43), channel_id=1, source_target_pairs={{0,2},{2,0},{4,6},{6,4},{8,10},{10,8},{12,14},{14,12},{1,3},{3,1},... | collective-permute-start | bytes 1474568 | tf_op jit(solution)/shard_map/ppermute | solution.py:351
  9.2 26.5 %collective-permute-start.3 = (f32[5,21,8,128]{3,2,1,0:T(8,128)S(1)}, f32[5,21,8,128]{3,2,1,0:T(8,128)S(1)}, u32[]{:S(2)}, u32[]{:S(2)}) collective-permute-start(f32[5,21,8,128]{3,2,1,0:T(8,128)S(1)} %get-tuple-element.45), channel_id=1, source_target_pairs={{0,14},{2,4},{4,2},{6,8},{8,6},{10,12},{12,10},{14,0},{1,15},{3,5}... | collective-permute-start | bytes 1290248 | tf_op jit(solution)/shard_map/ppermute | solution.py:351
  13.4 30.2 %collective-permute-start.4 = (f32[5,16,8,128]{3,2,1,0:T(8,128)S(1)}, f32[5,16,8,128]{3,2,1,0:T(8,128)S(1)}, u32[]{:S(2)}, u32[]{:S(2)}) collective-permute-start(f32[5,16,8,128]{3,2,1,0:T(8,128)S(1)} %get-tuple-element.50), channel_id=1, source_target_pairs={{0,2},{2,0},{4,6},{6,4},{8,10},{10,8},{12,14},{14,12},{1,3},{3,1},... | collective-permute-start | bytes 983048 | tf_op jit(solution)/shard_map/ppermute | solution.py:351
  14.1 28.6 %collective-permute-start.5 = (f32[5,12,8,128]{3,2,1,0:T(8,128)S(1)}, f32[5,12,8,128]{3,2,1,0:T(8,128)S(1)}, u32[]{:S(2)}, u32[]{:S(2)}) collective-permute-start(f32[5,12,8,128]{3,2,1,0:T(8,128)S(1)} %get-tuple-element.51), channel_id=1, source_target_pairs={{0,14},{2,4},{4,2},{6,8},{8,6},{10,12},{12,10},{14,0},{1,15},{3,5}... | collective-permute-start | bytes 737288 | tf_op jit(solution)/shard_map/ppermute | solution.py:351
  35.7 2.1 %collective-permute-start.6 = (f32[5,8,8,128]{3,2,1,0:T(8,128)S(1)}, f32[5,8,8,128]{3,2,1,0:T(8,128)S(1)}, u32[]{:S(2)}, u32[]{:S(2)}) collective-permute-start(f32[5,8,8,128]{3,2,1,0:T(8,128)S(1)} %slice.12), channel_id=1, source_target_pairs={{0,1},{1,0},{2,3},{3,2},{4,5},{5,4},{6,7},{7,6},{8,9},{9,8},{10,11... | collective-permute-start | bytes 491528 | tf_op jit(solution)/shard_map/ppermute | solution.py:362
  35.8 1.5 %collective-permute-start.7 = (f32[5,6,8,128]{3,2,1,0:T(8,128)S(1)}, f32[5,6,8,128]{3,2,1,0:T(8,128)S(1)}, u32[]{:S(2)}, u32[]{:S(2)}) collective-permute-start(f32[5,6,8,128]{3,2,1,0:T(8,128)S(1)} %slice.13), channel_id=1, source_target_pairs={{0,1},{1,0},{2,3},{3,2},{4,5},{5,4},{6,7},{7,6},{8,9},{9,8},{10,11... | collective-permute-start | bytes 368648 | tf_op jit(solution)/shard_map/ppermute | solution.py:362
  36.4 1.4 %collective-permute-start.8 = (f32[5,6,8,128]{3,2,1,0:T(8,128)S(1)}, f32[5,6,8,128]{3,2,1,0:T(8,128)S(1)}, u32[]{:S(2)}, u32[]{:S(2)}) collective-permute-start(f32[5,6,8,128]{3,2,1,0:T(8,128)S(1)} %slice.14), channel_id=1, source_target_pairs={{0,1},{1,0},{2,3},{3,2},{4,5},{5,4},{6,7},{7,6},{8,9},{9,8},{10,11... | collective-permute-start | bytes 368648 | tf_op jit(solution)/shard_map/ppermute | solution.py:362
  43.7 4.0 %collective-permute-start.9 = (f32[5,40,8,128]{3,2,1,0:T(8,128)S(1)}, f32[5,40,8,128]{3,2,1,0:T(8,128)S(1)}, u32[]{:S(2)}, u32[]{:S(2)}) collective-permute-start(f32[5,40,8,128]{3,2,1,0:T(8,128)S(1)} %pad_maximum_fusion), channel_id=1, source_target_pairs={{0,1},{1,0},{2,3},{3,2},{4,5},{5,4},{6,7},{7,6},{8,9},{9,8},{10,11... | collective-permute-start | bytes 2457608 | tf_op jit(solution)/shard_map/ppermute | solution.py:364
  43.8 8.9 %collective-permute-start.10 = (f32[5,8,8,128]{3,2,1,0:T(8,128)S(1)}, f32[5,8,8,128]{3,2,1,0:T(8,128)S(1)}, u32[]{:S(2)}, u32[]{:S(2)}) collective-permute-start(f32[5,8,8,128]{3,2,1,0:T(8,128)S(1)} %get-tuple-element.66), channel_id=1, source_target_pairs={{0,4},{2,6},{4,8},{6,10},{8,12},{10,14},{12,0},{14,2},{1,5},{3,7},... | collective-permute-start | bytes 491528 | tf_op jit(solution)/shard_map/ppermute | solution.py:403
  43.8 10.1 %collective-permute-start.11 = (f32[5,8,8,128]{3,2,1,0:T(8,128)S(1)}, f32[5,8,8,128]{3,2,1,0:T(8,128)S(1)}, u32[]{:S(2)}, u32[]{:S(2)}) collective-permute-start(f32[5,8,8,128]{3,2,1,0:T(8,128)S(1)} %get-tuple-element.67), channel_id=1, source_target_pairs={{0,12},{2,14},{4,0},{6,2},{8,4},{10,6},{12,8},{14,10},{1,13},{3,15... | collective-permute-start | bytes 491528 | tf_op jit(solution)/shard_map/ppermute | solution.py:404
  56.8 9.0 %collective-permute-start.12 = (f32[5,8,8,128]{3,2,1,0:T(8,128)S(1)}, f32[5,8,8,128]{3,2,1,0:T(8,128)S(1)}, u32[]{:S(2)}, u32[]{:S(2)}) collective-permute-start(f32[5,8,8,128]{3,2,1,0:T(8,128)S(1)} %get-tuple-element.72), channel_id=1, source_target_pairs={{0,4},{2,6},{4,8},{6,10},{8,12},{10,14},{12,0},{14,2},{1,5},{3,7},... | collective-permute-start | bytes 491528 | tf_op jit(solution)/shard_map/ppermute | solution.py:403
  57.4 9.6 %collective-permute-start.13 = (f32[5,8,8,128]{3,2,1,0:T(8,128)S(1)}, f32[5,8,8,128]{3,2,1,0:T(8,128)S(1)}, u32[]{:S(2)}, u32[]{:S(2)}) collective-permute-start(f32[5,8,8,128]{3,2,1,0:T(8,128)S(1)} %get-tuple-element.73), channel_id=1, source_target_pairs={{0,12},{2,14},{4,0},{6,2},{8,4},{10,6},{12,8},{14,10},{1,13},{3,15... | collective-permute-start | bytes 491528 | tf_op jit(solution)/shard_map/ppermute | solution.py:404
  70.0 5.6 %collective-permute-start.14 = (f32[5,8,8,128]{3,2,1,0:T(8,128)S(1)}, f32[5,8,8,128]{3,2,1,0:T(8,128)S(1)}, u32[]{:S(2)}, u32[]{:S(2)}) collective-permute-start(f32[5,8,8,128]{3,2,1,0:T(8,128)S(1)} %get-tuple-element.80), channel_id=1, source_target_pairs={{0,2},{2,0},{4,6},{6,4},{8,10},{10,8},{12,14},{14,12},{1,3},{3,1},... | collective-permute-start | bytes 491528 | tf_op jit(solution)/shard_map/ppermute | solution.py:419

commit v6 on v5

--- a/solution.py
+++ b/solution.py
@@ -305,6 +305,18 @@
         right[...] = state[:, far - next_width : far]
 
 
+def finish_kernel(keep, given, out, sem):
+    mine = parity()
+    copies = [
+        pltpu.make_async_copy(keep, out.at[mine], sem.at[0]),
+        pltpu.make_async_copy(given, out.at[1 - mine], sem.at[1]),
+    ]
+    for copy in copies:
+        copy.start()
+    for copy in copies:
+        copy.wait()
+
+
 def per_device(perturbation, forcing, frequency, base_flow, phase_slot):
     _, _, tile, rows, lanes = perturbation.shape
     count = lax.axis_size("space")
@@ -417,9 +429,15 @@
         outs = advance(which, [*factors_here, force, left_in, right_in, *begun])
     keep, give = outs
     given = lax.ppermute(give, "space", swap)
-    mine = parity()
-    low, high = jnp.where(mine == 0, keep, given), jnp.where(mine == 0, given, keep)
-    return jnp.stack([low, high])
+    return pl.pallas_call(
+        finish_kernel,
+        out_shape=jax.ShapeDtypeStruct(perturbation.shape, perturbation.dtype),
+        in_specs=[VMEM] * 2,
+        out_specs=HBM,
+        scratch_shapes=[pltpu.SemaphoreType.DMA((2,))],
+        compiler_params=pltpu.CompilerParams(vmem_limit_bytes=1 << 20),
+        name="finish",
+    )(keep, given)
 
 
 def solution(mesh):

time: 76.6 us -> 76.7 us (level)
  Pallas kernels: 19.7 us -> 20.5 us
  other arithmetic: 0.83 us -> 0.05 us
    another operation x2 -> x0, other arithmetic: 0.77 us -> none  [per_device(): return jnp.stack([low, high])]
where the time goes in v6:
time: 76.7 us; the launch traced here: 76.5 us
  waiting for transfers between devices  35.5 us (46%)
  Pallas kernels  20.5 us (27%)
  starting transfers between devices  20.1 us (26%)
    ppermute x5, waiting for transfers between devices, exchange(): lax.ppermute(part, 'space', perm)  19.6 us
    pallas_call x3, Pallas kernels, advance(): pallas(functools.partial(advance_kernel, group, widths, reach, first, las...  9.93 us
    ppermute x5, starting transfers between devices, exchange(): lax.ppermute(part, 'space', perm)  9.89 us
    ppermute x2, starting transfers between devices, per_device(): right_in = lax.ppermute(left, 'space', behind)  7.04 us
    ppermute x2, waiting for transfers between devices, per_device(): left_in = lax.ppermute(right, 'space', ahead)  6.13 us
    pallas_call x2, Pallas kernels, pack(): pallas(functools.partial(pack_kernel, sets, widths, reach, which), 'pack'...  4.34 us
    ppermute x1, waiting for transfers between devices, per_device(): given = lax.ppermute(give, 'space', swap)  4.32 us
    ppermute x2, waiting for transfers between devices, per_device(): right_in = lax.ppermute(left, 'space', behind)  2.5 us
  transfers between devices with their start and end apart: 15, of which 10 were waited for; matrix products, arithmetic and copies ran while one was open for 0% of the time, Pallas kernels for 15%

profile of v6, /device:TPU:0, one launch (start us, length us, event | category | flops | bytes accessed | tf_op | source)
XLA Modules:
  0.0 76.5 jit_solution(5809728491088639312)
XLA Ops:
  0.0 0.5 collective-permute-start
  0.5 1.7 %collective-permute-done.base_peer = f32[3,5,8,8,128]{4,3,2,1,0:T(8,128)S(1)} collective-permute-done((f32[3,5,8,8,128]{4,3,2,1,0:T(8,128)}, f32[3,5,8,8,128]{4,3,2,1,0:T(8,128)S(1)}, u32[]{:S(2)}, u32[]{:S(2)}) %collective-permute-start) | collective-permute-done | bytes 491552 | tf_op jit(solution)/shard_map/ppermute | solution.py:341
  2.2 2.0 %pack.2 = (f32[5,24,8,128]{3,2,1,0:T(8,128)S(1)}, f32[5,33,8,128]{3,2,1,0:T(8,128)S(1)}, f32[5,21,8,128]{3,2,1,0:T(8,128)S(1)}) custom-call(s32[6]{0:T(128)} %phase_slot.3, f32[2,5,8,8,128]{4,3,2,1,0:T(8,128)} %pert.3, f32[2,5,8,8,128]{4,3,2,1,0:T(8,128)} %force.3, f32[3,5,8,8,128]{4,3,2,1,0:T(8,128)} %base.3, ...), custom_call_target="tpu_custom_call" | custom-call | tf_op jit(solution)/shard_map/pack/pallas_call | solution.py:354
  4.2 5.0 %collective-permute-start.2 = (f32[5,33,8,128]{3,2,1,0:T(8,128)S(1)}, f32[5,33,8,128]{3,2,1,0:T(8,128)S(1)}, u32[]{:S(2)}, u32[]{:S(2)}) collective-permute-start(f32[5,33,8,128]{3,2,1,0:T(8,128)S(1)} %get-tuple-element.44), channel_id=1, source_target_pairs={{0,12},{2,6},{4,0},{6,10},{8,4},{10,14},{12,8},{14,2},{1,13},{3,7}... | collective-permute-start | bytes 2027528 | tf_op jit(solution)/shard_map/ppermute | solution.py:363
  9.2 1.9 %collective-permute-start.3 = (f32[5,21,8,128]{3,2,1,0:T(8,128)S(1)}, f32[5,21,8,128]{3,2,1,0:T(8,128)S(1)}, u32[]{:S(2)}, u32[]{:S(2)}) collective-permute-start(f32[5,21,8,128]{3,2,1,0:T(8,128)S(1)} %get-tuple-element.45), channel_id=1, source_target_pairs={{0,14},{2,4},{4,2},{6,8},{8,6},{10,12},{12,10},{14,0},{1,15},{3,5}... | collective-permute-start | bytes 1290248 | tf_op jit(solution)/shard_map/ppermute | solution.py:363
  11.1 2.3 %pack.3 = (f32[5,16,8,128]{3,2,1,0:T(8,128)S(1)}, f32[5,12,8,128]{3,2,1,0:T(8,128)S(1)}, f32[5,16,8,128]{3,2,1,0:T(8,128)S(1)}, f32[5,48,8,128]{3,2,1,0:T(8,128)S(1)}) custom-call(s32[6]{0:T(128)} %phase_slot.3, f32[2,5,8,8,128]{4,3,2,1,0:T(8,128)} %pert.3, f32[2,5,8,8,128]{4,3,2,1,0:T(8,128)} %force.3, f32[3,5,8,8,128]{4,3,2,1,0:T(8,128)} %base.3, ...), custom_call_target="tpu_custom_call" | custom-call | tf_op jit(solution)/shard_map/pack/pallas_call | solution.py:354
  13.4 0.7 collective-permute-start.4
  14.1 2.3 %collective-permute-start.5 = (f32[5,12,8,128]{3,2,1,0:T(8,128)S(1)}, f32[5,12,8,128]{3,2,1,0:T(8,128)S(1)}, u32[]{:S(2)}, u32[]{:S(2)}) collective-permute-start(f32[5,12,8,128]{3,2,1,0:T(8,128)S(1)} %get-tuple-element.51), channel_id=1, source_target_pairs={{0,14},{2,4},{4,2},{6,8},{8,6},{10,12},{12,10},{14,0},{1,15},{3,5}... | collective-permute-start | bytes 737288 | tf_op jit(solution)/shard_map/ppermute | solution.py:363
  16.4 0.7 waves.1
  17.1 18.5 %collective-permute-done.3.refs_2_.refs_5_ = f32[5,21,8,128]{3,2,1,0:T(8,128)S(1)} collective-permute-done((f32[5,21,8,128]{3,2,1,0:T(8,128)S(1)}, f32[5,21,8,128]{3,2,1,0:T(8,128)S(1)}, u32[]{:S(2)}, u32[]{:S(2)}) %collective-permute-start.3) | collective-permute-done | bytes 430112 | tf_op jit(solution)/shard_map/ppermute | solution.py:363
  35.8 0.6 collective-permute-start.7
  36.4 0.1 collective-permute-start.8
  36.5 0.9 %collective-permute-done.7.refs_4_ = f32[5,6,8,128]{3,2,1,0:T(8,128)S(1)} collective-permute-done((f32[5,6,8,128]{3,2,1,0:T(8,128)S(1)}, f32[5,6,8,128]{3,2,1,0:T(8,128)S(1)}, u32[]{:S(2)}, u32[]{:S(2)}) %collective-permute-start.7) | collective-permute-done | bytes 122912 | tf_op jit(solution)/shard_map/ppermute | solution.py:374
  37.4 0.4 collective-permute-done.8.refs_5_
  37.7 0.8 terms.2
  38.5 4.1 %advance.3 = (f32[5,32,8,128]{3,2,1,0:T(8,128)S(1)}, f32[5,16,8,128]{3,2,1,0:T(8,128)S(1)}, f32[5,8,8,128]{3,2,1,0:T(8,128)S(1)}, f32[5,8,8,128]{3,2,1,0:T(8,128)S(1)}) custom-call(f32[18,8,128]{2,1,0:T(8,128)S(1)} %waves.1, f32[26,32,8,128]{3,2,1,0:T(8,128)S(1)} %get-tuple-element.55.refs_0_, f32[26,32,8,128]{3,2,1,0:T(8,128)S(1)} %get-tuple-element.56.refs_1_, ...), custom_call_target="tpu_custom_call" | custom-call | tf_op jit(solution)/shard_map/advance/pallas_call | solution.py:397
  42.6 1.1 %collective-permute-done.4.refs_0_ = f32[5,16,8,128]{3,2,1,0:T(8,128)S(1)} collective-permute-done((f32[5,16,8,128]{3,2,1,0:T(8,128)S(1)}, f32[5,16,8,128]{3,2,1,0:T(8,128)S(1)}, u32[]{:S(2)}, u32[]{:S(2)}) %collective-permute-start.4) | collective-permute-done | bytes 327712 | tf_op jit(solution)/shard_map/ppermute | solution.py:363
  43.8 3.8 %collective-permute-start.11 = (f32[5,8,8,128]{3,2,1,0:T(8,128)S(1)}, f32[5,8,8,128]{3,2,1,0:T(8,128)S(1)}, u32[]{:S(2)}, u32[]{:S(2)}) collective-permute-start(f32[5,8,8,128]{3,2,1,0:T(8,128)S(1)} %get-tuple-element.67), channel_id=1, source_target_pairs={{0,12},{2,14},{4,0},{6,2},{8,4},{10,6},{12,8},{14,10},{1,13},{3,15... | collective-permute-start | bytes 491528 | tf_op jit(solution)/shard_map/ppermute | solution.py:416
  47.7 1.5 %terms.3 = (f32[26,32,8,128]{3,2,1,0:T(8,128)S(1)}, f32[26,32,8,128]{3,2,1,0:T(8,128)S(1)}, f32[26,32,8,128]{3,2,1,0:T(8,128)S(1)}, f32[26,32,8,128]{3,2,1,0:T(8,128)S(1)}) custom-call(f32[5,48,8,128]{3,2,1,0:T(8,128)S(1)} %get-tuple-element.49.held_base, f32[5,16,8,128]{3,2,1,0:T(8,128)S(1)} %collective-permute-done.4.refs_0_, ...), custom_call_target="tpu_custom_call" | custom-call | tf_op jit(solution)/shard_map/terms/pallas_call | solution.py:378
  49.2 1.2 %interior.2 = (f32[5,16,8,128]{3,2,1,0:T(8,128)S(1)}, f32[5,16,8,128]{3,2,1,0:T(8,128)S(1)}, f32[5,16,8,128]{3,2,1,0:T(8,128)S(1)}, f32[5,16,8,128]{3,2,1,0:T(8,128)S(1)}) custom-call(f32[18,8,128]{2,1,0:T(8,128)S(1)} %waves.1, f32[26,32,8,128]{3,2,1,0:T(8,128)S(1)} %get-tuple-element.64.refs_0_, f32[26,32,8,128]{3,2,1,0:T(8,128)S(1)} %get-tuple-element.65.refs_1_, ...), custom_call_target="tpu_custom_call" | custom-call | tf_op jit(solution)/shard_map/interior/pallas_call | solution.py:421
  50.4 2.2 %collective-permute-done.10.refs_3_ = f32[5,8,8,128]{3,2,1,0:T(8,128)S(1)} collective-permute-done((f32[5,8,8,128]{3,2,1,0:T(8,128)S(1)}, f32[5,8,8,128]{3,2,1,0:T(8,128)S(1)}, u32[]{:S(2)}, u32[]{:S(2)}) %collective-permute-start.10) | collective-permute-done | bytes 163872 | tf_op jit(solution)/shard_map/ppermute | solution.py:415
  52.7 1.2 %collective-permute-done.11.refs_4_ = f32[5,8,8,128]{3,2,1,0:T(8,128)S(1)} collective-permute-done((f32[5,8,8,128]{3,2,1,0:T(8,128)S(1)}, f32[5,8,8,128]{3,2,1,0:T(8,128)S(1)}, u32[]{:S(2)}, u32[]{:S(2)}) %collective-permute-start.11) | collective-permute-done | bytes 163872 | tf_op jit(solution)/shard_map/ppermute | solution.py:416
  53.9 2.9 %advance.4 = (f32[5,16,8,128]{3,2,1,0:T(8,128)S(1)}, f32[5,8,8,128]{3,2,1,0:T(8,128)S(1)}, f32[5,8,8,128]{3,2,1,0:T(8,128)S(1)}) custom-call(f32[18,8,128]{2,1,0:T(8,128)S(1)} %waves.1, f32[26,32,8,128]{3,2,1,0:T(8,128)S(1)} %get-tuple-element.64.refs_0_, f32[26,32,8,128]{3,2,1,0:T(8,128)S(1)} %get-tuple-element.65.refs_1_, ...), custom_call_target="tpu_custom_call" | custom-call | tf_op jit(solution)/shard_map/advance/pallas_call | solution.py:397
  56.8 0.6 collective-permute-start.12
  57.4 3.2 %collective-permute-start.13 = (f32[5,8,8,128]{3,2,1,0:T(8,128)S(1)}, f32[5,8,8,128]{3,2,1,0:T(8,128)S(1)}, u32[]{:S(2)}, u32[]{:S(2)}) collective-permute-start(f32[5,8,8,128]{3,2,1,0:T(8,128)S(1)} %get-tuple-element.73), channel_id=1, source_target_pairs={{0,12},{2,14},{4,0},{6,2},{8,4},{10,6},{12,8},{14,10},{1,13},{3,15... | collective-permute-start | bytes 491528 | tf_op jit(solution)/shard_map/ppermute | solution.py:416
  60.7 1.2 %interior.3 = (f32[5,16,8,128]{3,2,1,0:T(8,128)S(1)}, f32[5,16,8,128]{3,2,1,0:T(8,128)S(1)}, f32[5,16,8,128]{3,2,1,0:T(8,128)S(1)}, f32[5,16,8,128]{3,2,1,0:T(8,128)S(1)}) custom-call(f32[18,8,128]{2,1,0:T(8,128)S(1)} %waves.1, f32[26,32,8,128]{3,2,1,0:T(8,128)S(1)} %get-tuple-element.61.refs_0_, f32[26,32,8,128]{3,2,1,0:T(8,128)S(1)} %get-tuple-element.62.refs_1_, ...), custom_call_target="tpu_custom_call" | custom-call | tf_op jit(solution)/shard_map/interior/pallas_call | solution.py:421
  61.9 3.9 %collective-permute-done.12.refs_3_ = f32[5,8,8,128]{3,2,1,0:T(8,128)S(1)} collective-permute-done((f32[5,8,8,128]{3,2,1,0:T(8,128)S(1)}, f32[5,8,8,128]{3,2,1,0:T(8,128)S(1)}, u32[]{:S(2)}, u32[]{:S(2)}) %collective-permute-start.12) | collective-permute-done | bytes 163872 | tf_op jit(solution)/shard_map/ppermute | solution.py:415
  65.8 1.3 %collective-permute-done.13.refs_4_ = f32[5,8,8,128]{3,2,1,0:T(8,128)S(1)} collective-permute-done((f32[5,8,8,128]{3,2,1,0:T(8,128)S(1)}, f32[5,8,8,128]{3,2,1,0:T(8,128)S(1)}, u32[]{:S(2)}, u32[]{:S(2)}) %collective-permute-start.13) | collective-permute-done | bytes 163872 | tf_op jit(solution)/shard_map/ppermute | solution.py:416
  67.1 3.0 %advance.5 = (f32[5,8,8,128]{3,2,1,0:T(8,128)S(1)}, f32[5,8,8,128]{3,2,1,0:T(8,128)S(1)}) custom-call(f32[18,8,128]{2,1,0:T(8,128)S(1)} %waves.1, f32[26,32,8,128]{3,2,1,0:T(8,128)S(1)} %get-tuple-element.61.refs_0_, f32[26,32,8,128]{3,2,1,0:T(8,128)S(1)} %get-tuple-element.62.refs_1_, f32[5,32,8,128]{3,2,1,0:T(8,128)S(1)} %get-tuple-element.63.refs_2_, ...), custom_call_target="tpu_custom_call" | custom-call | tf_op jit(solution)/shard_map/advance/pallas_call | solution.py:397
  70.0 1.3 %collective-permute-start.14 = (f32[5,8,8,128]{3,2,1,0:T(8,128)S(1)}, f32[5,8,8,128]{3,2,1,0:T(8,128)S(1)}, u32[]{:S(2)}, u32[]{:S(2)}) collective-permute-start(f32[5,8,8,128]{3,2,1,0:T(8,128)S(1)} %get-tuple-element.80), channel_id=1, source_target_pairs={{0,2},{2,0},{4,6},{6,4},{8,10},{10,8},{12,14},{14,12},{1,3},{3,1},... | collective-permute-start | bytes 491528 | tf_op jit(solution)/shard_map/ppermute | solution.py:431
  71.3 4.3 %collective-permute-done.14.given = f32[5,8,8,128]{3,2,1,0:T(8,128)S(1)} collective-permute-done((f32[5,8,8,128]{3,2,1,0:T(8,128)S(1)}, f32[5,8,8,128]{3,2,1,0:T(8,128)S(1)}, u32[]{:S(2)}, u32[]{:S(2)}) %collective-permute-start.14) | collective-permute-done | bytes 163872 | tf_op jit(solution)/shard_map/ppermute | solution.py:431
  75.6 0.7 finish.1
  (14 shorter events, 0.3 us)
Async XLA Ops:
  0.0 2.2 %collective-permute-start = (f32[3,5,8,8,128]{4,3,2,1,0:T(8,128)}, f32[3,5,8,8,128]{4,3,2,1,0:T(8,128)S(1)}, u32[]{:S(2)}, u32[]{:S(2)}) collective-permute-start(f32[3,5,8,8,128]{4,3,2,1,0:T(8,128)} %base.3), channel_id=1, source_target_pairs={{0,1},{1,0},{2,3},{3,2},{4,5},{5,4},{6,7},{7,6},{8,9},{9,8},{10,11... | collective-permute-start | bytes 1474568 | tf_op jit(solution)/shard_map/ppermute | solution.py:341
  4.2 31.5 %collective-permute-start.2 = (f32[5,33,8,128]{3,2,1,0:T(8,128)S(1)}, f32[5,33,8,128]{3,2,1,0:T(8,128)S(1)}, u32[]{:S(2)}, u32[]{:S(2)}) collective-permute-start(f32[5,33,8,128]{3,2,1,0:T(8,128)S(1)} %get-tuple-element.44), channel_id=1, source_target_pairs={{0,12},{2,6},{4,0},{6,10},{8,4},{10,14},{12,8},{14,2},{1,13},{3,7}... | collective-permute-start | bytes 2027528 | tf_op jit(solution)/shard_map/ppermute | solution.py:363
  9.2 26.5 %collective-permute-start.1 = (f32[5,24,8,128]{3,2,1,0:T(8,128)S(1)}, f32[5,24,8,128]{3,2,1,0:T(8,128)S(1)}, u32[]{:S(2)}, u32[]{:S(2)}) collective-permute-start(f32[5,24,8,128]{3,2,1,0:T(8,128)S(1)} %get-tuple-element.43), channel_id=1, source_target_pairs={{0,2},{2,0},{4,6},{6,4},{8,10},{10,8},{12,14},{14,12},{1,3},{3,1},... | collective-permute-start | bytes 1474568 | tf_op jit(solution)/shard_map/ppermute | solution.py:363
  9.2 26.5 %collective-permute-start.3 = (f32[5,21,8,128]{3,2,1,0:T(8,128)S(1)}, f32[5,21,8,128]{3,2,1,0:T(8,128)S(1)}, u32[]{:S(2)}, u32[]{:S(2)}) collective-permute-start(f32[5,21,8,128]{3,2,1,0:T(8,128)S(1)} %get-tuple-element.45), channel_id=1, source_target_pairs={{0,14},{2,4},{4,2},{6,8},{8,6},{10,12},{12,10},{14,0},{1,15},{3,5}... | collective-permute-start | bytes 1290248 | tf_op jit(solution)/shard_map/ppermute | solution.py:363
  13.4 30.2 %collective-permute-start.4 = (f32[5,16,8,128]{3,2,1,0:T(8,128)S(1)}, f32[5,16,8,128]{3,2,1,0:T(8,128)S(1)}, u32[]{:S(2)}, u32[]{:S(2)}) collective-permute-start(f32[5,16,8,128]{3,2,1,0:T(8,128)S(1)} %get-tuple-element.50), channel_id=1, source_target_pairs={{0,2},{2,0},{4,6},{6,4},{8,10},{10,8},{12,14},{14,12},{1,3},{3,1},... | collective-permute-start | bytes 983048 | tf_op jit(solution)/shard_map/ppermute | solution.py:363
  14.1 28.5 %collective-permute-start.5 = (f32[5,12,8,128]{3,2,1,0:T(8,128)S(1)}, f32[5,12,8,128]{3,2,1,0:T(8,128)S(1)}, u32[]{:S(2)}, u32[]{:S(2)}) collective-permute-start(f32[5,12,8,128]{3,2,1,0:T(8,128)S(1)} %get-tuple-element.51), channel_id=1, source_target_pairs={{0,14},{2,4},{4,2},{6,8},{8,6},{10,12},{12,10},{14,0},{1,15},{3,5}... | collective-permute-start | bytes 737288 | tf_op jit(solution)/shard_map/ppermute | solution.py:363
  35.7 2.0 %collective-permute-start.6 = (f32[5,8,8,128]{3,2,1,0:T(8,128)S(1)}, f32[5,8,8,128]{3,2,1,0:T(8,128)S(1)}, u32[]{:S(2)}, u32[]{:S(2)}) collective-permute-start(f32[5,8,8,128]{3,2,1,0:T(8,128)S(1)} %slice.12), channel_id=1, source_target_pairs={{0,1},{1,0},{2,3},{3,2},{4,5},{5,4},{6,7},{7,6},{8,9},{9,8},{10,11... | collective-permute-start | bytes 491528 | tf_op jit(solution)/shard_map/ppermute | solution.py:374
  35.8 1.5 %collective-permute-start.7 = (f32[5,6,8,128]{3,2,1,0:T(8,128)S(1)}, f32[5,6,8,128]{3,2,1,0:T(8,128)S(1)}, u32[]{:S(2)}, u32[]{:S(2)}) collective-permute-start(f32[5,6,8,128]{3,2,1,0:T(8,128)S(1)} %slice.13), channel_id=1, source_target_pairs={{0,1},{1,0},{2,3},{3,2},{4,5},{5,4},{6,7},{7,6},{8,9},{9,8},{10,11... | collective-permute-start | bytes 368648 | tf_op jit(solution)/shard_map/ppermute | solution.py:374
  36.4 1.3 %collective-permute-start.8 = (f32[5,6,8,128]{3,2,1,0:T(8,128)S(1)}, f32[5,6,8,128]{3,2,1,0:T(8,128)S(1)}, u32[]{:S(2)}, u32[]{:S(2)}) collective-permute-start(f32[5,6,8,128]{3,2,1,0:T(8,128)S(1)} %slice.14), channel_id=1, source_target_pairs={{0,1},{1,0},{2,3},{3,2},{4,5},{5,4},{6,7},{7,6},{8,9},{9,8},{10,11... | collective-permute-start | bytes 368648 | tf_op jit(solution)/shard_map/ppermute | solution.py:374
  43.7 4.0 %collective-permute-start.9 = (f32[5,40,8,128]{3,2,1,0:T(8,128)S(1)}, f32[5,40,8,128]{3,2,1,0:T(8,128)S(1)}, u32[]{:S(2)}, u32[]{:S(2)}) collective-permute-start(f32[5,40,8,128]{3,2,1,0:T(8,128)S(1)} %pad_maximum_fusion), channel_id=1, source_target_pairs={{0,1},{1,0},{2,3},{3,2},{4,5},{5,4},{6,7},{7,6},{8,9},{9,8},{10,11... | collective-permute-start | bytes 2457608 | tf_op jit(solution)/shard_map/ppermute | solution.py:376
  43.8 8.9 %collective-permute-start.10 = (f32[5,8,8,128]{3,2,1,0:T(8,128)S(1)}, f32[5,8,8,128]{3,2,1,0:T(8,128)S(1)}, u32[]{:S(2)}, u32[]{:S(2)}) collective-permute-start(f32[5,8,8,128]{3,2,1,0:T(8,128)S(1)} %get-tuple-element.66), channel_id=1, source_target_pairs={{0,4},{2,6},{4,8},{6,10},{8,12},{10,14},{12,0},{14,2},{1,5},{3,7},... | collective-permute-start | bytes 491528 | tf_op jit(solution)/shard_map/ppermute | solution.py:415
  43.8 10.1 %collective-permute-start.11 = (f32[5,8,8,128]{3,2,1,0:T(8,128)S(1)}, f32[5,8,8,128]{3,2,1,0:T(8,128)S(1)}, u32[]{:S(2)}, u32[]{:S(2)}) collective-permute-start(f32[5,8,8,128]{3,2,1,0:T(8,128)S(1)} %get-tuple-element.67), channel_id=1, source_target_pairs={{0,12},{2,14},{4,0},{6,2},{8,4},{10,6},{12,8},{14,10},{1,13},{3,15... | collective-permute-start | bytes 491528 | tf_op jit(solution)/shard_map/ppermute | solution.py:416
  56.8 9.0 %collective-permute-start.12 = (f32[5,8,8,128]{3,2,1,0:T(8,128)S(1)}, f32[5,8,8,128]{3,2,1,0:T(8,128)S(1)}, u32[]{:S(2)}, u32[]{:S(2)}) collective-permute-start(f32[5,8,8,128]{3,2,1,0:T(8,128)S(1)} %get-tuple-element.72), channel_id=1, source_target_pairs={{0,4},{2,6},{4,8},{6,10},{8,12},{10,14},{12,0},{14,2},{1,5},{3,7},... | collective-permute-start | bytes 491528 | tf_op jit(solution)/shard_map/ppermute | solution.py:415
  57.4 9.6 %collective-permute-start.13 = (f32[5,8,8,128]{3,2,1,0:T(8,128)S(1)}, f32[5,8,8,128]{3,2,1,0:T(8,128)S(1)}, u32[]{:S(2)}, u32[]{:S(2)}) collective-permute-start(f32[5,8,8,128]{3,2,1,0:T(8,128)S(1)} %get-tuple-element.73), channel_id=1, source_target_pairs={{0,12},{2,14},{4,0},{6,2},{8,4},{10,6},{12,8},{14,10},{1,13},{3,15... | collective-permute-start | bytes 491528 | tf_op jit(solution)/shard_map/ppermute | solution.py:416
  70.0 5.6 %collective-permute-start.14 = (f32[5,8,8,128]{3,2,1,0:T(8,128)S(1)}, f32[5,8,8,128]{3,2,1,0:T(8,128)S(1)}, u32[]{:S(2)}, u32[]{:S(2)}) collective-permute-start(f32[5,8,8,128]{3,2,1,0:T(8,128)S(1)} %get-tuple-element.80), channel_id=1, source_target_pairs={{0,2},{2,0},{4,6},{6,4},{8,10},{10,8},{12,14},{14,12},{1,3},{3,1},... | collective-permute-start | bytes 491528 | tf_op jit(solution)/shard_map/ppermute | solution.py:431
